TPU v7x, 256 devices: a whole 4x4x8 slice. The times are simulated.
256 devices in a mesh: mem: 32 (over y, x, core), tile: 8 (over z).
Axes of the slice: x: 4, y: 4, z: 8, core: 2. Of those that a mesh axis runs over, the one named last changes fastest.
Arguments:
- perturbations: bfloat16 [64, 4, 256, 1024], P('mem', None, 'tile'), may hold values from -6 to 6
- right_side: float32 [4, 256, 1024], P(None, 'tile'), may hold values from -14 to 14
- fine_taps: float32 [2, 4, 5], replicated, may hold values from 0.3 to 1
- coarse_lat: float32 [64, 64], replicated, may hold values from -4 to 16, as said below
- coarse_lon: float32 [256, 256], replicated, may hold values from -4 to 16, as said below
Outputs:
- solution: float32 [4, 256, 1024], P(None, 'tile', 'mem')
- residual: float32 [4, 256, 1024], P(None, 'tile', 'mem')
Inputs may be any that keep to these rules, and one draw needn't show every extreme that they name: `coarse_lat`: symmetric. `coarse_lon`: symmetric.
All inputs are finite; a program needn't handle non-finite values.
Results may differ from a plain program's by a relative error of at most 0.0003.
Values may be sent and summed in bfloat16 or wider, within the bound.
No kernel may reach another device: no remote copies, remote signals or barrier semaphores. Data moves between devices by JAX's collectives and lax.ppermute only.
A program may use at most 64 MiB of HBM per device.

v0:
```python
import functools

import jax
import jax.numpy as jnp
from jax import lax
from jax.experimental import pallas as pl
from jax.experimental.pallas import tpu as pltpu
from jax.sharding import Mesh
from jax.sharding import PartitionSpec as P

MEM = ("mem_0", "mem_1", "mem_2")
F32 = jnp.float32
BF16 = jnp.bfloat16
EXACT = lax.Precision.HIGHEST
PAIRS, ROWS, LON = 8, 32, 1024
GROUPS, TILES = 32, 8


def mm(a, b):
    return jnp.dot(a, b, preferred_element_type=F32)


def exact_mm(a, b):
    return jnp.dot(a, b, preferred_element_type=F32, precision=EXACT)


def split2(x):
    high = x.astype(BF16)
    return high, (x - high.astype(F32)).astype(BF16)


def split3(x):
    high = x.astype(BF16)
    rest = x - high.astype(F32)
    mid = rest.astype(BF16)
    return high, mid, (rest - mid.astype(F32)).astype(BF16)


def iotas(rows, cols):
    return (
        lax.broadcasted_iota(jnp.int32, (rows, cols), 0),
        lax.broadcasted_iota(jnp.int32, (rows, cols), 1),
    )


def shrink_table(rows, cols, along_rows):
    i, j = iotas(rows, cols)
    hit = (i >> 2) == j if along_rows else i == (j >> 2)
    return jnp.where(hit, 0.25, 0.0).astype(BF16)


def expand_table(rows, cols, along_rows):
    i, j = iotas(rows, cols)
    hit = (i >> 2) == j if along_rows else i == (j >> 2)
    return jnp.where(hit, 1.0, 0.0).astype(BF16)


def block_mean(w):
    table = shrink_table(64, 256, False)
    part = sum(mm(table, piece) for piece in split3(w))
    stacked = jnp.concatenate([part[:, :512], part[:, 512:]], axis=0)
    table = shrink_table(512, 128, True)
    small = sum(mm(piece, table) for piece in split3(stacked))
    return jnp.concatenate([small[:64], small[64:]], axis=1)


def prolong(c):
    table = expand_table(256, 64, True)
    tall = sum(mm(table, piece) for piece in split2(c))
    stacked = jnp.concatenate([tall[:, :128], tall[:, 128:]], axis=0)
    table = expand_table(128, 512, False)
    wide = sum(mm(piece, table) for piece in split2(stacked))
    return jnp.concatenate([wide[:256], wide[256:]], axis=1)


def natural(blocks):
    rows = []
    for tall in range(16):
        lanes = [
            blocks[2 * tall + wide // 4, 8 * (wide % 4) : 8 * (wide % 4) + 8, :]
            for wide in range(8)
        ]
        rows.append(jnp.concatenate(lanes, axis=1))
    return jnp.concatenate(rows, axis=0)


def vector_of(ref):
    return natural(ref) if len(ref.shape) == 3 else ref[...]


def detail_kernel(x_ref, v_ref, c_ref, d_ref, top_ref, bottom_ref):
    v = vector_of(v_ref)
    w = x_ref[...].astype(F32) * jnp.concatenate([v, v], axis=0)
    c = block_mean(w)
    c_ref[...] = c.reshape(PAIRS, 8, 256)
    d = w - prolong(c)
    d_ref[...] = d
    for pair in range(PAIRS):
        top_ref[pair] = d[ROWS * pair : ROWS * pair + 8]
        bottom_ref[pair] = d[ROWS * pair + 24 : ROWS * pair + 32]


def table_kernel(tile_ref, lat_ref, lon_ref, high_ref, low_ref, band_ref):
    i, j = iotas(160, 192)
    first = jnp.zeros((160, 192), F32)
    for level in range(4):
        row = i - 40 * level
        dist = jnp.abs(j - 48 * level - row - 4)
        spot = tile_ref[0] * ROWS - 4 + row
        fits = (row >= 0) & (row < 40) & (j >= 48 * level) & (j < 48 * level + 48)
        fits = fits & (spot >= 0) & (spot < ROWS * TILES)
        for offset in range(5):
            first = jnp.where(fits & (dist == offset), lat_ref[level, offset], first)
    i, j = iotas(128, 160)
    second = jnp.zeros((128, 160), F32)
    for level in range(4):
        row = i - 32 * level
        dist = jnp.abs(j - 40 * level - row - 4)
        fits = (row >= 0) & (row < 32) & (j >= 40 * level) & (j < 40 * level + 40)
        for offset in range(5):
            second = jnp.where(fits & (dist == offset), lat_ref[level, offset], second)
    both = exact_mm(second, first)
    i, j = iotas(128, 128)
    mean = jnp.where((i >> 2) == (j >> 2), 0.25, 0.0)
    high, low = split2(jnp.concatenate([both, exact_mm(mean, both)], axis=0))
    high_ref[...] = high
    low_ref[...] = low
    for place in range(3):
        dist = jnp.abs(i + 128 * (place - 1) - j)
        for level in range(4):
            band = jnp.zeros((128, 128), F32)
            for offset in range(9):
                band = jnp.where(dist == offset, lon_ref[level, offset], band)
            high, low = split2(band)
            band_ref[level, 0, place] = high
            band_ref[level, 1, place] = low
            high, low = split2(-exact_mm(band, mean))
            band_ref[level, 2, place] = high
            band_ref[level, 3, place] = low


def banded(band_ref, level, kind):
    a, b, c = (band_ref[level, kind, place] for place in range(3))
    zero = jnp.zeros_like(a)
    left = jnp.concatenate([a, b, c, zero], axis=0)
    right = jnp.concatenate([zero, a, b, c], axis=0)
    return jnp.concatenate([left, right], axis=1)


def windows(parts, first_row):
    rows = []
    for block in range(4):
        for part in parts:
            lanes = [
                part[first_row : first_row + ROWS, 128 * tile : 128 * tile + 128]
                for tile in ((2 * block - 1) % 8, 2 * block, 2 * block + 1, (2 * block + 2) % 8)
            ]
            rows.append(jnp.concatenate(lanes, axis=1))
    return jnp.concatenate(rows, axis=0)


def lane_sums(values):
    i, j = iotas(8, 128)
    result = jnp.zeros((8, 128), F32)
    for lane, value in values:
        result = jnp.where((i == 0) & (j == lane), value, result)
    return result


def total(x):
    return jnp.sum(x, axis=(0, 1), keepdims=True)


def fine_kernel(scalars, *refs):
    if scalars:
        r_ref, a_ref, *refs = refs
    x_ref, d_ref, before_ref, after_ref, high_ref, low_ref, band_ref, *outs = refs
    fine_ref = outs[0]
    highs, lows = [], []
    for member in range(2):
        rows = []
        for level in range(4):
            pair = 4 * member + level
            rows += [
                before_ref[pair],
                d_ref[ROWS * pair : ROWS * pair + ROWS],
                after_ref[pair],
            ]
        high, low = split2(jnp.concatenate(rows, axis=0))
        passed = mm(high_ref[...], high) + mm(high_ref[...], low) + mm(low_ref[...], high)
        high, low = split2(passed)
        highs.append(high)
        lows.append(low)
    for level in range(4):
        result = None
        for kind in range(2):
            high = windows(highs, 128 * kind + ROWS * level)
            low = windows(lows, 128 * kind + ROWS * level)
            table_high = banded(band_ref, level, 2 * kind)
            table_low = banded(band_ref, level, 2 * kind + 1)
            term = mm(high, table_high) + mm(low, table_high) + mm(high, table_low)
            result = term if result is None else result + term
        for block in range(4):
            summed = None
            for member in range(2):
                row = ROWS * (4 * member + level)
                x = x_ref[row : row + ROWS, 256 * block : 256 * block + 256].astype(F32)
                at = 64 * block + ROWS * member
                term = x * result[at : at + ROWS]
                summed = term if summed is None else summed + term
            fine_ref[ROWS * level : ROWS * level + ROWS, 256 * block : 256 * block + 256] = summed
    if scalars:
        r, a, fine = r_ref[...], natural(a_ref), fine_ref[...]
        pairs = ((r, r), (r, a), (a, a), (r, fine), (a, fine))
        outs[1][...] = lane_sums([(k, total(p * q)) for k, (p, q) in enumerate(pairs)])


def smooth_kernel(c_ref, lat_ref, lon_ref, out_ref):
    c = c_ref[...].reshape(64, 256)
    out_ref[...] = exact_mm(exact_mm(lat_ref[...], c), lon_ref[...]).reshape(TILES, 8, 256)


def smooth_dots_kernel(c_ref, first_ref, lat_ref, lon_ref, sums_ref, out_ref):
    c = c_ref[...].reshape(64, 256)
    smoothed = exact_mm(exact_mm(lat_ref[...], c), lon_ref[...])
    out_ref[:, :8, :] = smoothed.reshape(TILES, 8, 256)
    dots = (total(first_ref[...].reshape(64, 256) * smoothed), total(c * smoothed))
    sums = sums_ref[...] + lane_sums([(5 + k, dot * 16.0) for k, dot in enumerate(dots)])
    sums = jnp.concatenate([sums, jnp.zeros_like(sums)], axis=1)
    for tile in range(TILES):
        out_ref[tile, 8:16, :] = sums


def blended(x_ref, fine_ref, smoothed):
    spread = prolong(smoothed.reshape(64, 256))
    return (
        fine_ref[...]
        + x_ref[:128].astype(F32) * spread[:128]
        + x_ref[128:].astype(F32) * spread[128:]
    )


def partial_kernel(x_ref, fine_ref, smoothed_ref, out_ref):
    p = blended(x_ref, fine_ref, smoothed_ref[...])
    for tall in range(16):
        for wide in range(8):
            out_ref[2 * tall + wide // 4, 8 * (wide % 4) : 8 * (wide % 4) + 8, :] = p[
                8 * tall : 8 * tall + 8, 128 * wide : 128 * wide + 128
            ]


def last_partial_kernel(x_ref, fine_ref, smoothed_ref, out_ref):
    p = blended(x_ref, fine_ref, smoothed_ref[:, :8, :])
    turned = p.T
    sums = jnp.sum(smoothed_ref[:, 8:16, :128], axis=0)
    for group in range(GROUPS):
        out_ref[group, :32, :] = turned[32 * group : 32 * group + 32]
        out_ref[group, 32:40, :] = sums


def share_kernel(scale, group_ref, arrived_ref, r_ref, out_ref):
    group = group_ref[0]
    share = r_ref[
        pl.ds(pl.multiple_of(8 * (group >> 1), 8), 8),
        pl.ds(pl.multiple_of(512 * (group & 1), 512), 512),
    ]
    share = jnp.concatenate([share[:, 128 * k : 128 * k + 128] for k in range(4)], axis=0)
    share = share + jnp.sum(arrived_ref[...], axis=0) * scale
    for other in range(GROUPS):
        out_ref[other] = share


def final_kernel(scale, group_ref, arrived_ref, r_ref, a_ref, x_out, res_out, r_turned, a_turned):
    group = group_ref[0]
    wide = group >> 2
    lanes = pl.ds(pl.multiple_of(128 * wide, 128), 128)
    r_turned[...] = r_ref[:, lanes].T
    rows = [
        a_ref[2 * tall + (wide >> 2), pl.ds(pl.multiple_of(8 * (wide & 3), 8), 8), :]
        for tall in range(16)
    ]
    a_turned[...] = jnp.concatenate(rows, axis=0).T
    mine = pl.ds(pl.multiple_of(32 * (group & 3), 32), 32)
    r, a = r_turned[mine, :], a_turned[mine, :]
    arrived = jnp.sum(arrived_ref[...], axis=0)
    b = a + arrived[:32] * scale
    i, j = iotas(8, 128)
    rr, ra, aa, rf, af, rc, ac = (
        total(jnp.where((i == 0) & (j == k), arrived[32:40], 0.0)) for k in range(7)
    )
    rr, ra, aa = rr / GROUPS, ra / GROUPS, aa / GROUPS
    step = rr / ra
    rb = ra + (rf + rc) * scale
    ab = aa + (af + ac) * scale
    squares = step * step * aa - rr
    next_step = squares / ((ra - step * aa) - step * (rb - step * ab))
    r_next = r - step * a
    x_out[...] = (step * r + next_step * r_next).T.reshape(4, ROWS, 32)
    res_out[...] = (r_next - next_step * (a - step * b)).T.reshape(4, ROWS, 32)


VMEM = pl.BlockSpec(memory_space=pltpu.VMEM)
SMEM = pl.BlockSpec(memory_space=pltpu.SMEM)


def call(kernel, outs, specs, args, flops, scratch=(), limit=48):
    shapes = [jax.ShapeDtypeStruct(*out) for out in outs]
    size = sum(a.size * a.dtype.itemsize for a in args)
    return pl.pallas_call(
        kernel,
        out_shape=shapes if len(shapes) > 1 else shapes[0],
        in_specs=specs,
        out_specs=[VMEM] * len(shapes) if len(shapes) > 1 else VMEM,
        scratch_shapes=list(scratch),
        compiler_params=pltpu.CompilerParams(vmem_limit_bytes=limit << 20),
        cost_estimate=pl.CostEstimate(flops=flops, bytes_accessed=size, transcendentals=0),
    )(*args)


def exchange(blocks, axis):
    return lax.all_to_all(blocks, axis, 0, 0, tiled=True)


def normalized(fine_taps):
    energy = fine_taps[:, :, 0] ** 2 + 2.0 * jnp.sum(fine_taps[:, :, 1:] ** 2, axis=2)
    return fine_taps / jnp.sqrt(energy)[:, :, None]


def twice(taps):
    full = jnp.concatenate([taps[:, :0:-1], taps], axis=1)
    padded = jnp.pad(full, ((0, 0), (8, 8)))
    return jnp.stack(
        [jnp.sum(full * padded[:, 8 - o : 17 - o], axis=1) for o in range(9)], axis=1
    )


def local(perturbations, right_side, fine_taps, coarse_lat, coarse_lon):
    count, levels, height, extent = perturbations.shape
    members = count * lax.axis_size(MEM)
    scale = 1.0 / (members - 1)
    kernel = normalized(fine_taps)
    tile = lax.axis_index("tile").astype(jnp.int32).reshape(1)
    group = lax.axis_index(MEM).astype(jnp.int32).reshape(1)
    x = perturbations.reshape(count * levels * height, extent)
    r = right_side.reshape(levels * height, extent)
    full, half = ((256, LON), F32), ((128, LON), F32)
    coarse, edge = ((PAIRS, 8, 256), F32), ((PAIRS, 8, LON), F32)
    up = [(i, i + 1) for i in range(TILES - 1)]
    down = [(i + 1, i) for i in range(TILES - 1)]

    tables = call(
        table_kernel,
        [((256, 192), BF16), ((256, 192), BF16), ((4, 4, 3, 128, 128), BF16)],
        [SMEM] * 3,
        (tile, kernel[0], twice(kernel[1])),
        10**9,
    )

    def details(v):
        c, d, top, bottom = call(
            detail_kernel, [coarse, full, edge, edge], [VMEM] * 2, (x, v), 10**9
        )
        before = lax.ppermute(bottom, "tile", up)
        after = lax.ppermute(top, "tile", down)
        return exchange(c, "tile"), (x, d, before, after, *tables)

    c_first, fine_args = details(r)
    fine = call(
        functools.partial(fine_kernel, False), [half], [VMEM] * 7, fine_args, 5 * 10**9
    )
    smoothed = call(
        smooth_kernel, [coarse], [VMEM] * 3, (c_first, coarse_lat, coarse_lon), 10**8
    )
    smoothed = exchange(smoothed, "tile")
    shares = call(
        partial_kernel, [((GROUPS, 32, 128), F32)], [VMEM] * 3, (x, fine, smoothed), 10**9
    )
    arrived = exchange(shares, MEM)
    share = call(
        functools.partial(share_kernel, scale),
        [((GROUPS, 32, 128), F32)],
        [SMEM, VMEM, VMEM],
        (group, arrived, r),
        10**6,
    )
    a = exchange(share, MEM)

    c_next, fine_args = details(a)
    fine, sums = call(
        functools.partial(fine_kernel, True),
        [half, ((8, 128), F32)],
        [VMEM] * 9,
        (r, a, *fine_args),
        5 * 10**9,
    )
    smoothed = call(
        smooth_dots_kernel,
        [((TILES, 16, 256), F32)],
        [VMEM] * 5,
        (c_next, c_first, coarse_lat, coarse_lon, sums),
        10**8,
    )
    smoothed = exchange(smoothed, "tile")
    shares = call(
        last_partial_kernel, [((GROUPS, 40, 128), F32)], [VMEM] * 3, (x, fine, smoothed), 10**9
    )
    arrived = exchange(shares, MEM)
    out = ((levels, height, extent // GROUPS), F32)
    return tuple(
        call(
            functools.partial(final_kernel, scale),
            [out, out],
            [SMEM, VMEM, VMEM, VMEM],
            (group, arrived, r, a),
            10**6,
            scratch=(pltpu.VMEM((128, 128), F32), pltpu.VMEM((128, 128), F32)),
        )
    )


def solution(mesh):
    torus = Mesh(
        mesh.devices.reshape(4, 4, 2, mesh.shape["tile"]), ("mem_0", "mem_1", "mem_2", "tile")
    )
    placed = (P(MEM, None, "tile", None), P(None, "tile", None), P(), P(), P())
    return jax.shard_map(
        local,
        mesh=torus,
        in_specs=placed,
        out_specs=(P(None, "tile", MEM), P(None, "tile", MEM)),
        check_vma=False,
    )
```

profile of v0, /device:TPU:1, one launch (start us, length us, event | category | flops | bytes accessed | tf_op | source)
XLA Modules:
  0.0 133.2 jit_solution(15177034076429039731)
XLA Ops:
  0.6 0.0 copy-start
  0.6 1.0 copy-done
  1.7 1.0 copy-done.4
  2.7 1.4 %shard_map.68 = (f32[8,8,256]{2,1,0:T(8,128)}, f32[256,1024]{1,0:T(8,128)S(1)}, f32[8,8,1024]{2,1,0:T(8,128)S(1)}, f32[8,8,1024]{2,1,0:T(8,128)S(1)}) custom-call(bf16[256,1024]{1,0:T(8,128)(2,1)S(1)} %bitcast.30, f32[128,1024]{1,0:T(8,128)S(1)} %bitcast.26), custom_call_target="tpu_custom_call" | custom-call | flops 1000000000 | bytes 1048576 | tf_op jit(solution)/shard_map/pallas_call | solution.py:309
  4.1 9.0 %all-to-all-start = ((f32[8,8,256]{2,1,0:T(8,128)}), f32[8,8,256]{2,1,0:T(8,128)S(1)}, u32[]{:S(2)}, u32[]{:S(2)}) async-start(f32[8,8,256]{2,1,0:T(8,128)} %get-tuple-element.21), calls=%async_computation | async-start | bytes 131072 | tf_op jit(solution)/shard_map/all_to_all | solution.py:321
  13.1 3.4 %collective-permute-start = (f32[8,8,1024]{2,1,0:T(8,128)S(1)}, f32[8,8,1024]{2,1,0:T(8,128)S(1)}, u32[]{:S(2)}, u32[]{:S(2)}) collective-permute-start(f32[8,8,1024]{2,1,0:T(8,128)S(1)} %get-tuple-element.16), channel_id=1, source_target_pairs={{0,1},{1,2},{2,3},{3,4},{4,5},{5,6},{6,7},{8,9},{9,10},{10,11},{11... | collective-permute-start | bytes 786440 | tf_op jit(solution)/shard_map/ppermute | solution.py:363
  16.5 1.3 collective-permute-start.1
  17.8 0.0 copy-done.13
  17.8 0.2 multiply_reduce_fusion
  18.0 0.1 copy.17
  18.1 0.1 broadcast_divide_fusion
  18.1 0.1 slice.44
  18.2 0.1 rev.3
  18.3 0.1 pad_maximum_fusion
  18.4 0.3 multiply_reduce_fusion.1
  18.7 0.1 copy.15
  18.8 0.1 copy.16
  18.9 0.1 copy.14
  19.0 0.1 copy.13
  19.1 0.1 copy.12
  19.2 0.1 copy.11
  19.3 0.1 copy.10
  19.4 0.1 copy.9
  19.5 0.1 copy.8
  19.6 0.1 stack.39.lon_ref
  19.7 0.0 copy-start.5
  19.7 2.1 %shard_map.69 = (bf16[256,192]{1,0:T(8,128)(2,1)S(1)}, bf16[256,192]{1,0:T(8,128)(2,1)S(1)}, bf16[4,4,3,128,128]{4,3,2,1,0:T(8,128)(2,1)S(1)}) custom-call(s32[1]{0:T(128)} %bitcast.3.tile_ref, f32[4,5]{1,0:T(4,128)S(1)} %get-tuple-element.38.lat_ref, f32[4,9]{1,0:T(4,128)S(1)} %stack.39.lon_ref), custom_call_target="tpu_custom_call" | custom-call | flops 1000000000 | bytes 228 | tf_op jit(solution)/shard_map/pallas_call | solution.py:309
  21.8 0.0 copy-start.10
  21.8 1.2 copy-done.10
  23.0 0.0 all-to-all-done.c_ref.first_ref
  23.0 0.0 copy-done.2
  23.0 0.0 copy-done.3
  23.0 1.1 shard_map.71
  24.1 8.5 %all-to-all-start.1 = ((f32[8,8,256]{2,1,0:T(8,128)}), f32[8,8,256]{2,1,0:T(8,128)S(1)}, u32[]{:S(2)}, u32[]{:S(2)}) async-start(f32[8,8,256]{2,1,0:T(8,128)} %shard_map.71), calls=%async_computation.1 | async-start | bytes 131072 | tf_op jit(solution)/shard_map/all_to_all | solution.py:321
  32.6 0.0 collective-permute-done.refs_2_
  32.6 0.0 collective-permute-done.1.refs_3_
  32.6 0.0 copy-done.5
  32.6 0.0 copy-start.11
  32.6 1.4 %copy-done.11 = bf16[4,4,3,128,128]{4,3,2,1,0:T(8,128)(2,1)S(1)} copy-done((bf16[4,4,3,128,128]{4,3,2,1,0:T(8,128)(2,1)S(1)}, bf16[4,4,3,128,128]{4,3,2,1,0:T(8,128)(2,1)}, u32[]{:S(2)}) %copy-start.11) | copy-done | bytes 1572888
  34.0 2.7 %shard_map.70.fine_ref = f32[128,1024]{1,0:T(8,128)S(1)} custom-call(bf16[256,1024]{1,0:T(8,128)(2,1)S(1)} %bitcast.31, f32[256,1024]{1,0:T(8,128)S(1)} %get-tuple-element.15.refs_1_, f32[8,8,1024]{2,1,0:T(8,128)S(1)} %collective-permute-done.refs_2_, f32[8,8,1024]{2,1,0:T(8,128)S(1)} %collective-permute-done.1.refs_3_, ...), custom_call_target="tpu_custom_call" | custom-call | flops 5000000000 | bytes 3866624 | tf_op jit(solution)/shard_map/pallas_call | solution.py:309
  36.8 0.8 copy-done.8
  37.6 2.3 %all-to-all-done.1.smoothed_ref = f32[8,8,256]{2,1,0:T(8,128)S(1)} async-done(((f32[8,8,256]{2,1,0:T(8,128)}), f32[8,8,256]{2,1,0:T(8,128)S(1)}, u32[]{:S(2)}, u32[]{:S(2)}) %all-to-all-start.1) | async-done | bytes 65568 | tf_op jit(solution)/shard_map/all_to_all | solution.py:321
  39.8 1.0 copy-done.9
  40.9 1.4 %shard_map.72 = f32[32,32,128]{2,1,0:T(8,128)} custom-call(bf16[256,1024]{1,0:T(8,128)(2,1)S(1)} %bitcast.32, f32[128,1024]{1,0:T(8,128)S(1)} %copy-done.9, f32[8,8,256]{2,1,0:T(8,128)S(1)} %all-to-all-done.1.smoothed_ref), custom_call_target="tpu_custom_call" | custom-call | flops 1000000000 | bytes 1114112 | tf_op jit(solution)/shard_map/pallas_call | solution.py:309
  42.2 10.3 %all-to-all-start.2 = ((f32[32,32,128]{2,1,0:T(8,128)}), f32[32,32,128]{2,1,0:T(8,128)S(1)}, u32[]{:S(2)}, u32[]{:S(2)}) async-start(f32[32,32,128]{2,1,0:T(8,128)} %shard_map.72), calls=%async_computation.2 | async-start | bytes 1048576 | tf_op jit(solution)/shard_map/all_to_all | solution.py:321
  52.6 11.5 %all-to-all-done.2.arrived_ref = f32[32,32,128]{2,1,0:T(8,128)S(1)} async-done(((f32[32,32,128]{2,1,0:T(8,128)}), f32[32,32,128]{2,1,0:T(8,128)S(1)}, u32[]{:S(2)}, u32[]{:S(2)}) %all-to-all-start.2) | async-done | bytes 524320 | tf_op jit(solution)/shard_map/all_to_all | solution.py:321
  64.1 0.1 shard_map.73
  64.2 15.2 %all_to_all.35.v_ref.refs_1_.a_ref = f32[32,32,128]{2,1,0:T(8,128)S(1)} all-to-all(f32[32,32,128]{2,1,0:T(8,128)S(1)} %shard_map.73), channel_id=1, replica_groups=mesh['mem_0'=4,'mem_1'=4,'mem_2'=2,'tile'=8] {'mem_0','mem_1','mem_2'}, dimensions={0} | all-to-all | bytes 1048576 | tf_op jit(solution)/shard_map/all_to_all | solution.py:321
  79.4 1.4 %shard_map.74 = (f32[8,8,256]{2,1,0:T(8,128)}, f32[256,1024]{1,0:T(8,128)S(1)}, f32[8,8,1024]{2,1,0:T(8,128)S(1)}, f32[8,8,1024]{2,1,0:T(8,128)S(1)}) custom-call(bf16[256,1024]{1,0:T(8,128)(2,1)S(1)} %bitcast.33, f32[32,32,128]{2,1,0:T(8,128)S(1)} %all_to_all.35.v_ref.refs_1_.a_ref), custom_call_target="tpu_custom_call" | custom-call | flops 1000000000 | bytes 1048576 | tf_op jit(solution)/shard_map/pallas_call | solution.py:309
  80.8 1.0 copy-done.6
  81.8 2.2 %collective-permute-start.2 = (f32[8,8,1024]{2,1,0:T(8,128)S(1)}, f32[8,8,1024]{2,1,0:T(8,128)S(1)}, u32[]{:S(2)}, u32[]{:S(2)}) collective-permute-start(f32[8,8,1024]{2,1,0:T(8,128)S(1)} %get-tuple-element.23), channel_id=1, source_target_pairs={{0,1},{1,2},{2,3},{3,4},{4,5},{5,6},{6,7},{8,9},{9,10},{10,11},{11... | collective-permute-start | bytes 786440 | tf_op jit(solution)/shard_map/ppermute | solution.py:363
  84.0 1.3 collective-permute-start.3
  85.3 6.6 %all-to-all-start.4 = ((f32[8,8,256]{2,1,0:T(8,128)}), f32[8,8,256]{2,1,0:T(8,128)S(1)}, u32[]{:S(2)}, u32[]{:S(2)}) async-start(f32[8,8,256]{2,1,0:T(8,128)} %get-tuple-element.26), calls=%async_computation.4 | async-start | bytes 131072 | tf_op jit(solution)/shard_map/all_to_all | solution.py:321
  91.9 0.0 collective-permute-done.2.refs_4_
  91.9 1.1 collective-permute-done.3.refs_5_
  93.0 1.2 copy-done.7
  94.2 1.4 %copy-done.12 = bf16[4,4,3,128,128]{4,3,2,1,0:T(8,128)(2,1)S(1)} copy-done((bf16[4,4,3,128,128]{4,3,2,1,0:T(8,128)(2,1)S(1)}, bf16[4,4,3,128,128]{4,3,2,1,0:T(8,128)(2,1)}, u32[]{:S(2)}) %copy-start.12) | copy-done | bytes 1572888
  95.6 2.9 %shard_map.75 = (f32[128,1024]{1,0:T(8,128)S(1)}, f32[8,128]{1,0:T(8,128)S(1)}) custom-call(f32[128,1024]{1,0:T(8,128)S(1)} %bitcast.28, f32[32,32,128]{2,1,0:T(8,128)S(1)} %all_to_all.35.v_ref.refs_1_.a_ref, bf16[256,1024]{1,0:T(8,128)(2,1)S(1)} %bitcast.34, f32[256,1024]{1,0:T(8,128)S(1)} %copy-done.7, f32[8,8,1024]{2,1,0:T(8,128)S(1)} %collective-permute-done.2.refs_4_, ...), custom_call_target="tpu_custom_call" | custom-call | flops 5000000000 | bytes 4915200 | tf_op jit(solution)/shard_map/pallas_call | solution.py:309
  98.6 0.5 all-to-all-done.4.c_ref
  99.1 0.6 shard_map.76
  99.7 12.7 %all_to_all.36.smoothed_ref = f32[8,16,256]{2,1,0:T(8,128)S(1)} all-to-all(f32[8,16,256]{2,1,0:T(8,128)S(1)} %shard_map.76), channel_id=1, replica_groups=mesh['mem_0'=4,'mem_1'=4,'mem_2'=2,'tile'=8] {'tile'}, dimensions={0} | all-to-all | bytes 262144 | tf_op jit(solution)/shard_map/all_to_all | solution.py:321
  112.5 0.7 shard_map.77
  113.2 19.1 %all_to_all.37.arrived_ref = f32[32,40,128]{2,1,0:T(8,128)S(1)} all-to-all(f32[32,40,128]{2,1,0:T(8,128)S(1)} %shard_map.77), channel_id=1, replica_groups=mesh['mem_0'=4,'mem_1'=4,'mem_2'=2,'tile'=8] {'mem_0','mem_1','mem_2'}, dimensions={0} | all-to-all | bytes 1310720 | tf_op jit(solution)/shard_map/all_to_all | solution.py:321
  132.3 0.9 shard_map.78
  (13 shorter events, 0.0 us)
Async XLA Ops:
  0.6 1.0 copy-start
  1.7 1.0 copy-start.4
  2.7 15.1 %copy-start.13 = (f32[2,4,5]{2,1,0:T(4,128)S(1)}, f32[2,4,5]{2,1,0:T(4,128)}, u32[]{:S(2)}) copy-start(f32[2,4,5]{2,1,0:T(4,128)} %param.7) | copy-start | bytes 484
  4.1 18.9 %all-to-all-start = ((f32[8,8,256]{2,1,0:T(8,128)}), f32[8,8,256]{2,1,0:T(8,128)S(1)}, u32[]{:S(2)}, u32[]{:S(2)}) async-start(f32[8,8,256]{2,1,0:T(8,128)} %get-tuple-element.21), calls=%async_computation | async-start | bytes 131072 | tf_op jit(solution)/shard_map/all_to_all | solution.py:321
  13.1 19.5 %collective-permute-start = (f32[8,8,1024]{2,1,0:T(8,128)S(1)}, f32[8,8,1024]{2,1,0:T(8,128)S(1)}, u32[]{:S(2)}, u32[]{:S(2)}) collective-permute-start(f32[8,8,1024]{2,1,0:T(8,128)S(1)} %get-tuple-element.16), channel_id=1, source_target_pairs={{0,1},{1,2},{2,3},{3,4},{4,5},{5,6},{6,7},{8,9},{9,10},{10,11},{11... | collective-permute-start | bytes 786440 | tf_op jit(solution)/shard_map/ppermute | solution.py:363
  16.5 16.1 %collective-permute-start.1 = (f32[8,8,1024]{2,1,0:T(8,128)S(1)}, f32[8,8,1024]{2,1,0:T(8,128)S(1)}, u32[]{:S(2)}, u32[]{:S(2)}) collective-permute-start(f32[8,8,1024]{2,1,0:T(8,128)S(1)} %get-tuple-element.17), channel_id=1, source_target_pairs={{1,0},{2,1},{3,2},{4,3},{5,4},{6,5},{7,6},{9,8},{10,9},{11,10},{12... | collective-permute-start | bytes 786440 | tf_op jit(solution)/shard_map/ppermute | solution.py:364
  19.7 3.3 %copy-start.2 = (f32[256,256]{1,0:T(8,128)S(1)}, f32[256,256]{1,0:T(8,128)}, u32[]{:S(2)}) copy-start(f32[256,256]{1,0:T(8,128)} %lon_ref.3) | copy-start | bytes 786436
  19.7 3.3 %copy-start.3 = (f32[64,64]{1,0:T(8,128)S(1)}, f32[64,64]{1,0:T(8,128)}, u32[]{:S(2)}) copy-start(f32[64,64]{1,0:T(8,128)} %lat_ref.3) | copy-start | bytes 49156
  19.7 12.9 %copy-start.5 = (bf16[2,4,32,1024]{3,2,1,0:T(8,128)(2,1)S(1)}, bf16[2,4,32,1024]{3,2,1,0:T(8,128)(2,1)}, u32[]{:S(2)}) copy-start(bf16[2,4,32,1024]{3,2,1,0:T(8,128)(2,1)} %param.5) | copy-start | bytes 1572868
  21.8 1.2 copy-start.10
  24.1 15.7 %all-to-all-start.1 = ((f32[8,8,256]{2,1,0:T(8,128)}), f32[8,8,256]{2,1,0:T(8,128)S(1)}, u32[]{:S(2)}, u32[]{:S(2)}) async-start(f32[8,8,256]{2,1,0:T(8,128)} %shard_map.71), calls=%async_computation.1 | async-start | bytes 131072 | tf_op jit(solution)/shard_map/all_to_all | solution.py:321
  32.6 1.4 %copy-start.11 = (bf16[4,4,3,128,128]{4,3,2,1,0:T(8,128)(2,1)S(1)}, bf16[4,4,3,128,128]{4,3,2,1,0:T(8,128)(2,1)}, u32[]{:S(2)}) copy-start(bf16[4,4,3,128,128]{4,3,2,1,0:T(8,128)(2,1)} %copy-done.10) | copy-start | bytes 4718596
  36.8 0.8 copy-start.8
  37.6 26.6 %copy-start.1 = (f32[4,32,1024]{2,1,0:T(8,128)S(1)}, f32[4,32,1024]{2,1,0:T(8,128)}, u32[]{:S(2)}) copy-start(f32[4,32,1024]{2,1,0:T(8,128)} %param.6) | copy-start | bytes 1572868
  39.8 1.0 copy-start.9
  42.2 21.9 %all-to-all-start.2 = ((f32[32,32,128]{2,1,0:T(8,128)}), f32[32,32,128]{2,1,0:T(8,128)S(1)}, u32[]{:S(2)}, u32[]{:S(2)}) async-start(f32[32,32,128]{2,1,0:T(8,128)} %shard_map.72), calls=%async_computation.2 | async-start | bytes 1048576 | tf_op jit(solution)/shard_map/all_to_all | solution.py:321
  80.8 1.0 copy-start.6
  81.8 10.1 %collective-permute-start.2 = (f32[8,8,1024]{2,1,0:T(8,128)S(1)}, f32[8,8,1024]{2,1,0:T(8,128)S(1)}, u32[]{:S(2)}, u32[]{:S(2)}) collective-permute-start(f32[8,8,1024]{2,1,0:T(8,128)S(1)} %get-tuple-element.23), channel_id=1, source_target_pairs={{0,1},{1,2},{2,3},{3,4},{4,5},{5,6},{6,7},{8,9},{9,10},{10,11},{11... | collective-permute-start | bytes 786440 | tf_op jit(solution)/shard_map/ppermute | solution.py:363
  84.0 9.0 %collective-permute-start.3 = (f32[8,8,1024]{2,1,0:T(8,128)S(1)}, f32[8,8,1024]{2,1,0:T(8,128)S(1)}, u32[]{:S(2)}, u32[]{:S(2)}) collective-permute-start(f32[8,8,1024]{2,1,0:T(8,128)S(1)} %get-tuple-element.24), channel_id=1, source_target_pairs={{1,0},{2,1},{3,2},{4,3},{5,4},{6,5},{7,6},{9,8},{10,9},{11,10},{12... | collective-permute-start | bytes 786440 | tf_op jit(solution)/shard_map/ppermute | solution.py:364
  85.3 13.8 %all-to-all-start.4 = ((f32[8,8,256]{2,1,0:T(8,128)}), f32[8,8,256]{2,1,0:T(8,128)S(1)}, u32[]{:S(2)}, u32[]{:S(2)}) async-start(f32[8,8,256]{2,1,0:T(8,128)} %get-tuple-element.26), calls=%async_computation.4 | async-start | bytes 131072 | tf_op jit(solution)/shard_map/all_to_all | solution.py:321
  93.0 1.2 copy-start.7
  94.2 1.4 %copy-start.12 = (bf16[4,4,3,128,128]{4,3,2,1,0:T(8,128)(2,1)S(1)}, bf16[4,4,3,128,128]{4,3,2,1,0:T(8,128)(2,1)}, u32[]{:S(2)}) copy-start(bf16[4,4,3,128,128]{4,3,2,1,0:T(8,128)(2,1)} %copy-done.10) | copy-start | bytes 4718596
where the time goes:
time: 134 us; the launch traced here: 133 us
  blocking collectives  47.1 us (35%)
  starting transfers between devices  42.5 us (32%)
  waiting for transfers between devices  15.5 us (12%)
  Pallas kernels  15.4 us (11%)
  local copies, waits for them, and re-layouts  11.3 us (8%)
    all_to_all x3, blocking collectives, exchange(): return lax.all_to_all(blocks, axis, 0, 0, tiled=True)  47.1 us
    all_to_all x4, starting transfers between devices, exchange(): return lax.all_to_all(blocks, axis, 0, 0, tiled=True)  34.4 us
    pallas_call x11, Pallas kernels, call(): pl.pallas_call(kernel, out_shape=shapes if len(shapes) > 1 else shapes[0]...  15.4 us
    all_to_all x4, waiting for transfers between devices, exchange(): return lax.all_to_all(blocks, axis, 0, 0, tiled=True)  14.3 us
    unnamed x29, local copies, waits for them, and re-layouts  10.2 us
    ppermute x2, starting transfers between devices, details(): before = lax.ppermute(bottom, 'tile', up)  5.56 us
  transfers between devices with their start and end apart: 8, of which 4 were waited for; matrix products, arithmetic and copies ran while one was open for 1% of the time, Pallas kernels for 7%

commit v1 on v0

v1 whole, which is shorter than its diff:
```python
import functools

import jax
import jax.numpy as jnp
from jax import lax
from jax.experimental import pallas as pl
from jax.experimental.pallas import tpu as pltpu
from jax.sharding import Mesh
from jax.sharding import PartitionSpec as P

MEM = ("mem_0", "mem_1", "mem_2")
F32 = jnp.float32
BF16 = jnp.bfloat16
EXACT = lax.Precision.HIGHEST
PAIRS, ROWS, LON = 8, 32, 1024
GROUPS, TILES = 32, 8


def mm(a, b):
    return jnp.dot(a, b, preferred_element_type=F32)


def exact_mm(a, b):
    return jnp.dot(a, b, preferred_element_type=F32, precision=EXACT)


def split2(x):
    high = x.astype(BF16)
    return high, (x - high.astype(F32)).astype(BF16)


def split3(x):
    high = x.astype(BF16)
    rest = x - high.astype(F32)
    mid = rest.astype(BF16)
    return high, mid, (rest - mid.astype(F32)).astype(BF16)


def iotas(rows, cols):
    return (
        lax.broadcasted_iota(jnp.int32, (rows, cols), 0),
        lax.broadcasted_iota(jnp.int32, (rows, cols), 1),
    )


def shrink_table(rows, cols, along_rows):
    i, j = iotas(rows, cols)
    hit = (i >> 2) == j if along_rows else i == (j >> 2)
    return jnp.where(hit, 0.25, 0.0).astype(BF16)


def expand_table(rows, cols, along_rows):
    i, j = iotas(rows, cols)
    hit = (i >> 2) == j if along_rows else i == (j >> 2)
    return jnp.where(hit, 1.0, 0.0).astype(BF16)


def block_mean(w):
    table = shrink_table(64, 256, False)
    part = sum(mm(table, piece) for piece in split3(w))
    stacked = jnp.concatenate([part[:, :512], part[:, 512:]], axis=0)
    table = shrink_table(512, 128, True)
    small = sum(mm(piece, table) for piece in split3(stacked))
    return jnp.concatenate([small[:64], small[64:]], axis=1)


def prolong(c):
    table = expand_table(256, 64, True)
    tall = sum(mm(table, piece) for piece in split2(c))
    stacked = jnp.concatenate([tall[:, :128], tall[:, 128:]], axis=0)
    table = expand_table(128, 512, False)
    wide = sum(mm(piece, table) for piece in split2(stacked))
    return jnp.concatenate([wide[:256], wide[256:]], axis=1)


def natural(blocks):
    rows = []
    for tall in range(16):
        lanes = [
            blocks[2 * tall + wide // 4, 8 * (wide % 4) : 8 * (wide % 4) + 8, :]
            for wide in range(8)
        ]
        rows.append(jnp.concatenate(lanes, axis=1))
    return jnp.concatenate(rows, axis=0)


def detail_kernel(x_ref, v_ref, *out_refs):
    detail(x_ref[...], natural(v_ref), *out_refs)


def first_detail_kernel(x_hbm, v_hbm, *refs):
    *out_refs, x_ref, v_ref, x_sems, v_sems = refs
    copies = []
    for k in range(4):
        rows = pl.ds(32 * k, 32)
        copies.append(pltpu.make_async_copy(v_hbm.at[rows], v_ref.at[rows], v_sems.at[k]))
        rows = pl.ds(64 * k, 64)
        copies.append(pltpu.make_async_copy(x_hbm.at[rows], x_ref.at[rows], x_sems.at[k]))
    for copy in copies:
        copy.start()
    for copy in copies:
        copy.wait()
    detail(x_ref[...], v_ref[...], *out_refs)


def detail(x, v, c_ref, own_ref, top_ref, bottom_ref):
    w = x.astype(F32) * jnp.concatenate([v, v], axis=0)
    c = block_mean(w)
    if c_ref.shape == (TILES, 64, 256):
        for tile in range(TILES):
            c_ref[tile] = c
    else:
        c_ref[...] = c.reshape(PAIRS, 8, 256)
    own_ref[...] = c
    d = w - prolong(c)
    for pair in range(PAIRS):
        top_ref[pair] = d[ROWS * pair : ROWS * pair + 8]
        bottom_ref[pair] = d[ROWS * pair + 24 : ROWS * pair + 32]


def table_kernel(place_ref, taps_ref, lat_ref, *refs):
    *hbm_refs, mix_ref, high_ref, low_ref, band_ref, sems = refs
    tile = place_ref[0]
    taps = taps_ref[...]
    square = taps * taps
    energy = square[:, 0:1] + 2.0 * jnp.sum(square[:, 1:5], axis=1, keepdims=True)
    taps = taps / jnp.sqrt(energy)
    single = [taps[:, o : o + 1] for o in range(5)]
    once = [single[abs(o)] for o in range(-4, 5)]
    double = []
    for o in range(9):
        terms = [once[i] * once[o + 8 - i] for i in range(o, 9)]
        double.append(functools.reduce(jnp.add, terms))
    i, j = iotas(160, 192)
    first = jnp.zeros((160, 192), F32)
    for level in range(4):
        row, col = i - 40 * level, j - 48 * level
        dist = jnp.abs(col - row - 4)
        spot, source = tile * ROWS - 4 + row, tile * ROWS - 8 + col
        fits = (row >= 0) & (row < 40) & (col >= 0) & (col < 48)
        fits = fits & (spot >= 0) & (spot < ROWS * TILES)
        fits = fits & (source >= 0) & (source < ROWS * TILES)
        dist = jnp.where(fits, dist, 9)
        for o in range(5):
            first = jnp.where(dist == o, single[o][level : level + 1], first)
    i, j = iotas(128, 160)
    second = jnp.zeros((128, 160), F32)
    for level in range(4):
        row, col = i - 32 * level, j - 40 * level
        fits = (row >= 0) & (row < 32) & (col >= 0) & (col < 40)
        dist = jnp.where(fits, jnp.abs(col - row - 4), 9)
        for o in range(5):
            second = jnp.where(dist == o, single[o][level : level + 1], second)
    both = exact_mm(second, first)
    i, j = iotas(128, 128)
    mean = jnp.where((i >> 2) == (j >> 2), 0.25, 0.0)
    high, low = split2(jnp.concatenate([both, exact_mm(mean, both)], axis=0))
    high_ref[...] = high
    low_ref[...] = low
    i, j = iotas(8, 128)
    before = jnp.abs(i - 8 - j)
    after = jnp.abs(i + 128 - j)
    i, j = iotas(128, 128)
    inner = jnp.abs(i - j)
    for level in range(4):
        corner = (jnp.zeros((8, 128), F32), jnp.zeros((8, 128), F32))
        middle = jnp.zeros((128, 128), F32)
        for o in range(9):
            tap = double[o][4 + level : 5 + level]
            corner = tuple(
                jnp.where(dist == o, tap, c) for dist, c in zip((before, after), corner)
            )
            middle = jnp.where(inner == o, tap, middle)
        rest = jnp.zeros((120, 128), F32)
        bands = jnp.concatenate([rest, corner[0], middle, corner[1], rest], axis=0)
        parts = jnp.concatenate([corner[0], middle, corner[1]], axis=0)
        meant = -exact_mm(parts, mean)
        meant = jnp.concatenate([rest, meant, rest], axis=0)
        for kind, piece in enumerate((*split2(bands), *split2(meant))):
            band_ref[level, kind] = piece
    i, j = iotas(64, 512)
    repeat = jnp.where((i >> 3) == (j >> 6), jnp.where((i & 7) == (j & 7), 1.0, 0.0), 0.0)
    mine = lat_ref[pl.ds(pl.multiple_of(8 * tile, 8), 8), :]
    wide = exact_mm(mine, repeat)
    mix = jnp.concatenate([wide] * PAIRS, axis=0)
    mix_ref[...] = jnp.where((i >> 3) == ((j >> 3) & 7), mix, 0.0)
    copies = [
        pltpu.make_async_copy(source, target, sems.at[k])
        for k, (source, target) in enumerate(zip((high_ref, low_ref, band_ref), hbm_refs))
    ]
    for copy in copies:
        copy.start()
    for copy in copies:
        copy.wait()


def banded(band_ref, level, kind):
    band = band_ref[level, kind]
    zero = jnp.zeros((128, 128), BF16)
    left = jnp.concatenate([band, zero], axis=0)
    right = jnp.concatenate([zero, band], axis=0)
    return jnp.concatenate([left, right], axis=1)


def windows(parts, first_row):
    rows = []
    for block in range(4):
        for part in parts:
            lanes = [
                part[first_row : first_row + ROWS, 128 * tile : 128 * tile + 128]
                for tile in ((2 * block - 1) % 8, 2 * block, 2 * block + 1, (2 * block + 2) % 8)
            ]
            rows.append(jnp.concatenate(lanes, axis=1))
    return jnp.concatenate(rows, axis=0)


def lane_sums(values):
    i, j = iotas(8, 128)
    result = jnp.zeros((8, 128), F32)
    for lane, value in values:
        result = jnp.where((i == 0) & (j == lane), value, result)
    return result


def total(x):
    return jnp.sum(x, axis=(0, 1), keepdims=True)


def fine_kernel(last, *refs):
    if last:
        r_ref, *refs = refs
    v_ref, x_ref, c_ref, before_ref, after_ref, *refs = refs
    *refs, high_ref, low_ref, band_ref, sems = refs
    copies = [
        pltpu.make_async_copy(source, target, sems.at[k])
        for k, (source, target) in enumerate(zip(refs[:3], (high_ref, low_ref, band_ref)))
    ]
    for copy in copies:
        copy.start()
    outs = refs[3:]
    fine_ref = outs[0]
    v = natural(v_ref) if last else v_ref[...]
    d = x_ref[...].astype(F32) * jnp.concatenate([v, v], axis=0) - prolong(c_ref[...])
    copies[0].wait()
    copies[1].wait()
    highs, lows = [], []
    for member in range(2):
        rows = []
        for level in range(4):
            pair = 4 * member + level
            rows += [before_ref[pair], d[ROWS * pair : ROWS * pair + ROWS], after_ref[pair]]
        high, low = split2(jnp.concatenate(rows, axis=0))
        passed = mm(high_ref[...], high) + mm(high_ref[...], low) + mm(low_ref[...], high)
        high, low = split2(passed)
        highs.append(high)
        lows.append(low)
    copies[2].wait()
    for level in range(4):
        result = None
        for kind in range(2):
            high = windows(highs, 128 * kind + ROWS * level)
            low = windows(lows, 128 * kind + ROWS * level)
            table_high = banded(band_ref, level, 2 * kind)
            table_low = banded(band_ref, level, 2 * kind + 1)
            term = mm(high, table_high) + mm(low, table_high) + mm(high, table_low)
            result = term if result is None else result + term
        for block in range(4):
            summed = None
            for member in range(2):
                row = ROWS * (4 * member + level)
                x = x_ref[row : row + ROWS, 256 * block : 256 * block + 256].astype(F32)
                at = 64 * block + ROWS * member
                term = x * result[at : at + ROWS]
                summed = term if summed is None else summed + term
            fine_ref[ROWS * level : ROWS * level + ROWS, 256 * block : 256 * block + 256] = summed
    if last:
        r, fine = r_ref[...], fine_ref[...]
        pairs = ((r, r), (r, v), (v, v), (r, fine), (v, fine))
        outs[1][...] = lane_sums([(k, total(p * q)) for k, (p, q) in enumerate(pairs)])


def smooth_dots_kernel(c_ref, first_ref, lat_ref, lon_ref, sums_ref, out_ref):
    c = c_ref[...].reshape(64, 256)
    first = first_ref[...]
    smoothed = exact_mm(exact_mm(lat_ref[...], c), lon_ref[...])
    dots = (total(first * smoothed), total(c * smoothed))
    sums = sums_ref[...] + lane_sums([(5 + k, dot * 16.0) for k, dot in enumerate(dots)])
    for tile in range(TILES):
        out_ref[tile, 0:8, :] = smoothed[8 * tile : 8 * tile + 8, :128]
        out_ref[tile, 8:16, :] = smoothed[8 * tile : 8 * tile + 8, 128:]
        out_ref[tile, 16:24, :] = sums


def blended(x_ref, fine_ref, smoothed):
    spread = prolong(smoothed)
    return (
        fine_ref[...]
        + x_ref[:128].astype(F32) * spread[:128]
        + x_ref[128:].astype(F32) * spread[128:]
    )


def partial_kernel(place_ref, x_ref, fine_ref, c_ref, mix_ref, lon_ref, out_ref, mine_ref):
    mine = pl.ds(pl.multiple_of(8 * place_ref[0], 8), 8)
    for tile in range(TILES):
        mine_ref[8 * tile : 8 * tile + 8, :] = c_ref[tile, mine, :]
    across = exact_mm(mix_ref[...], c_ref[...].reshape(512, 256))
    p = blended(x_ref, fine_ref, exact_mm(across, lon_ref[...]))
    for tall in range(16):
        for wide in range(8):
            out_ref[2 * tall + wide // 4, 8 * (wide % 4) : 8 * (wide % 4) + 8, :] = p[
                8 * tall : 8 * tall + 8, 128 * wide : 128 * wide + 128
            ]


def last_partial_kernel(x_ref, fine_ref, smoothed_ref, out_ref):
    halves = [smoothed_ref[:, 8 * k : 8 * k + 8, :].reshape(64, 128) for k in range(2)]
    p = blended(x_ref, fine_ref, jnp.concatenate(halves, axis=1))
    turned = p.T
    sums = jnp.sum(smoothed_ref[:, 16:24, :], axis=0)
    for group in range(GROUPS):
        out_ref[group, :32, :] = turned[32 * group : 32 * group + 32]
        out_ref[group, 32:40, :] = sums


def share_kernel(scale, place_ref, arrived_ref, r_ref, out_ref):
    group = place_ref[1]
    share = r_ref[
        pl.ds(pl.multiple_of(8 * (group >> 1), 8), 8),
        pl.ds(pl.multiple_of(512 * (group & 1), 512), 512),
    ]
    share = jnp.concatenate([share[:, 128 * k : 128 * k + 128] for k in range(4)], axis=0)
    share = share + jnp.sum(arrived_ref[...], axis=0) * scale
    for other in range(GROUPS):
        out_ref[other] = share


def final_kernel(scale, place_ref, arrived_ref, r_ref, a_ref, x_out, res_out, r_turned, a_turned):
    group = place_ref[1]
    wide = group >> 2
    lanes = pl.ds(pl.multiple_of(128 * wide, 128), 128)
    r_turned[...] = r_ref[:, lanes].T
    rows = [
        a_ref[2 * tall + (wide >> 2), pl.ds(pl.multiple_of(8 * (wide & 3), 8), 8), :]
        for tall in range(16)
    ]
    a_turned[...] = jnp.concatenate(rows, axis=0).T
    mine = pl.ds(pl.multiple_of(32 * (group & 3), 32), 32)
    r, a = r_turned[mine, :], a_turned[mine, :]
    arrived = jnp.sum(arrived_ref[...], axis=0)
    b = a + arrived[:32] * scale
    i, j = iotas(8, 128)
    rr, ra, aa, rf, af, rc, ac = (
        total(jnp.where((i == 0) & (j == k), arrived[32:40], 0.0)) for k in range(7)
    )
    rr, ra, aa = rr / GROUPS, ra / GROUPS, aa / GROUPS
    step = rr / ra
    rb = ra + (rf + rc) * scale
    ab = aa + (af + ac) * scale
    squares = step * step * aa - rr
    next_step = squares / ((ra - step * aa) - step * (rb - step * ab))
    r_next = r - step * a
    x_out[...] = (step * r + next_step * r_next).T.reshape(4, ROWS, 32)
    res_out[...] = (r_next - next_step * (a - step * b)).T.reshape(4, ROWS, 32)


VMEM = pl.BlockSpec(memory_space=pltpu.VMEM)
SMEM = pl.BlockSpec(memory_space=pltpu.SMEM)
HBM = pl.BlockSpec(memory_space=pltpu.HBM)


def call(kernel, outs, specs, args, flops, limit, scratch=(), out_specs=None):
    out_specs = out_specs or [VMEM] * len(outs)
    shapes = [
        pltpu.HBM(*out) if spec is HBM else jax.ShapeDtypeStruct(*out)
        for out, spec in zip(outs, out_specs)
    ]
    size = sum(a.size * a.dtype.itemsize for a in args)
    args = [
        pltpu.with_memory_space_constraint(arg, pltpu.HBM) if spec is HBM else arg
        for arg, spec in zip(args, specs)
    ]
    return pl.pallas_call(
        kernel,
        out_shape=shapes if len(shapes) > 1 else shapes[0],
        in_specs=specs,
        out_specs=out_specs if len(shapes) > 1 else out_specs[0],
        scratch_shapes=list(scratch),
        compiler_params=pltpu.CompilerParams(vmem_limit_bytes=limit << 20),
        cost_estimate=pl.CostEstimate(flops=flops, bytes_accessed=size, transcendentals=0),
    )(*args)


def exchange(blocks, axis):
    return lax.all_to_all(blocks, axis, 0, 0, tiled=True)


def local(perturbations, right_side, fine_taps, coarse_lat, coarse_lon):
    count, levels, height, extent = perturbations.shape
    members = count * lax.axis_size(MEM)
    scale = 1.0 / (members - 1)
    place = jnp.stack([lax.axis_index("tile"), lax.axis_index(MEM)]).astype(jnp.int32)
    x = perturbations.reshape(count * levels * height, extent)
    r = right_side.reshape(levels * height, extent)
    half = ((128, LON), F32)
    edge = ((PAIRS, 8, LON), F32)
    shared = ((GROUPS, 32, 128), F32)
    up = [(i, (i + 1) % TILES) for i in range(TILES)]
    down = [(j, i) for i, j in up]

    def edges(top, bottom):
        return lax.ppermute(bottom, "tile", up), lax.ppermute(top, "tile", down)

    own = ((64, 256), F32)
    c, c_own, top, bottom = call(
        first_detail_kernel,
        [((TILES, 64, 256), F32), own, edge, edge],
        [HBM] * 2,
        (x, r),
        10**9,
        12,
        scratch=(
            pltpu.VMEM((256, LON), BF16),
            pltpu.VMEM((128, LON), F32),
            pltpu.SemaphoreType.DMA((4,)),
            pltpu.SemaphoreType.DMA((4,)),
        ),
    )
    c_first = exchange(c, "tile")
    table_shapes = [((256, 192), BF16), ((256, 192), BF16), ((4, 4, 384, 128), BF16)]
    table_scratch = [pltpu.VMEM(*shape) for shape in table_shapes]
    table_scratch.append(pltpu.SemaphoreType.DMA((3,)))
    *tables, mix = call(
        table_kernel,
        table_shapes + [((64, 512), F32)],
        [SMEM, VMEM, VMEM],
        (place, fine_taps.reshape(2 * levels, 5), coarse_lat),
        10**9,
        8,
        scratch=table_scratch,
        out_specs=[HBM] * 3 + [VMEM],
    )
    fine = call(
        functools.partial(fine_kernel, False),
        [half],
        [VMEM] * 5 + [HBM] * 3,
        (r, x, c_own, *edges(top, bottom), *tables),
        5 * 10**9,
        16,
        scratch=table_scratch,
    )
    shares, c_first = call(
        partial_kernel,
        [shared, own],
        [SMEM] + [VMEM] * 5,
        (place, x, fine, c_first, mix, coarse_lon),
        10**9,
        12,
    )
    arrived = exchange(shares, MEM)
    share = call(
        functools.partial(share_kernel, scale),
        [shared],
        [SMEM, VMEM, VMEM],
        (place, arrived, r),
        10**6,
        6,
    )
    a = exchange(share, MEM)

    c, c_own, top, bottom = call(
        detail_kernel,
        [((PAIRS, 8, 256), F32), own, edge, edge],
        [VMEM] * 2,
        (x, a),
        10**9,
        12,
    )
    beside = edges(top, bottom)
    c = exchange(c, "tile")
    fine, sums = call(
        functools.partial(fine_kernel, True),
        [half, ((8, 128), F32)],
        [VMEM] * 6 + [HBM] * 3,
        (r, a, x, c_own, *beside, *tables),
        5 * 10**9,
        16,
        scratch=table_scratch,
    )
    smoothed = call(
        smooth_dots_kernel,
        [((TILES, 24, 128), F32)],
        [VMEM] * 5,
        (c, c_first, coarse_lat, coarse_lon, sums),
        10**8,
        6,
    )
    smoothed = exchange(smoothed, "tile")
    shares = call(
        last_partial_kernel, [((GROUPS, 40, 128), F32)], [VMEM] * 3, (x, fine, smoothed), 10**9, 12
    )
    arrived = exchange(shares, MEM)
    out = ((levels, height, extent // GROUPS), F32)
    return tuple(
        call(
            functools.partial(final_kernel, scale),
            [out, out],
            [SMEM, VMEM, VMEM, VMEM],
            (place, arrived, r, a),
            10**6,
            6,
            scratch=(pltpu.VMEM((128, 128), F32), pltpu.VMEM((128, 128), F32)),
        )
    )


def solution(mesh):
    torus = Mesh(
        mesh.devices.reshape(4, 4, 2, mesh.shape["tile"]), ("mem_0", "mem_1", "mem_2", "tile")
    )
    placed = (P(MEM, None, "tile", None), P(None, "tile", None), P(), P(), P())
    return jax.shard_map(
        local,
        mesh=torus,
        in_specs=placed,
        out_specs=(P(None, "tile", MEM), P(None, "tile", MEM)),
        check_vma=False,
    )
```

time: 134 us -> 123 us (0.918)
  starting transfers between devices: 42.5 us -> 18.7 us
  blocking collectives: 47.1 us -> 65.3 us
  local copies, waits for them, and re-layouts: 11.3 us -> 0.02 us
  Pallas kernels: 15.4 us -> 21.1 us
  waiting for transfers between devices: 15.5 us -> 17 us
    all_to_all x4 -> x2, starting transfers between devices: 34.4 us -> 13.3 us  [exchange(): return lax.all_to_all(blocks, axis, 0, 0, tiled=True)]
    all_to_all x3 -> x4, blocking collectives: 47.1 us -> 65.3 us  [exchange(): return lax.all_to_all(blocks, axis, 0, 0, tiled=True)]
    ppermute x4, waiting for transfers between devices: 1.13 us -> 15.7 us  [edges(): return (lax.ppermute(bottom, 'tile', up), lax.ppermute(top, 'tile', down))]
    all_to_all x4 -> x2, waiting for transfers between devices: 14.3 us -> 1.3 us  [exchange(): return lax.all_to_all(blocks, axis, 0, 0, tiled=True)]
    unnamed x29 -> x10, local copies, waits for them, and re-layouts: 10.2 us -> 0.02 us
    pallas_call x11 -> x10, Pallas kernels: 15.4 us -> 21.1 us  [call(): pl.pallas_call(kernel, out_shape=shapes if len(shapes) > 1 else shapes[0]...]
    ppermute x4, starting transfers between devices: 8.14 us -> 5.37 us  [edges(): return (lax.ppermute(bottom, 'tile', up), lax.ppermute(top, 'tile', down))]
  transfers between devices with their start and end apart: 8 -> 6, of which waited for: 4 -> 3; matrix products, arithmetic and copies ran while one was open for 1% -> 0% of each run, Pallas kernels for 7% -> 9%
where the time goes in v1:
time: 123 us
  blocking collectives  65.3 us (53%)
  Pallas kernels  21.1 us (17%)
  starting transfers between devices  18.7 us (15%)
  waiting for transfers between devices  17 us (14%)
    all_to_all x4, blocking collectives, exchange(): return lax.all_to_all(blocks, axis, 0, 0, tiled=True)  65.3 us
    pallas_call x10, Pallas kernels, call(): pl.pallas_call(kernel, out_shape=shapes if len(shapes) > 1 else shapes[0]...  21.1 us
    ppermute x4, waiting for transfers between devices, edges(): return (lax.ppermute(bottom, 'tile', up), lax.ppermute(top, 'tile', down))  15.7 us
    all_to_all x2, starting transfers between devices, exchange(): return lax.all_to_all(blocks, axis, 0, 0, tiled=True)  13.3 us
    ppermute x4, starting transfers between devices, edges(): return (lax.ppermute(bottom, 'tile', up), lax.ppermute(top, 'tile', down))  5.37 us
  transfers between devices with their start and end apart: 6, of which 3 were waited for; matrix products, arithmetic and copies ran while one was open for 0% of the time, Pallas kernels for 9%

profile of v1, /device:TPU:1, one launch (start us, length us, event | category | flops | bytes accessed | tf_op | source)
XLA Modules:
  0.0 122.9 jit_solution(9103358813681041596)
XLA Ops:
  0.6 0.0 copy-start.2
  0.6 0.0 copy-start.4
  0.6 2.9 %shard_map.68 = (f32[8,64,256]{2,1,0:T(8,128)}, f32[64,256]{1,0:T(8,128)S(1)}, f32[8,8,1024]{2,1,0:T(8,128)S(1)}, f32[8,8,1024]{2,1,0:T(8,128)S(1)}) custom-call(bf16[256,1024]{1,0:T(8,128)(2,1)} %bitcast.10, f32[128,1024]{1,0:T(8,128)} %bitcast.5), custom_call_target="tpu_custom_call" | custom-call | flops 1000000000 | bytes 1048576 | tf_op jit(solution)/shard_map/pallas_call | solution.py:383
  3.6 9.0 %all-to-all-start = ((f32[8,64,256]{2,1,0:T(8,128)}), f32[8,64,256]{2,1,0:T(8,128)S(1)}, u32[]{:S(2)}, u32[]{:S(2)}) async-start(f32[8,64,256]{2,1,0:T(8,128)} %get-tuple-element.24), calls=%async_computation | async-start | bytes 1048576 | tf_op jit(solution)/shard_map/all_to_all | solution.py:395
  12.6 1.5 %collective-permute-start = (f32[8,8,1024]{2,1,0:T(8,128)S(1)}, f32[8,8,1024]{2,1,0:T(8,128)S(1)}, u32[]{:S(2)}, u32[]{:S(2)}) collective-permute-start(f32[8,8,1024]{2,1,0:T(8,128)S(1)} %get-tuple-element.19), channel_id=1, source_target_pairs={{0,1},{1,2},{2,3},{3,4},{4,5},{5,6},{6,7},{7,0},{8,9},{9,10},{10,1... | collective-permute-start | bytes 786440 | tf_op jit(solution)/shard_map/ppermute | solution.py:412
  14.1 1.2 %collective-permute-start.1 = (f32[8,8,1024]{2,1,0:T(8,128)S(1)}, f32[8,8,1024]{2,1,0:T(8,128)S(1)}, u32[]{:S(2)}, u32[]{:S(2)}) collective-permute-start(f32[8,8,1024]{2,1,0:T(8,128)S(1)} %get-tuple-element.20), channel_id=1, source_target_pairs={{1,0},{2,1},{3,2},{4,3},{5,4},{6,5},{7,6},{0,7},{9,8},{10,9},{11,1... | collective-permute-start | bytes 786440 | tf_op jit(solution)/shard_map/ppermute | solution.py:412
  15.3 0.1 pad_add_fusion.place_ref
  15.4 0.0 copy-done.2
  15.4 0.0 copy-done.4
  15.4 0.0 copy-start
  15.4 0.0 copy-start.3
  15.4 3.1 %shard_map.69 = (bf16[256,192]{1,0:T(8,128)(2,1)}, bf16[256,192]{1,0:T(8,128)(2,1)}, bf16[4,4,384,128]{3,2,1,0:T(8,128)(2,1)}, f32[64,512]{1,0:T(8,128)S(1)}) custom-call(s32[2]{0:T(128)S(1)} %pad_add_fusion.place_ref, f32[8,5]{1,0:T(8,128)S(1)} %bitcast.16, f32[64,64]{1,0:T(8,128)S(1)} %copy-done.2), custom_call_target="tpu_custom_call" | custom-call | flops 1000000000 | bytes 16552 | tf_op jit(solution)/shard_map/pallas_call | solution.py:383
  18.5 14.0 %collective-permute-done.refs_3_ = f32[8,8,1024]{2,1,0:T(8,128)S(1)} collective-permute-done((f32[8,8,1024]{2,1,0:T(8,128)S(1)}, f32[8,8,1024]{2,1,0:T(8,128)S(1)}, u32[]{:S(2)}, u32[]{:S(2)}) %collective-permute-start) | collective-permute-done | bytes 262176 | tf_op jit(solution)/shard_map/ppermute | solution.py:412
  32.5 0.0 collective-permute-done.1.refs_4_
  32.5 0.0 copy-done
  32.5 0.0 copy-done.3
  32.5 0.0 copy-start.1
  32.6 4.0 %shard_map.70.fine_ref = f32[128,1024]{1,0:T(8,128)S(1)} custom-call(f32[128,1024]{1,0:T(8,128)S(1)} %bitcast.6, bf16[256,1024]{1,0:T(8,128)(2,1)S(1)} %bitcast.11, f32[64,256]{1,0:T(8,128)S(1)} %get-tuple-element.18.refs_2_, f32[8,8,1024]{2,1,0:T(8,128)S(1)} %collective-permute-done.refs_3_, f32[8,8,1024]{2,1,0:T(8,128)S(1)} %collective-permute-done.1.refs_4_, ...), custom_call_target="tpu_custom_call" | custom-call | flops 5000000000 | bytes 3407872 | tf_op jit(solution)/shard_map/pallas_call | solution.py:383
  36.6 0.0 all-to-all-done.c_ref
  36.6 0.0 copy-done.1
  36.6 2.0 %shard_map.71 = (f32[32,32,128]{2,1,0:T(8,128)S(1)}, f32[64,256]{1,0:T(8,128)S(1)}) custom-call(s32[2]{0:T(128)S(1)} %pad_add_fusion.place_ref, bf16[256,1024]{1,0:T(8,128)(2,1)S(1)} %bitcast.12, f32[128,1024]{1,0:T(8,128)S(1)} %shard_map.70.fine_ref, f32[8,64,256]{2,1,0:T(8,128)S(1)} %all-to-all-done.c_ref, f32[64,512]{1,0:T(8,128)S(1)} %get-tuple-element.25.mix_ref, ...), custom_call_target="tpu_custom_call" | custom-call | flops 1000000000 | bytes 1966088 | tf_op jit(solution)/shard_map/pallas_call | solution.py:383
  38.7 19.9 %all_to_all.30.arrived_ref = f32[32,32,128]{2,1,0:T(8,128)S(1)} all-to-all(f32[32,32,128]{2,1,0:T(8,128)S(1)} %get-tuple-element.26), channel_id=1, replica_groups=mesh['mem_0'=4,'mem_1'=4,'mem_2'=2,'tile'=8] {'mem_0','mem_1','mem_2'}, dimensions={0} | all-to-all | bytes 1048576 | tf_op jit(solution)/shard_map/all_to_all | solution.py:395
  58.5 0.6 shard_map.72
  59.2 15.2 %all_to_all.31.v_ref.refs_1_.a_ref = f32[32,32,128]{2,1,0:T(8,128)S(1)} all-to-all(f32[32,32,128]{2,1,0:T(8,128)S(1)} %shard_map.72), channel_id=1, replica_groups=mesh['mem_0'=4,'mem_1'=4,'mem_2'=2,'tile'=8] {'mem_0','mem_1','mem_2'}, dimensions={0} | all-to-all | bytes 1048576 | tf_op jit(solution)/shard_map/all_to_all | solution.py:395
  74.4 1.4 %shard_map.73 = (f32[8,8,256]{2,1,0:T(8,128)}, f32[64,256]{1,0:T(8,128)S(1)}, f32[8,8,1024]{2,1,0:T(8,128)S(1)}, f32[8,8,1024]{2,1,0:T(8,128)S(1)}) custom-call(bf16[256,1024]{1,0:T(8,128)(2,1)S(1)} %bitcast.13, f32[32,32,128]{2,1,0:T(8,128)S(1)} %all_to_all.31.v_ref.refs_1_.a_ref), custom_call_target="tpu_custom_call" | custom-call | flops 1000000000 | bytes 1048576 | tf_op jit(solution)/shard_map/pallas_call | solution.py:383
  75.8 0.0 collective-permute-start.2
  75.8 2.7 %collective-permute-start.3 = (f32[8,8,1024]{2,1,0:T(8,128)S(1)}, f32[8,8,1024]{2,1,0:T(8,128)S(1)}, u32[]{:S(2)}, u32[]{:S(2)}) collective-permute-start(f32[8,8,1024]{2,1,0:T(8,128)S(1)} %get-tuple-element.29), channel_id=1, source_target_pairs={{1,0},{2,1},{3,2},{4,3},{5,4},{6,5},{7,6},{0,7},{9,8},{10,9},{11,1... | collective-permute-start | bytes 786440 | tf_op jit(solution)/shard_map/ppermute | solution.py:412
  78.4 4.3 %all-to-all-start.3 = ((f32[8,8,256]{2,1,0:T(8,128)}), f32[8,8,256]{2,1,0:T(8,128)S(1)}, u32[]{:S(2)}, u32[]{:S(2)}) async-start(f32[8,8,256]{2,1,0:T(8,128)} %get-tuple-element.31), calls=%async_computation.3 | async-start | bytes 131072 | tf_op jit(solution)/shard_map/all_to_all | solution.py:395
  82.7 1.7 %collective-permute-done.2.refs_4_ = f32[8,8,1024]{2,1,0:T(8,128)S(1)} collective-permute-done((f32[8,8,1024]{2,1,0:T(8,128)S(1)}, f32[8,8,1024]{2,1,0:T(8,128)S(1)}, u32[]{:S(2)}, u32[]{:S(2)}) %collective-permute-start.2) | collective-permute-done | bytes 262176 | tf_op jit(solution)/shard_map/ppermute | solution.py:412
  84.4 0.0 collective-permute-done.3.refs_5_
  84.4 4.2 %shard_map.74 = (f32[128,1024]{1,0:T(8,128)S(1)}, f32[8,128]{1,0:T(8,128)S(1)}) custom-call(f32[128,1024]{1,0:T(8,128)S(1)} %bitcast.8, f32[32,32,128]{2,1,0:T(8,128)S(1)} %all_to_all.31.v_ref.refs_1_.a_ref, bf16[256,1024]{1,0:T(8,128)(2,1)S(1)} %bitcast.14, f32[64,256]{1,0:T(8,128)S(1)} %get-tuple-element.27.refs_3_, ...), custom_call_target="tpu_custom_call" | custom-call | flops 5000000000 | bytes 3932160 | tf_op jit(solution)/shard_map/pallas_call | solution.py:383
  88.6 1.3 %all-to-all-done.3.c_ref = f32[8,8,256]{2,1,0:T(8,128)S(1)} async-done(((f32[8,8,256]{2,1,0:T(8,128)}), f32[8,8,256]{2,1,0:T(8,128)S(1)}, u32[]{:S(2)}, u32[]{:S(2)}) %all-to-all-start.3) | async-done | bytes 65568 | tf_op jit(solution)/shard_map/all_to_all | solution.py:395
  89.9 0.6 shard_map.75
  90.6 11.1 %all_to_all.32.smoothed_ref = f32[8,24,128]{2,1,0:T(8,128)S(1)} all-to-all(f32[8,24,128]{2,1,0:T(8,128)S(1)} %shard_map.75), channel_id=1, replica_groups=mesh['mem_0'=4,'mem_1'=4,'mem_2'=2,'tile'=8] {'tile'}, dimensions={0} | all-to-all | bytes 196608 | tf_op jit(solution)/shard_map/all_to_all | solution.py:395
  101.7 0.7 shard_map.76
  102.4 19.0 %all_to_all.33.arrived_ref = f32[32,40,128]{2,1,0:T(8,128)S(1)} all-to-all(f32[32,40,128]{2,1,0:T(8,128)S(1)} %shard_map.76), channel_id=1, replica_groups=mesh['mem_0'=4,'mem_1'=4,'mem_2'=2,'tile'=8] {'mem_0','mem_1','mem_2'}, dimensions={0} | all-to-all | bytes 1310720 | tf_op jit(solution)/shard_map/all_to_all | solution.py:395
  121.4 1.5 %shard_map.77 = (f32[4,32,32]{2,1,0:T(8,128)}, f32[4,32,32]{2,1,0:T(8,128)}) custom-call(s32[2]{0:T(128)S(1)} %pad_add_fusion.place_ref, f32[32,40,128]{2,1,0:T(8,128)S(1)} %all_to_all.33.arrived_ref, f32[128,1024]{1,0:T(8,128)S(1)} %bitcast.9, f32[32,32,128]{2,1,0:T(8,128)S(1)} %all_to_all.31.v_ref.refs_1_.a_ref), custom_call_target="tpu_custom_call" | custom-call | flops 1000000 | bytes 1703944 | tf_op jit(solution)/shard_map/pallas_call | solution.py:383
Async XLA Ops:
  0.6 14.8 %copy-start.2 = (f32[64,64]{1,0:T(8,128)S(1)}, f32[64,64]{1,0:T(8,128)}, u32[]{:S(2)}) copy-start(f32[64,64]{1,0:T(8,128)} %lat_ref.3) | copy-start | bytes 49156
  0.6 14.8 %copy-start.4 = (f32[2,4,5]{2,1,0:T(4,128)S(1)}, f32[2,4,5]{2,1,0:T(4,128)}, u32[]{:S(2)}) copy-start(f32[2,4,5]{2,1,0:T(4,128)} %param.7) | copy-start | bytes 484
  3.6 33.0 %all-to-all-start = ((f32[8,64,256]{2,1,0:T(8,128)}), f32[8,64,256]{2,1,0:T(8,128)S(1)}, u32[]{:S(2)}, u32[]{:S(2)}) async-start(f32[8,64,256]{2,1,0:T(8,128)} %get-tuple-element.24), calls=%async_computation | async-start | bytes 1048576 | tf_op jit(solution)/shard_map/all_to_all | solution.py:395
  12.6 19.9 %collective-permute-start = (f32[8,8,1024]{2,1,0:T(8,128)S(1)}, f32[8,8,1024]{2,1,0:T(8,128)S(1)}, u32[]{:S(2)}, u32[]{:S(2)}) collective-permute-start(f32[8,8,1024]{2,1,0:T(8,128)S(1)} %get-tuple-element.19), channel_id=1, source_target_pairs={{0,1},{1,2},{2,3},{3,4},{4,5},{5,6},{6,7},{7,0},{8,9},{9,10},{10,1... | collective-permute-start | bytes 786440 | tf_op jit(solution)/shard_map/ppermute | solution.py:412
  14.1 18.5 %collective-permute-start.1 = (f32[8,8,1024]{2,1,0:T(8,128)S(1)}, f32[8,8,1024]{2,1,0:T(8,128)S(1)}, u32[]{:S(2)}, u32[]{:S(2)}) collective-permute-start(f32[8,8,1024]{2,1,0:T(8,128)S(1)} %get-tuple-element.20), channel_id=1, source_target_pairs={{1,0},{2,1},{3,2},{4,3},{5,4},{6,5},{7,6},{0,7},{9,8},{10,9},{11,1... | collective-permute-start | bytes 786440 | tf_op jit(solution)/shard_map/ppermute | solution.py:412
  15.4 17.1 %copy-start = (f32[4,32,1024]{2,1,0:T(8,128)S(1)}, f32[4,32,1024]{2,1,0:T(8,128)}, u32[]{:S(2)}) copy-start(f32[4,32,1024]{2,1,0:T(8,128)} %param.6) | copy-start | bytes 1572868
  15.4 17.1 %copy-start.3 = (bf16[2,4,32,1024]{3,2,1,0:T(8,128)(2,1)S(1)}, bf16[2,4,32,1024]{3,2,1,0:T(8,128)(2,1)}, u32[]{:S(2)}) copy-start(bf16[2,4,32,1024]{3,2,1,0:T(8,128)(2,1)} %param.5) | copy-start | bytes 1572868
  32.5 4.1 %copy-start.1 = (f32[256,256]{1,0:T(8,128)S(1)}, f32[256,256]{1,0:T(8,128)}, u32[]{:S(2)}) copy-start(f32[256,256]{1,0:T(8,128)} %lon_ref.3) | copy-start | bytes 786436
  75.8 8.6 %collective-permute-start.2 = (f32[8,8,1024]{2,1,0:T(8,128)S(1)}, f32[8,8,1024]{2,1,0:T(8,128)S(1)}, u32[]{:S(2)}, u32[]{:S(2)}) collective-permute-start(f32[8,8,1024]{2,1,0:T(8,128)S(1)} %get-tuple-element.28), channel_id=1, source_target_pairs={{0,1},{1,2},{2,3},{3,4},{4,5},{5,6},{6,7},{7,0},{8,9},{9,10},{10,1... | collective-permute-start | bytes 786440 | tf_op jit(solution)/shard_map/ppermute | solution.py:412
  75.8 8.6 %collective-permute-start.3 = (f32[8,8,1024]{2,1,0:T(8,128)S(1)}, f32[8,8,1024]{2,1,0:T(8,128)S(1)}, u32[]{:S(2)}, u32[]{:S(2)}) collective-permute-start(f32[8,8,1024]{2,1,0:T(8,128)S(1)} %get-tuple-element.29), channel_id=1, source_target_pairs={{1,0},{2,1},{3,2},{4,3},{5,4},{6,5},{7,6},{0,7},{9,8},{10,9},{11,1... | collective-permute-start | bytes 786440 | tf_op jit(solution)/shard_map/ppermute | solution.py:412
  78.4 11.5 %all-to-all-start.3 = ((f32[8,8,256]{2,1,0:T(8,128)}), f32[8,8,256]{2,1,0:T(8,128)S(1)}, u32[]{:S(2)}, u32[]{:S(2)}) async-start(f32[8,8,256]{2,1,0:T(8,128)} %get-tuple-element.31), calls=%async_computation.3 | async-start | bytes 131072 | tf_op jit(solution)/shard_map/all_to_all | solution.py:395

commit v2 on v1

--- a/solution.py
+++ b/solution.py
@@ -55,22 +55,28 @@
     return jnp.where(hit, 1.0, 0.0).astype(BF16)
 
 
-def block_mean(w):
+def block_mean(w, split):
     table = shrink_table(64, 256, False)
-    part = sum(mm(table, piece) for piece in split3(w))
+    part = sum(mm(table, piece) for piece in split(w))
     stacked = jnp.concatenate([part[:, :512], part[:, 512:]], axis=0)
     table = shrink_table(512, 128, True)
-    small = sum(mm(piece, table) for piece in split3(stacked))
+    small = sum(mm(piece, table) for piece in split(stacked))
     return jnp.concatenate([small[:64], small[64:]], axis=1)
 
 
-def prolong(c):
-    table = expand_table(256, 64, True)
+def prolong(c, edges=False):
+    if edges:
+        i, j = iotas(128, 64)
+        spot = 8 * (i >> 4) + ((i & 15) >> 2) + 4 * ((i & 15) >> 3)
+        table = jnp.where(spot == j, 1.0, 0.0).astype(BF16)
+    else:
+        table = expand_table(256, 64, True)
+    rows = table.shape[0]
     tall = sum(mm(table, piece) for piece in split2(c))
     stacked = jnp.concatenate([tall[:, :128], tall[:, 128:]], axis=0)
     table = expand_table(128, 512, False)
     wide = sum(mm(piece, table) for piece in split2(stacked))
-    return jnp.concatenate([wide[:256], wide[256:]], axis=1)
+    return jnp.concatenate([wide[:rows], wide[rows:]], axis=1)
 
 
 def natural(blocks):
@@ -91,10 +97,10 @@
 def first_detail_kernel(x_hbm, v_hbm, *refs):
     *out_refs, x_ref, v_ref, x_sems, v_sems = refs
     copies = []
-    for k in range(4):
+    for k in range(8):
+        rows = pl.ds(16 * k, 16)
+        copies.append(pltpu.make_async_copy(v_hbm.at[rows], v_ref.at[rows], v_sems.at[k]))
         rows = pl.ds(32 * k, 32)
-        copies.append(pltpu.make_async_copy(v_hbm.at[rows], v_ref.at[rows], v_sems.at[k]))
-        rows = pl.ds(64 * k, 64)
         copies.append(pltpu.make_async_copy(x_hbm.at[rows], x_ref.at[rows], x_sems.at[k]))
     for copy in copies:
         copy.start()
@@ -105,21 +111,22 @@
 
 def detail(x, v, c_ref, own_ref, top_ref, bottom_ref):
     w = x.astype(F32) * jnp.concatenate([v, v], axis=0)
-    c = block_mean(w)
+    c = block_mean(w, split3)
     if c_ref.shape == (TILES, 64, 256):
         for tile in range(TILES):
             c_ref[tile] = c
     else:
         c_ref[...] = c.reshape(PAIRS, 8, 256)
     own_ref[...] = c
-    d = w - prolong(c)
+    spread = prolong(c, edges=True)
     for pair in range(PAIRS):
-        top_ref[pair] = d[ROWS * pair : ROWS * pair + 8]
-        bottom_ref[pair] = d[ROWS * pair + 24 : ROWS * pair + 32]
+        at = ROWS * pair
+        top_ref[pair] = w[at : at + 8] - spread[16 * pair : 16 * pair + 8]
+        bottom_ref[pair] = w[at + 24 : at + 32] - spread[16 * pair + 8 : 16 * pair + 16]
 
 
 def table_kernel(place_ref, taps_ref, lat_ref, *refs):
-    *hbm_refs, mix_ref, high_ref, low_ref, band_ref, sems = refs
+    rows_ref, band_ref, mix_ref = refs
     tile = place_ref[0]
     taps = taps_ref[...]
     square = taps * taps
@@ -152,11 +159,8 @@
         for o in range(5):
             second = jnp.where(dist == o, single[o][level : level + 1], second)
     both = exact_mm(second, first)
-    i, j = iotas(128, 128)
-    mean = jnp.where((i >> 2) == (j >> 2), 0.25, 0.0)
-    high, low = split2(jnp.concatenate([both, exact_mm(mean, both)], axis=0))
-    high_ref[...] = high
-    low_ref[...] = low
+    for kind, piece in enumerate(split2(both)):
+        rows_ref[kind] = piece
     i, j = iotas(8, 128)
     before = jnp.abs(i - 8 - j)
     after = jnp.abs(i + 128 - j)
@@ -171,12 +175,9 @@
                 jnp.where(dist == o, tap, c) for dist, c in zip((before, after), corner)
             )
             middle = jnp.where(inner == o, tap, middle)
-        rest = jnp.zeros((120, 128), F32)
-        bands = jnp.concatenate([rest, corner[0], middle, corner[1], rest], axis=0)
-        parts = jnp.concatenate([corner[0], middle, corner[1]], axis=0)
-        meant = -exact_mm(parts, mean)
-        meant = jnp.concatenate([rest, meant, rest], axis=0)
-        for kind, piece in enumerate((*split2(bands), *split2(meant))):
+        rest = jnp.zeros((8, 128), F32)
+        band = jnp.concatenate([rest, corner[0], middle, corner[1], rest], axis=0)
+        for kind, piece in enumerate(split2(band)):
             band_ref[level, kind] = piece
     i, j = iotas(64, 512)
     repeat = jnp.where((i >> 3) == (j >> 6), jnp.where((i & 7) == (j & 7), 1.0, 0.0), 0.0)
@@ -184,21 +185,13 @@
     wide = exact_mm(mine, repeat)
     mix = jnp.concatenate([wide] * PAIRS, axis=0)
     mix_ref[...] = jnp.where((i >> 3) == ((j >> 3) & 7), mix, 0.0)
-    copies = [
-        pltpu.make_async_copy(source, target, sems.at[k])
-        for k, (source, target) in enumerate(zip((high_ref, low_ref, band_ref), hbm_refs))
-    ]
-    for copy in copies:
-        copy.start()
-    for copy in copies:
-        copy.wait()
 
 
 def banded(band_ref, level, kind):
     band = band_ref[level, kind]
-    zero = jnp.zeros((128, 128), BF16)
-    left = jnp.concatenate([band, zero], axis=0)
-    right = jnp.concatenate([zero, band], axis=0)
+    edge, half = jnp.zeros((112, 128), BF16), jnp.zeros((128, 128), BF16)
+    left = jnp.concatenate([edge, band, edge, half], axis=0)
+    right = jnp.concatenate([half, edge, band, edge], axis=0)
     return jnp.concatenate([left, right], axis=1)
 
 
@@ -229,20 +222,11 @@
 def fine_kernel(last, *refs):
     if last:
         r_ref, *refs = refs
-    v_ref, x_ref, c_ref, before_ref, after_ref, *refs = refs
-    *refs, high_ref, low_ref, band_ref, sems = refs
-    copies = [
-        pltpu.make_async_copy(source, target, sems.at[k])
-        for k, (source, target) in enumerate(zip(refs[:3], (high_ref, low_ref, band_ref)))
-    ]
-    for copy in copies:
-        copy.start()
-    outs = refs[3:]
-    fine_ref = outs[0]
+    v_ref, x_ref, c_ref, before_ref, after_ref, rows_ref, band_ref, *refs = refs
+    fine_ref, mean_ref, *refs = refs
+    f_ref = refs[-1]
     v = natural(v_ref) if last else v_ref[...]
     d = x_ref[...].astype(F32) * jnp.concatenate([v, v], axis=0) - prolong(c_ref[...])
-    copies[0].wait()
-    copies[1].wait()
     highs, lows = [], []
     for member in range(2):
         rows = []
@@ -250,41 +234,40 @@
             pair = 4 * member + level
             rows += [before_ref[pair], d[ROWS * pair : ROWS * pair + ROWS], after_ref[pair]]
         high, low = split2(jnp.concatenate(rows, axis=0))
-        passed = mm(high_ref[...], high) + mm(high_ref[...], low) + mm(low_ref[...], high)
+        passed = mm(rows_ref[0], high) + mm(rows_ref[0], low) + mm(rows_ref[1], high)
         high, low = split2(passed)
         highs.append(high)
         lows.append(low)
-    copies[2].wait()
     for level in range(4):
-        result = None
-        for kind in range(2):
-            high = windows(highs, 128 * kind + ROWS * level)
-            low = windows(lows, 128 * kind + ROWS * level)
-            table_high = banded(band_ref, level, 2 * kind)
-            table_low = banded(band_ref, level, 2 * kind + 1)
-            term = mm(high, table_high) + mm(low, table_high) + mm(high, table_low)
-            result = term if result is None else result + term
+        high = windows(highs, ROWS * level)
+        low = windows(lows, ROWS * level)
+        table_high, table_low = banded(band_ref, level, 0), banded(band_ref, level, 1)
+        result = mm(high, table_high) + mm(low, table_high) + mm(high, table_low)
         for block in range(4):
+            lanes = slice(256 * block, 256 * block + 256)
             summed = None
             for member in range(2):
                 row = ROWS * (4 * member + level)
-                x = x_ref[row : row + ROWS, 256 * block : 256 * block + 256].astype(F32)
                 at = 64 * block + ROWS * member
-                term = x * result[at : at + ROWS]
+                f = result[at : at + ROWS]
+                f_ref[row : row + ROWS, lanes] = f
+                term = x_ref[row : row + ROWS, lanes].astype(F32) * f
                 summed = term if summed is None else summed + term
-            fine_ref[ROWS * level : ROWS * level + ROWS, 256 * block : 256 * block + 256] = summed
+            fine_ref[ROWS * level : ROWS * level + ROWS, lanes] = summed
+    means = block_mean(f_ref[...], split2)
+    mean_ref[...] = means
     if last:
-        r, fine = r_ref[...], fine_ref[...]
-        pairs = ((r, r), (r, v), (v, v), (r, fine), (v, fine))
-        outs[1][...] = lane_sums([(k, total(p * q)) for k, (p, q) in enumerate(pairs)])
-
-
-def smooth_dots_kernel(c_ref, first_ref, lat_ref, lon_ref, sums_ref, out_ref):
+        r = r_ref[...]
+        products = total(v * fine_ref[...]) - 16.0 * total(c_ref[...] * means)
+        refs[0][...] = lane_sums(
+            ((0, total(r * r)), (1, total(r * v)), (2, total(v * v)), (3, products))
+        )
+
+
+def smooth_kernel(c_ref, lat_ref, lon_ref, sums_ref, out_ref):
     c = c_ref[...].reshape(64, 256)
-    first = first_ref[...]
     smoothed = exact_mm(exact_mm(lat_ref[...], c), lon_ref[...])
-    dots = (total(first * smoothed), total(c * smoothed))
-    sums = sums_ref[...] + lane_sums([(5 + k, dot * 16.0) for k, dot in enumerate(dots)])
+    sums = sums_ref[...] + lane_sums([(4, 16.0 * total(c * smoothed))])
     for tile in range(TILES):
         out_ref[tile, 0:8, :] = smoothed[8 * tile : 8 * tile + 8, :128]
         out_ref[tile, 8:16, :] = smoothed[8 * tile : 8 * tile + 8, 128:]
@@ -300,12 +283,9 @@
     )
 
 
-def partial_kernel(place_ref, x_ref, fine_ref, c_ref, mix_ref, lon_ref, out_ref, mine_ref):
-    mine = pl.ds(pl.multiple_of(8 * place_ref[0], 8), 8)
-    for tile in range(TILES):
-        mine_ref[8 * tile : 8 * tile + 8, :] = c_ref[tile, mine, :]
+def partial_kernel(x_ref, fine_ref, mean_ref, c_ref, mix_ref, lon_ref, out_ref):
     across = exact_mm(mix_ref[...], c_ref[...].reshape(512, 256))
-    p = blended(x_ref, fine_ref, exact_mm(across, lon_ref[...]))
+    p = blended(x_ref, fine_ref, exact_mm(across, lon_ref[...]) - mean_ref[...])
     for tall in range(16):
         for wide in range(8):
             out_ref[2 * tall + wide // 4, 8 * (wide % 4) : 8 * (wide % 4) + 8, :] = p[
@@ -313,9 +293,9 @@
             ]
 
 
-def last_partial_kernel(x_ref, fine_ref, smoothed_ref, out_ref):
+def last_partial_kernel(x_ref, fine_ref, mean_ref, smoothed_ref, out_ref):
     halves = [smoothed_ref[:, 8 * k : 8 * k + 8, :].reshape(64, 128) for k in range(2)]
-    p = blended(x_ref, fine_ref, jnp.concatenate(halves, axis=1))
+    p = blended(x_ref, fine_ref, jnp.concatenate(halves, axis=1) - mean_ref[...])
     turned = p.T
     sums = jnp.sum(smoothed_ref[:, 16:24, :], axis=0)
     for group in range(GROUPS):
@@ -350,15 +330,14 @@
     arrived = jnp.sum(arrived_ref[...], axis=0)
     b = a + arrived[:32] * scale
     i, j = iotas(8, 128)
-    rr, ra, aa, rf, af, rc, ac = (
-        total(jnp.where((i == 0) & (j == k), arrived[32:40], 0.0)) for k in range(7)
+    rr, ra, aa, af, ac = (
+        total(jnp.where((i == 0) & (j == k), arrived[32:40], 0.0)) for k in range(5)
     )
     rr, ra, aa = rr / GROUPS, ra / GROUPS, aa / GROUPS
     step = rr / ra
-    rb = ra + (rf + rc) * scale
     ab = aa + (af + ac) * scale
     squares = step * step * aa - rr
-    next_step = squares / ((ra - step * aa) - step * (rb - step * ab))
+    next_step = squares / ((ra - step * aa) - step * (aa - step * ab))
     r_next = r - step * a
     x_out[...] = (step * r + next_step * r_next).T.reshape(4, ROWS, 32)
     res_out[...] = (r_next - next_step * (a - step * b)).T.reshape(4, ROWS, 32)
@@ -422,38 +401,38 @@
         scratch=(
             pltpu.VMEM((256, LON), BF16),
             pltpu.VMEM((128, LON), F32),
-            pltpu.SemaphoreType.DMA((4,)),
-            pltpu.SemaphoreType.DMA((4,)),
+            pltpu.SemaphoreType.DMA((8,)),
+            pltpu.SemaphoreType.DMA((8,)),
         ),
     )
     c_first = exchange(c, "tile")
-    table_shapes = [((256, 192), BF16), ((256, 192), BF16), ((4, 4, 384, 128), BF16)]
-    table_scratch = [pltpu.VMEM(*shape) for shape in table_shapes]
-    table_scratch.append(pltpu.SemaphoreType.DMA((3,)))
     *tables, mix = call(
         table_kernel,
-        table_shapes + [((64, 512), F32)],
+        [
+            ((2, 128, 192), BF16),
+            ((levels, 2, 160, 128), BF16),
+            ((64, 512), F32),
+        ],
         [SMEM, VMEM, VMEM],
         (place, fine_taps.reshape(2 * levels, 5), coarse_lat),
         10**9,
-        8,
-        scratch=table_scratch,
-        out_specs=[HBM] * 3 + [VMEM],
-    )
-    fine = call(
+        6,
+    )
+    fine_scratch = [pltpu.VMEM((256, LON), F32)]
+    fine, means = call(
         functools.partial(fine_kernel, False),
-        [half],
-        [VMEM] * 5 + [HBM] * 3,
+        [half, own],
+        [VMEM] * 7,
         (r, x, c_own, *edges(top, bottom), *tables),
-        5 * 10**9,
+        10**11,
         16,
-        scratch=table_scratch,
-    )
-    shares, c_first = call(
+        scratch=fine_scratch,
+    )
+    shares = call(
         partial_kernel,
-        [shared, own],
-        [SMEM] + [VMEM] * 5,
-        (place, x, fine, c_first, mix, coarse_lon),
+        [shared],
+        [VMEM] * 6,
+        (x, fine, means, c_first, mix, coarse_lon),
         10**9,
         12,
     )
@@ -478,26 +457,31 @@
     )
     beside = edges(top, bottom)
     c = exchange(c, "tile")
-    fine, sums = call(
+    fine, means, sums = call(
         functools.partial(fine_kernel, True),
-        [half, ((8, 128), F32)],
-        [VMEM] * 6 + [HBM] * 3,
+        [half, own, ((8, 128), F32)],
+        [VMEM] * 8,
         (r, a, x, c_own, *beside, *tables),
-        5 * 10**9,
+        10**11,
         16,
-        scratch=table_scratch,
+        scratch=fine_scratch,
     )
     smoothed = call(
-        smooth_dots_kernel,
+        smooth_kernel,
         [((TILES, 24, 128), F32)],
-        [VMEM] * 5,
-        (c, c_first, coarse_lat, coarse_lon, sums),
+        [VMEM] * 4,
+        (c, coarse_lat, coarse_lon, sums),
         10**8,
         6,
     )
     smoothed = exchange(smoothed, "tile")
     shares = call(
-        last_partial_kernel, [((GROUPS, 40, 128), F32)], [VMEM] * 3, (x, fine, smoothed), 10**9, 12
+        last_partial_kernel,
+        [((GROUPS, 40, 128), F32)],
+        [VMEM] * 4,
+        (x, fine, means, smoothed),
+        10**9,
+        12,
     )
     arrived = exchange(shares, MEM)
     out = ((levels, height, extent // GROUPS), F32)

time: 123 us -> 118 us (0.959)
  Pallas kernels: 21.1 us -> 16.2 us
  waiting for transfers between devices: 17 us -> 14.2 us
  local copies, waits for them, and re-layouts: 0.02 us -> 2.23 us
    ppermute x4, waiting for transfers between devices: 15.7 us -> 2.61 us  [edges(): return (lax.ppermute(bottom, 'tile', up), lax.ppermute(top, 'tile', down))]
    all_to_all x2, waiting for transfers between devices: 1.3 us -> 11.6 us  [exchange(): return lax.all_to_all(blocks, axis, 0, 0, tiled=True)]
    pallas_call x10, Pallas kernels: 21.1 us -> 16.2 us  [call(): pl.pallas_call(kernel, out_shape=shapes if len(shapes) > 1 else shapes[0]...]
    all_to_all x2, starting transfers between devices: 13.3 us -> 8.55 us  [exchange(): return lax.all_to_all(blocks, axis, 0, 0, tiled=True)]
    ppermute x4, starting transfers between devices: 5.37 us -> 9.25 us  [edges(): return (lax.ppermute(bottom, 'tile', up), lax.ppermute(top, 'tile', down))]
    unnamed x10 -> x16, local copies, waits for them, and re-layouts: 0.02 us -> 2.23 us
  transfers between devices with their start and end apart: 6 -> 6, of which waited for: 3 -> 3; matrix products, arithmetic and copies ran while one was open for 0% -> 0% of each run, Pallas kernels for 9% -> 6%
where the time goes in v2:
time: 118 us; the launch traced here: 117 us
  blocking collectives  66.2 us (56%)
  starting transfers between devices  17.8 us (15%)
  Pallas kernels  16.2 us (14%)
  waiting for transfers between devices  14.2 us (12%)
  local copies, waits for them, and re-layouts  2.23 us (2%)
    all_to_all x4, blocking collectives, exchange(): return lax.all_to_all(blocks, axis, 0, 0, tiled=True)  66.2 us
    pallas_call x10, Pallas kernels, call(): pl.pallas_call(kernel, out_shape=shapes if len(shapes) > 1 else shapes[0]...  16.2 us
    all_to_all x2, waiting for transfers between devices, exchange(): return lax.all_to_all(blocks, axis, 0, 0, tiled=True)  11.6 us
    ppermute x4, starting transfers between devices, edges(): return (lax.ppermute(bottom, 'tile', up), lax.ppermute(top, 'tile', down))  9.25 us
    all_to_all x2, starting transfers between devices, exchange(): return lax.all_to_all(blocks, axis, 0, 0, tiled=True)  8.55 us
    ppermute x4, waiting for transfers between devices, edges(): return (lax.ppermute(bottom, 'tile', up), lax.ppermute(top, 'tile', down))  2.61 us
  transfers between devices with their start and end apart: 6, of which 3 were waited for; matrix products, arithmetic and copies ran while one was open for 0% of the time, Pallas kernels for 6%

profile of v2, /device:TPU:1, one launch (start us, length us, event | category | flops | bytes accessed | tf_op | source)
XLA Modules:
  0.0 117.4 jit_solution(9143014878949419895)
XLA Ops:
  0.6 2.9 %shard_map.68 = (f32[8,64,256]{2,1,0:T(8,128)}, f32[64,256]{1,0:T(8,128)S(1)}, f32[8,8,1024]{2,1,0:T(8,128)S(1)}, f32[8,8,1024]{2,1,0:T(8,128)S(1)}) custom-call(bf16[256,1024]{1,0:T(8,128)(2,1)} %bitcast.10, f32[128,1024]{1,0:T(8,128)} %bitcast.5), custom_call_target="tpu_custom_call" | custom-call | flops 1000000000 | bytes 1048576 | tf_op jit(solution)/shard_map/pallas_call | solution.py:362
  3.5 2.5 %collective-permute-start = (f32[8,8,1024]{2,1,0:T(8,128)S(1)}, f32[8,8,1024]{2,1,0:T(8,128)S(1)}, u32[]{:S(2)}, u32[]{:S(2)}) collective-permute-start(f32[8,8,1024]{2,1,0:T(8,128)S(1)} %get-tuple-element.19), channel_id=1, source_target_pairs={{0,1},{1,2},{2,3},{3,4},{4,5},{5,6},{6,7},{7,0},{8,9},{9,10},{10,1... | collective-permute-start | bytes 786440 | tf_op jit(solution)/shard_map/ppermute | solution.py:391
  6.1 4.0 %collective-permute-start.1 = (f32[8,8,1024]{2,1,0:T(8,128)S(1)}, f32[8,8,1024]{2,1,0:T(8,128)S(1)}, u32[]{:S(2)}, u32[]{:S(2)}) collective-permute-start(f32[8,8,1024]{2,1,0:T(8,128)S(1)} %get-tuple-element.20), channel_id=1, source_target_pairs={{1,0},{2,1},{3,2},{4,3},{5,4},{6,5},{7,6},{0,7},{9,8},{10,9},{11,1... | collective-permute-start | bytes 786440 | tf_op jit(solution)/shard_map/ppermute | solution.py:391
  10.1 5.2 %all-to-all-start = ((f32[8,64,256]{2,1,0:T(8,128)}), f32[8,64,256]{2,1,0:T(8,128)S(1)}, u32[]{:S(2)}, u32[]{:S(2)}) async-start(f32[8,64,256]{2,1,0:T(8,128)} %get-tuple-element.25), calls=%async_computation | async-start | bytes 1048576 | tf_op jit(solution)/shard_map/all_to_all | solution.py:374
  15.3 0.0 copy-start.2
  15.3 0.0 copy-start.5
  15.3 0.1 pad_add_fusion.place_ref
  15.4 0.7 copy-done.2
  16.1 0.0 copy-done.5
  16.1 0.0 copy-start
  16.1 0.0 copy-start.4
  16.1 1.4 %shard_map.69 = (bf16[2,128,192]{2,1,0:T(8,128)(2,1)S(1)}, bf16[4,2,160,128]{3,2,1,0:T(8,128)(2,1)S(1)}, f32[64,512]{1,0:T(8,128)S(1)}) custom-call(s32[2]{0:T(128)S(1)} %pad_add_fusion.place_ref, f32[8,5]{1,0:T(8,128)S(1)} %bitcast.16, f32[64,64]{1,0:T(8,128)S(1)} %copy-done.2), custom_call_target="tpu_custom_call" | custom-call | flops 1000000000 | bytes 16552 | tf_op jit(solution)/shard_map/pallas_call | solution.py:362
  17.5 0.0 collective-permute-done.refs_3_
  17.5 0.0 collective-permute-done.1.refs_4_
  17.5 0.0 copy-done
  17.5 0.0 copy-done.4
  17.5 0.0 copy-start.1
  17.6 2.7 %shard_map.70 = (f32[128,1024]{1,0:T(8,128)S(1)}, f32[64,256]{1,0:T(8,128)S(1)}) custom-call(f32[128,1024]{1,0:T(8,128)S(1)} %bitcast.6, bf16[256,1024]{1,0:T(8,128)(2,1)S(1)} %bitcast.11, f32[64,256]{1,0:T(8,128)S(1)} %get-tuple-element.18.refs_2_, f32[8,8,1024]{2,1,0:T(8,128)S(1)} %collective-permute-done.refs_3_, ...), custom_call_target="tpu_custom_call" | custom-call | flops 99999997952 | bytes 2064384 | tf_op jit(solution)/shard_map/pallas_call | solution.py:362
  20.3 0.0 copy-start.6
  20.3 0.6 copy-done.6
  20.9 10.8 %all-to-all-done.c_ref = f32[8,64,256]{2,1,0:T(8,128)S(1)} async-done(((f32[8,64,256]{2,1,0:T(8,128)}), f32[8,64,256]{2,1,0:T(8,128)S(1)}, u32[]{:S(2)}, u32[]{:S(2)}) %all-to-all-start) | async-done | bytes 524320 | tf_op jit(solution)/shard_map/all_to_all | solution.py:374
  31.7 0.0 copy-done.1
  31.7 1.5 %shard_map.71 = f32[32,32,128]{2,1,0:T(8,128)S(1)} custom-call(bf16[256,1024]{1,0:T(8,128)(2,1)S(1)} %bitcast.12, f32[128,1024]{1,0:T(8,128)S(1)} %get-tuple-element.23.fine_ref, f32[64,256]{1,0:T(8,128)S(1)} %get-tuple-element.24.mean_ref, f32[8,64,256]{2,1,0:T(8,128)S(1)} %all-to-all-done.c_ref, f32[64,512]{1,0:T(8,128)S(1)} %get-tuple-element.26.mix_ref, ...), custom_call_target="tpu_custom_call" | custom-call | flops 1000000000 | bytes 2031616 | tf_op jit(solution)/shard_map/pallas_call | solution.py:362
  33.2 20.5 %all_to_all.30.arrived_ref = f32[32,32,128]{2,1,0:T(8,128)S(1)} all-to-all(f32[32,32,128]{2,1,0:T(8,128)S(1)} %shard_map.71), channel_id=1, replica_groups=mesh['mem_0'=4,'mem_1'=4,'mem_2'=2,'tile'=8] {'mem_0','mem_1','mem_2'}, dimensions={0} | all-to-all | bytes 1048576 | tf_op jit(solution)/shard_map/all_to_all | solution.py:374
  53.7 0.6 shard_map.72
  54.3 15.2 %all_to_all.31.v_ref.refs_1_.a_ref = f32[32,32,128]{2,1,0:T(8,128)S(1)} all-to-all(f32[32,32,128]{2,1,0:T(8,128)S(1)} %shard_map.72), channel_id=1, replica_groups=mesh['mem_0'=4,'mem_1'=4,'mem_2'=2,'tile'=8] {'mem_0','mem_1','mem_2'}, dimensions={0} | all-to-all | bytes 1048576 | tf_op jit(solution)/shard_map/all_to_all | solution.py:374
  69.5 1.4 %shard_map.73 = (f32[8,8,256]{2,1,0:T(8,128)}, f32[64,256]{1,0:T(8,128)S(1)}, f32[8,8,1024]{2,1,0:T(8,128)S(1)}, f32[8,8,1024]{2,1,0:T(8,128)S(1)}) custom-call(bf16[256,1024]{1,0:T(8,128)(2,1)S(1)} %bitcast.13, f32[32,32,128]{2,1,0:T(8,128)S(1)} %all_to_all.31.v_ref.refs_1_.a_ref), custom_call_target="tpu_custom_call" | custom-call | flops 1000000000 | bytes 1048576 | tf_op jit(solution)/shard_map/pallas_call | solution.py:362
  70.9 0.3 collective-permute-start.2
  71.2 2.4 %collective-permute-start.3 = (f32[8,8,1024]{2,1,0:T(8,128)S(1)}, f32[8,8,1024]{2,1,0:T(8,128)S(1)}, u32[]{:S(2)}, u32[]{:S(2)}) collective-permute-start(f32[8,8,1024]{2,1,0:T(8,128)S(1)} %get-tuple-element.29), channel_id=1, source_target_pairs={{1,0},{2,1},{3,2},{4,3},{5,4},{6,5},{7,6},{0,7},{9,8},{10,9},{11,1... | collective-permute-start | bytes 786440 | tf_op jit(solution)/shard_map/ppermute | solution.py:391
  73.6 3.4 %all-to-all-start.3 = ((f32[8,8,256]{2,1,0:T(8,128)}), f32[8,8,256]{2,1,0:T(8,128)S(1)}, u32[]{:S(2)}, u32[]{:S(2)}) async-start(f32[8,8,256]{2,1,0:T(8,128)} %get-tuple-element.32), calls=%async_computation.3 | async-start | bytes 131072 | tf_op jit(solution)/shard_map/all_to_all | solution.py:374
  76.9 2.6 %collective-permute-done.2.refs_4_ = f32[8,8,1024]{2,1,0:T(8,128)S(1)} collective-permute-done((f32[8,8,1024]{2,1,0:T(8,128)S(1)}, f32[8,8,1024]{2,1,0:T(8,128)S(1)}, u32[]{:S(2)}, u32[]{:S(2)}) %collective-permute-start.2) | collective-permute-done | bytes 262176 | tf_op jit(solution)/shard_map/ppermute | solution.py:391
  79.5 0.0 collective-permute-done.3.refs_5_
  79.5 0.0 copy-start.7
  79.6 0.9 copy-done.7
  80.5 0.0 copy-start.3
  80.5 2.9 %shard_map.74 = (f32[128,1024]{1,0:T(8,128)S(1)}, f32[64,256]{1,0:T(8,128)S(1)}, f32[8,128]{1,0:T(8,128)S(1)}) custom-call(f32[128,1024]{1,0:T(8,128)S(1)} %bitcast.8, f32[32,32,128]{2,1,0:T(8,128)S(1)} %all_to_all.31.v_ref.refs_1_.a_ref, bf16[256,1024]{1,0:T(8,128)(2,1)S(1)} %bitcast.14, f32[64,256]{1,0:T(8,128)S(1)} %get-tuple-element.27.refs_3_, ...), custom_call_target="tpu_custom_call" | custom-call | flops 99999997952 | bytes 2588672 | tf_op jit(solution)/shard_map/pallas_call | solution.py:362
  83.3 0.8 all-to-all-done.3.c_ref
  84.1 0.0 copy-done.3
  84.1 0.6 shard_map.75
  84.7 10.6 %all_to_all.32.smoothed_ref = f32[8,24,128]{2,1,0:T(8,128)S(1)} all-to-all(f32[8,24,128]{2,1,0:T(8,128)S(1)} %shard_map.75), channel_id=1, replica_groups=mesh['mem_0'=4,'mem_1'=4,'mem_2'=2,'tile'=8] {'tile'}, dimensions={0} | all-to-all | bytes 196608 | tf_op jit(solution)/shard_map/all_to_all | solution.py:374
  95.3 0.7 shard_map.76
  96.0 19.9 %all_to_all.33.arrived_ref = f32[32,40,128]{2,1,0:T(8,128)S(1)} all-to-all(f32[32,40,128]{2,1,0:T(8,128)S(1)} %shard_map.76), channel_id=1, replica_groups=mesh['mem_0'=4,'mem_1'=4,'mem_2'=2,'tile'=8] {'mem_0','mem_1','mem_2'}, dimensions={0} | all-to-all | bytes 1310720 | tf_op jit(solution)/shard_map/all_to_all | solution.py:374
  115.9 1.5 %shard_map.77 = (f32[4,32,32]{2,1,0:T(8,128)}, f32[4,32,32]{2,1,0:T(8,128)}) custom-call(s32[2]{0:T(128)S(1)} %pad_add_fusion.place_ref, f32[32,40,128]{2,1,0:T(8,128)S(1)} %all_to_all.33.arrived_ref, f32[128,1024]{1,0:T(8,128)S(1)} %bitcast.9, f32[32,32,128]{2,1,0:T(8,128)S(1)} %all_to_all.31.v_ref.refs_1_.a_ref), custom_call_target="tpu_custom_call" | custom-call | flops 1000000 | bytes 1703944 | tf_op jit(solution)/shard_map/pallas_call | solution.py:362
Async XLA Ops:
  3.5 14.0 %collective-permute-start = (f32[8,8,1024]{2,1,0:T(8,128)S(1)}, f32[8,8,1024]{2,1,0:T(8,128)S(1)}, u32[]{:S(2)}, u32[]{:S(2)}) collective-permute-start(f32[8,8,1024]{2,1,0:T(8,128)S(1)} %get-tuple-element.19), channel_id=1, source_target_pairs={{0,1},{1,2},{2,3},{3,4},{4,5},{5,6},{6,7},{7,0},{8,9},{9,10},{10,1... | collective-permute-start | bytes 786440 | tf_op jit(solution)/shard_map/ppermute | solution.py:391
  6.1 11.4 %collective-permute-start.1 = (f32[8,8,1024]{2,1,0:T(8,128)S(1)}, f32[8,8,1024]{2,1,0:T(8,128)S(1)}, u32[]{:S(2)}, u32[]{:S(2)}) collective-permute-start(f32[8,8,1024]{2,1,0:T(8,128)S(1)} %get-tuple-element.20), channel_id=1, source_target_pairs={{1,0},{2,1},{3,2},{4,3},{5,4},{6,5},{7,6},{0,7},{9,8},{10,9},{11,1... | collective-permute-start | bytes 786440 | tf_op jit(solution)/shard_map/ppermute | solution.py:391
  10.1 21.6 %all-to-all-start = ((f32[8,64,256]{2,1,0:T(8,128)}), f32[8,64,256]{2,1,0:T(8,128)S(1)}, u32[]{:S(2)}, u32[]{:S(2)}) async-start(f32[8,64,256]{2,1,0:T(8,128)} %get-tuple-element.25), calls=%async_computation | async-start | bytes 1048576 | tf_op jit(solution)/shard_map/all_to_all | solution.py:374
  15.3 0.8 copy-start.2
  15.3 0.7 copy-start.5
  16.1 1.5 %copy-start = (f32[4,32,1024]{2,1,0:T(8,128)S(1)}, f32[4,32,1024]{2,1,0:T(8,128)}, u32[]{:S(2)}) copy-start(f32[4,32,1024]{2,1,0:T(8,128)} %param.6) | copy-start | bytes 1572868
  16.1 1.5 %copy-start.4 = (bf16[2,4,32,1024]{3,2,1,0:T(8,128)(2,1)S(1)}, bf16[2,4,32,1024]{3,2,1,0:T(8,128)(2,1)}, u32[]{:S(2)}) copy-start(bf16[2,4,32,1024]{3,2,1,0:T(8,128)(2,1)} %param.5) | copy-start | bytes 1572868
  17.5 14.2 %copy-start.1 = (f32[256,256]{1,0:T(8,128)S(1)}, f32[256,256]{1,0:T(8,128)}, u32[]{:S(2)}) copy-start(f32[256,256]{1,0:T(8,128)} %lon_ref.3) | copy-start | bytes 786436
  20.3 0.7 copy-start.6
  70.9 8.6 %collective-permute-start.2 = (f32[8,8,1024]{2,1,0:T(8,128)S(1)}, f32[8,8,1024]{2,1,0:T(8,128)S(1)}, u32[]{:S(2)}, u32[]{:S(2)}) collective-permute-start(f32[8,8,1024]{2,1,0:T(8,128)S(1)} %get-tuple-element.28), channel_id=1, source_target_pairs={{0,1},{1,2},{2,3},{3,4},{4,5},{5,6},{6,7},{7,0},{8,9},{9,10},{10,1... | collective-permute-start | bytes 786440 | tf_op jit(solution)/shard_map/ppermute | solution.py:391
  71.2 8.4 %collective-permute-start.3 = (f32[8,8,1024]{2,1,0:T(8,128)S(1)}, f32[8,8,1024]{2,1,0:T(8,128)S(1)}, u32[]{:S(2)}, u32[]{:S(2)}) collective-permute-start(f32[8,8,1024]{2,1,0:T(8,128)S(1)} %get-tuple-element.29), channel_id=1, source_target_pairs={{1,0},{2,1},{3,2},{4,3},{5,4},{6,5},{7,6},{0,7},{9,8},{10,9},{11,1... | collective-permute-start | bytes 786440 | tf_op jit(solution)/shard_map/ppermute | solution.py:391
  73.6 10.5 %all-to-all-start.3 = ((f32[8,8,256]{2,1,0:T(8,128)}), f32[8,8,256]{2,1,0:T(8,128)S(1)}, u32[]{:S(2)}, u32[]{:S(2)}) async-start(f32[8,8,256]{2,1,0:T(8,128)} %get-tuple-element.32), calls=%async_computation.3 | async-start | bytes 131072 | tf_op jit(solution)/shard_map/all_to_all | solution.py:374
  79.5 0.9 copy-start.7
  80.5 3.6 %copy-start.3 = (f32[64,64]{1,0:T(8,128)S(1)}, f32[64,64]{1,0:T(8,128)}, u32[]{:S(2)}) copy-start(f32[64,64]{1,0:T(8,128)} %lat_ref.3) | copy-start | bytes 49156

commit v3 on v2

--- a/solution.py
+++ b/solution.py
@@ -81,7 +81,7 @@
 
 def natural(blocks):
     rows = []
-    for tall in range(16):
+    for tall in range(blocks.shape[0] // 2):
         lanes = [
             blocks[2 * tall + wide // 4, 8 * (wide % 4) : 8 * (wide % 4) + 8, :]
             for wide in range(8)
@@ -90,8 +90,16 @@
     return jnp.concatenate(rows, axis=0)
 
 
-def detail_kernel(x_ref, v_ref, *out_refs):
-    detail(x_ref[...], natural(v_ref), *out_refs)
+def for_each(v):
+    return jnp.concatenate([v] * (256 // v.shape[0]), axis=0)
+
+
+def members_of(refs):
+    return refs[0][...] if len(refs) == 1 else jnp.concatenate([ref[...] for ref in refs], axis=0)
+
+
+def detail_kernel(v_ref, *refs):
+    detail(members_of(refs[:4]), natural(v_ref), *refs[4:])
 
 
 def first_detail_kernel(x_hbm, v_hbm, *refs):
@@ -109,15 +117,15 @@
     detail(x_ref[...], v_ref[...], *out_refs)
 
 
-def detail(x, v, c_ref, own_ref, top_ref, bottom_ref):
-    w = x.astype(F32) * jnp.concatenate([v, v], axis=0)
+def detail(x, v, top_ref, bottom_ref, c_ref, own_ref=None):
+    w = x.astype(F32) * for_each(v)
     c = block_mean(w, split3)
-    if c_ref.shape == (TILES, 64, 256):
+    if own_ref is None:
         for tile in range(TILES):
             c_ref[tile] = c
     else:
         c_ref[...] = c.reshape(PAIRS, 8, 256)
-    own_ref[...] = c
+        own_ref[...] = c
     spread = prolong(c, edges=True)
     for pair in range(PAIRS):
         at = ROWS * pair
@@ -125,9 +133,46 @@
         bottom_ref[pair] = w[at + 24 : at + 32] - spread[16 * pair + 8 : 16 * pair + 16]
 
 
-def table_kernel(place_ref, taps_ref, lat_ref, *refs):
-    rows_ref, band_ref, mix_ref = refs
-    tile = place_ref[0]
+def row_table(taps, tile):
+    i, j = iotas(160, 192)
+    first = jnp.zeros((160, 192), F32)
+    for k in range(4):
+        row, col = i - 40 * k, j - 48 * k
+        dist = jnp.abs(col - row - 4)
+        spot, source = tile * ROWS - 4 + row, tile * ROWS - 8 + col
+        fits = (row >= 0) & (row < 40) & (col >= 0) & (col < 48)
+        fits = fits & (spot >= 0) & (spot < ROWS * TILES)
+        fits = fits & (source >= 0) & (source < ROWS * TILES)
+        dist = jnp.where(fits, dist, 9)
+        for o in range(5):
+            first = jnp.where(dist == o, taps[o][k], first)
+    i, j = iotas(128, 160)
+    second = jnp.zeros((128, 160), F32)
+    for k in range(4):
+        row, col = i - 32 * k, j - 40 * k
+        fits = (row >= 0) & (row < 32) & (col >= 0) & (col < 40)
+        dist = jnp.where(fits, jnp.abs(col - row - 4), 9)
+        for o in range(5):
+            second = jnp.where(dist == o, taps[o][k], second)
+    return exact_mm(second, first)
+
+
+def band_table(taps):
+    i, j = iotas(8, 128)
+    before, after = jnp.abs(i - 8 - j), jnp.abs(i + 128 - j)
+    i, j = iotas(128, 128)
+    inner = jnp.abs(i - j)
+    left, right = jnp.zeros((8, 128), F32), jnp.zeros((8, 128), F32)
+    middle = jnp.zeros((128, 128), F32)
+    for o in range(9):
+        left = jnp.where(before == o, taps[o], left)
+        right = jnp.where(after == o, taps[o], right)
+        middle = jnp.where(inner == o, taps[o], middle)
+    rest = jnp.zeros((8, 128), F32)
+    return jnp.concatenate([rest, left, middle, right, rest], axis=0)
+
+
+def taps_of(taps_ref):
     taps = taps_ref[...]
     square = taps * taps
     energy = square[:, 0:1] + 2.0 * jnp.sum(square[:, 1:5], axis=1, keepdims=True)
@@ -138,47 +183,37 @@
     for o in range(9):
         terms = [once[i] * once[o + 8 - i] for i in range(o, 9)]
         double.append(functools.reduce(jnp.add, terms))
-    i, j = iotas(160, 192)
-    first = jnp.zeros((160, 192), F32)
-    for level in range(4):
-        row, col = i - 40 * level, j - 48 * level
-        dist = jnp.abs(col - row - 4)
-        spot, source = tile * ROWS - 4 + row, tile * ROWS - 8 + col
-        fits = (row >= 0) & (row < 40) & (col >= 0) & (col < 48)
-        fits = fits & (spot >= 0) & (spot < ROWS * TILES)
-        fits = fits & (source >= 0) & (source < ROWS * TILES)
-        dist = jnp.where(fits, dist, 9)
-        for o in range(5):
-            first = jnp.where(dist == o, single[o][level : level + 1], first)
-    i, j = iotas(128, 160)
-    second = jnp.zeros((128, 160), F32)
-    for level in range(4):
-        row, col = i - 32 * level, j - 40 * level
-        fits = (row >= 0) & (row < 32) & (col >= 0) & (col < 40)
-        dist = jnp.where(fits, jnp.abs(col - row - 4), 9)
-        for o in range(5):
-            second = jnp.where(dist == o, single[o][level : level + 1], second)
-    both = exact_mm(second, first)
-    for kind, piece in enumerate(split2(both)):
+    lat = [[tap[k : k + 1] for k in range(4)] for tap in single]
+    lon = [[tap[4 + k : 5 + k] for k in range(4)] for tap in double]
+    return lat, lon
+
+
+def fill_tables(lat, lon, tile, rows_ref, band_ref):
+    for kind, piece in enumerate(split2(row_table(lat, tile))):
         rows_ref[kind] = piece
-    i, j = iotas(8, 128)
-    before = jnp.abs(i - 8 - j)
-    after = jnp.abs(i + 128 - j)
-    i, j = iotas(128, 128)
-    inner = jnp.abs(i - j)
-    for level in range(4):
-        corner = (jnp.zeros((8, 128), F32), jnp.zeros((8, 128), F32))
-        middle = jnp.zeros((128, 128), F32)
-        for o in range(9):
-            tap = double[o][4 + level : 5 + level]
-            corner = tuple(
-                jnp.where(dist == o, tap, c) for dist, c in zip((before, after), corner)
-            )
-            middle = jnp.where(inner == o, tap, middle)
-        rest = jnp.zeros((8, 128), F32)
-        band = jnp.concatenate([rest, corner[0], middle, corner[1], rest], axis=0)
-        for kind, piece in enumerate(split2(band)):
+    for level in range(band_ref.shape[0]):
+        for kind, piece in enumerate(split2(band_table([tap[level] for tap in lon]))):
             band_ref[level, kind] = piece
+
+
+def table_kernel(place_ref, taps_ref, lat_ref, x_ref, *refs):
+    mix_ref, rows_ref, band_ref, *x_next_refs = refs
+    tile, own = place_ref[0], place_ref[1] >> 3
+
+    def picked(values):
+        value = values[3]
+        for k in range(3):
+            value = jnp.where(own == k, values[k], value)
+        return value
+
+    lat, lon = ([[picked(tap)] * 4 for tap in taps] for taps in taps_of(taps_ref))
+    fill_tables(lat, lon, tile, rows_ref, band_ref)
+    for ahead, x_next_ref in enumerate(x_next_refs):
+        for member in range(2):
+            row = ROWS * (4 * member + ((own + ahead) & 3))
+            x_next_ref[ROWS * member : ROWS * member + ROWS] = x_ref[
+                pl.ds(pl.multiple_of(row, ROWS), ROWS), :
+            ]
     i, j = iotas(64, 512)
     repeat = jnp.where((i >> 3) == (j >> 6), jnp.where((i & 7) == (j & 7), 1.0, 0.0), 0.0)
     mine = lat_ref[pl.ds(pl.multiple_of(8 * tile, 8), 8), :]
@@ -195,12 +230,12 @@
     return jnp.concatenate([left, right], axis=1)
 
 
-def windows(parts, first_row):
+def windows(parts, first_row, height):
     rows = []
     for block in range(4):
         for part in parts:
             lanes = [
-                part[first_row : first_row + ROWS, 128 * tile : 128 * tile + 128]
+                part[first_row : first_row + height, 128 * tile : 128 * tile + 128]
                 for tile in ((2 * block - 1) % 8, 2 * block, 2 * block + 1, (2 * block + 2) % 8)
             ]
             rows.append(jnp.concatenate(lanes, axis=1))
@@ -221,45 +256,68 @@
 
 def fine_kernel(last, *refs):
     if last:
-        r_ref, *refs = refs
-    v_ref, x_ref, c_ref, before_ref, after_ref, rows_ref, band_ref, *refs = refs
-    fine_ref, mean_ref, *refs = refs
-    f_ref = refs[-1]
-    v = natural(v_ref) if last else v_ref[...]
-    d = x_ref[...].astype(F32) * jnp.concatenate([v, v], axis=0) - prolong(c_ref[...])
+        place_ref, r_ref, *refs = refs
+        v_ref, c_ref, *refs = refs
+    else:
+        *refs, fine_ref, c_ref, rows_ref, band_ref, sems = refs
+        place_ref, v_ref, c_hbm, taps_ref, *refs = refs
+        loading = pltpu.make_async_copy(c_hbm.at[0], c_ref, sems.at[0])
+        loading.start()
+        fill_tables(*taps_of(taps_ref), place_ref[0], rows_ref, band_ref)
+    before_ref, after_ref, *refs = refs
+    if last:
+        rows_ref, band_ref, *refs = refs
+    x_refs, refs = (refs[:4], refs[4:]) if last else (refs[:1], refs[1:])
+    x = members_of(x_refs)
+    if last:
+        fine_ref, mean_ref, sums_ref, f_ref = refs
+        v = natural(v_ref)
+    else:
+        fine_hbm, mean_ref, f_ref = refs
+        v = v_ref[...]
+        loading.wait()
+    d = x.astype(F32) * for_each(v) - prolong(c_ref[...])
     highs, lows = [], []
-    for member in range(2):
+    for part in range(2):
         rows = []
-        for level in range(4):
-            pair = 4 * member + level
+        for pair in range(4 * part, 4 * part + 4):
             rows += [before_ref[pair], d[ROWS * pair : ROWS * pair + ROWS], after_ref[pair]]
         high, low = split2(jnp.concatenate(rows, axis=0))
         passed = mm(rows_ref[0], high) + mm(rows_ref[0], low) + mm(rows_ref[1], high)
         high, low = split2(passed)
         highs.append(high)
         lows.append(low)
-    for level in range(4):
-        high = windows(highs, ROWS * level)
-        low = windows(lows, ROWS * level)
+    levels = band_ref.shape[0]
+    height = 128 // levels
+    for level in range(levels):
+        high = windows(highs, height * level, height)
+        low = windows(lows, height * level, height)
         table_high, table_low = banded(band_ref, level, 0), banded(band_ref, level, 1)
         result = mm(high, table_high) + mm(low, table_high) + mm(high, table_low)
         for block in range(4):
             lanes = slice(256 * block, 256 * block + 256)
             summed = None
-            for member in range(2):
-                row = ROWS * (4 * member + level)
-                at = 64 * block + ROWS * member
-                f = result[at : at + ROWS]
-                f_ref[row : row + ROWS, lanes] = f
-                term = x_ref[row : row + ROWS, lanes].astype(F32) * f
-                summed = term if summed is None else summed + term
+            for part in range(2):
+                for inner in range(height // ROWS):
+                    row = 128 * part + height * level + ROWS * inner
+                    at = height * (2 * block + part) + ROWS * inner
+                    f = result[at : at + ROWS]
+                    f_ref[row : row + ROWS, lanes] = f
+                    term = x[row : row + ROWS, lanes].astype(F32) * f
+                    summed = term if summed is None else summed + term
             fine_ref[ROWS * level : ROWS * level + ROWS, lanes] = summed
+    if not last:
+        copy = pltpu.make_async_copy(fine_ref, fine_hbm, sems.at[1])
+        copy.start()
     means = block_mean(f_ref[...], split2)
     mean_ref[...] = means
-    if last:
-        r = r_ref[...]
+    if not last:
+        copy.wait()
+    else:
+        own = place_ref[1] >> 3
+        r = r_ref[pl.ds(pl.multiple_of(ROWS * own, ROWS), ROWS), :]
         products = total(v * fine_ref[...]) - 16.0 * total(c_ref[...] * means)
-        refs[0][...] = lane_sums(
+        sums_ref[...] = lane_sums(
             ((0, total(r * r)), (1, total(r * v)), (2, total(v * v)), (3, products))
         )
 
@@ -274,18 +332,20 @@
         out_ref[tile, 16:24, :] = sums
 
 
-def blended(x_ref, fine_ref, smoothed):
-    spread = prolong(smoothed)
-    return (
-        fine_ref[...]
-        + x_ref[:128].astype(F32) * spread[:128]
-        + x_ref[128:].astype(F32) * spread[128:]
-    )
-
-
-def partial_kernel(x_ref, fine_ref, mean_ref, c_ref, mix_ref, lon_ref, out_ref):
+def blended(x, fine_ref, smoothed):
+    product = x.astype(F32) * prolong(smoothed)
+    height = fine_ref.shape[0]
+    pieces = [product[k : k + height] for k in range(0, 256, height)]
+    return functools.reduce(jnp.add, pieces, fine_ref[...])
+
+
+def partial_kernel(x_ref, fine_hbm, mean_ref, c_ref, mix_ref, lon_ref, out_ref, fine_ref, sem):
+    copy = pltpu.make_async_copy(fine_hbm, fine_ref, sem)
+    copy.start()
     across = exact_mm(mix_ref[...], c_ref[...].reshape(512, 256))
-    p = blended(x_ref, fine_ref, exact_mm(across, lon_ref[...]) - mean_ref[...])
+    smoothed = exact_mm(across, lon_ref[...]) - mean_ref[...]
+    copy.wait()
+    p = blended(x_ref[...], fine_ref, smoothed)
     for tall in range(16):
         for wide in range(8):
             out_ref[2 * tall + wide // 4, 8 * (wide % 4) : 8 * (wide % 4) + 8, :] = p[
@@ -293,14 +353,34 @@
             ]
 
 
-def last_partial_kernel(x_ref, fine_ref, mean_ref, smoothed_ref, out_ref):
+def packed(field):
+    group = lax.broadcasted_iota(jnp.int32, (8, 128), 1) >> 5
+    shares = []
+    for wide in range(8):
+        tiles = [field[8 * i : 8 * i + 8, 128 * wide : 128 * wide + 128] for i in range(4)]
+        for g in range(4):
+            share = None
+            for i in range(4):
+                turned = pltpu.roll(tiles[i], (32 * (i - g)) % 128, 1) if i != g else tiles[i]
+                share = turned if share is None else jnp.where(group == i, turned, share)
+            shares.append(share)
+    return shares
+
+
+def last_partial_kernel(place_ref, fine_ref, mean_ref, smoothed_ref, v_ref, *refs):
+    *x_refs, out_ref, v_packed = refs
     halves = [smoothed_ref[:, 8 * k : 8 * k + 8, :].reshape(64, 128) for k in range(2)]
-    p = blended(x_ref, fine_ref, jnp.concatenate(halves, axis=1) - mean_ref[...])
-    turned = p.T
+    p = blended(members_of(x_refs), fine_ref, jnp.concatenate(halves, axis=1) - mean_ref[...])
     sums = jnp.sum(smoothed_ref[:, 16:24, :], axis=0)
+    for group, share in enumerate(packed(p)):
+        out_ref[group, 0:8, :] = share
+    for group, share in enumerate(packed(natural(v_ref))):
+        v_packed[group] = share
+    i, j = iotas(8, 128)
+    mine = pl.ds(place_ref[1] & 7, 1)
     for group in range(GROUPS):
-        out_ref[group, :32, :] = turned[32 * group : 32 * group + 32]
-        out_ref[group, 32:40, :] = sums
+        row = jnp.broadcast_to(v_packed[group, mine, :], (8, 128))
+        out_ref[group, 8:16, :] = jnp.where(i == 1, row, sums)
 
 
 def share_kernel(scale, place_ref, arrived_ref, r_ref, out_ref):
@@ -311,36 +391,37 @@
     ]
     share = jnp.concatenate([share[:, 128 * k : 128 * k + 128] for k in range(4)], axis=0)
     share = share + jnp.sum(arrived_ref[...], axis=0) * scale
-    for other in range(GROUPS):
+    for other in range(out_ref.shape[0]):
         out_ref[other] = share
 
 
-def final_kernel(scale, place_ref, arrived_ref, r_ref, a_ref, x_out, res_out, r_turned, a_turned):
+def final_kernel(scale, place_ref, arrived_ref, r_ref, x_out, res_out):
     group = place_ref[1]
-    wide = group >> 2
-    lanes = pl.ds(pl.multiple_of(128 * wide, 128), 128)
-    r_turned[...] = r_ref[:, lanes].T
-    rows = [
-        a_ref[2 * tall + (wide >> 2), pl.ds(pl.multiple_of(8 * (wide & 3), 8), 8), :]
-        for tall in range(16)
-    ]
-    a_turned[...] = jnp.concatenate(rows, axis=0).T
-    mine = pl.ds(pl.multiple_of(32 * (group & 3), 32), 32)
-    r, a = r_turned[mine, :], a_turned[mine, :]
-    arrived = jnp.sum(arrived_ref[...], axis=0)
-    b = a + arrived[:32] * scale
+    lanes = pl.ds(pl.multiple_of(128 * (group >> 2), 128), 128)
     i, j = iotas(8, 128)
-    rr, ra, aa, af, ac = (
-        total(jnp.where((i == 0) & (j == k), arrived[32:40], 0.0)) for k in range(5)
-    )
-    rr, ra, aa = rr / GROUPS, ra / GROUPS, aa / GROUPS
+    sums = jnp.sum(arrived_ref[:, 8:16, :], axis=0)
+    rr, ra, aa, af, ac = (total(jnp.where((i == 0) & (j == k), sums, 0.0)) for k in range(5))
+    rr, ra, aa = rr / 8, ra / 8, aa / 8
     step = rr / ra
     ab = aa + (af + ac) * scale
     squares = step * step * aa - rr
     next_step = squares / ((ra - step * aa) - step * (aa - step * ab))
-    r_next = r - step * a
-    x_out[...] = (step * r + next_step * r_next).T.reshape(4, ROWS, 32)
-    res_out[...] = (r_next - next_step * (a - step * b)).T.reshape(4, ROWS, 32)
+    for level in range(4):
+        r = jnp.zeros((8, 128), F32)
+        for k in range(4):
+            row = ROWS * level + 8 * k
+            tile = r_ref[row : row + 8, lanes]
+            turned = pltpu.roll(tile, (32 * (k + 4 - (group & 3))) & 127, 1)
+            r = jnp.where((j >> 5) == k, turned, r)
+        a = jnp.concatenate([arrived_ref[8 * level + k, 9:10, :] for k in range(8)], axis=0)
+        p = jnp.sum(arrived_ref[8 * level : 8 * level + 8, 0:8, :], axis=0)
+        b = a + p * scale
+        r_next = r - step * a
+        x_new = step * r + next_step * r_next
+        res_new = r_next - next_step * (a - step * b)
+        for k in range(4):
+            x_out[level, 8 * k : 8 * k + 8, :] = x_new[:, 32 * k : 32 * k + 32]
+            res_out[level, 8 * k : 8 * k + 8, :] = res_new[:, 32 * k : 32 * k + 32]
 
 
 VMEM = pl.BlockSpec(memory_space=pltpu.VMEM)
@@ -391,9 +472,9 @@
         return lax.ppermute(bottom, "tile", up), lax.ppermute(top, "tile", down)
 
     own = ((64, 256), F32)
-    c, c_own, top, bottom = call(
+    top, bottom, c = call(
         first_detail_kernel,
-        [((TILES, 64, 256), F32), own, edge, edge],
+        [edge, edge, ((TILES, 64, 256), F32)],
         [HBM] * 2,
         (x, r),
         10**9,
@@ -406,62 +487,80 @@
         ),
     )
     c_first = exchange(c, "tile")
-    *tables, mix = call(
-        table_kernel,
-        [
-            ((2, 128, 192), BF16),
-            ((levels, 2, 160, 128), BF16),
-            ((64, 512), F32),
-        ],
-        [SMEM, VMEM, VMEM],
-        (place, fine_taps.reshape(2 * levels, 5), coarse_lat),
-        10**9,
-        6,
-    )
+    taps = fine_taps.reshape(2 * levels, 5)
+    rows_shape, band_shape = (2, 128, 192), (2, 160, 128)
     fine_scratch = [pltpu.VMEM((256, LON), F32)]
     fine, means = call(
         functools.partial(fine_kernel, False),
         [half, own],
-        [VMEM] * 7,
-        (r, x, c_own, *edges(top, bottom), *tables),
+        [SMEM, VMEM, HBM] + [VMEM] * 4,
+        (place, r, c, taps, *edges(top, bottom), x),
         10**11,
         16,
-        scratch=fine_scratch,
-    )
+        scratch=[
+            *fine_scratch,
+            pltpu.VMEM(*half),
+            pltpu.VMEM(*own),
+            pltpu.VMEM(rows_shape, BF16),
+            pltpu.VMEM((levels, *band_shape), BF16),
+            pltpu.SemaphoreType.DMA((2,)),
+        ],
+        out_specs=[HBM, VMEM],
+    )
+    means, x_again = lax.optimization_barrier((means, x))
+    mix, rows_next, band_next, *x_next = call(
+        table_kernel,
+        [
+            ((64, 512), F32),
+            (rows_shape, BF16),
+            ((1, *band_shape), BF16),
+            *[((count * height, extent), BF16)] * 4,
+        ],
+        [SMEM] + [VMEM] * 3,
+        (place, taps, coarse_lat, x_again),
+        10**9,
+        6,
+    )
+    for ahead in range(1, 4):
+        ring = [(i, (i + ahead) % 4) for i in range(4)]
+        x_next[ahead] = lax.ppermute(x_next[ahead], "mem_0", ring)
+    fine, x_next = lax.optimization_barrier((fine, x_next))
     shares = call(
         partial_kernel,
         [shared],
-        [VMEM] * 6,
+        [VMEM, HBM] + [VMEM] * 4,
         (x, fine, means, c_first, mix, coarse_lon),
         10**9,
         12,
+        scratch=[pltpu.VMEM(*half), pltpu.SemaphoreType.DMA],
     )
     arrived = exchange(shares, MEM)
     share = call(
         functools.partial(share_kernel, scale),
-        [shared],
+        [((TILES, 32, 128), F32)],
         [SMEM, VMEM, VMEM],
         (place, arrived, r),
         10**6,
         6,
     )
-    a = exchange(share, MEM)
-
-    c, c_own, top, bottom = call(
+    a = exchange(share, ("mem_1", "mem_2"))
+
+    top, bottom, c, c_own = call(
         detail_kernel,
-        [((PAIRS, 8, 256), F32), own, edge, edge],
-        [VMEM] * 2,
-        (x, a),
+        [edge, edge, ((PAIRS, 8, 256), F32), own],
+        [VMEM] * 5,
+        (a, *x_next),
         10**9,
         12,
     )
     beside = edges(top, bottom)
     c = exchange(c, "tile")
+    level = ((height, LON), F32)
     fine, means, sums = call(
         functools.partial(fine_kernel, True),
-        [half, own, ((8, 128), F32)],
-        [VMEM] * 8,
-        (r, a, x, c_own, *beside, *tables),
+        [level, own, ((8, 128), F32)],
+        [SMEM] + [VMEM] * 11,
+        (place, r, a, c_own, *beside, rows_next, band_next, *x_next),
         10**11,
         16,
         scratch=fine_scratch,
@@ -477,11 +576,12 @@
     smoothed = exchange(smoothed, "tile")
     shares = call(
         last_partial_kernel,
-        [((GROUPS, 40, 128), F32)],
-        [VMEM] * 4,
-        (x, fine, means, smoothed),
+        [((GROUPS, 16, 128), F32)],
+        [SMEM] + [VMEM] * 8,
+        (place, fine, means, smoothed, a, *x_next),
         10**9,
         12,
+        scratch=[pltpu.VMEM((GROUPS, 8, 128), F32)],
     )
     arrived = exchange(shares, MEM)
     out = ((levels, height, extent // GROUPS), F32)
@@ -489,11 +589,10 @@
         call(
             functools.partial(final_kernel, scale),
             [out, out],
-            [SMEM, VMEM, VMEM, VMEM],
-            (place, arrived, r, a),
+            [SMEM, VMEM, VMEM],
+            (place, arrived, r),
             10**6,
             6,
-            scratch=(pltpu.VMEM((128, 128), F32), pltpu.VMEM((128, 128), F32)),
         )
     )
 

time: 118 us -> 110 us (0.932)
  blocking collectives: 66.2 us -> 54.4 us
  starting transfers between devices: 17.8 us -> 25.7 us
  waiting for transfers between devices: 14.2 us -> 8.62 us
  Pallas kernels: 16.2 us -> 20.2 us
  local copies, waits for them, and re-layouts: 2.23 us -> 0.09 us
    all_to_all x4, blocking collectives: 66.2 us -> 54.4 us  [exchange(): return lax.all_to_all(blocks, axis, 0, 0, tiled=True)]
    all_to_all x2, waiting for transfers between devices: 11.6 us -> 3.77 us  [exchange(): return lax.all_to_all(blocks, axis, 0, 0, tiled=True)]
    ppermute x0 -> x3, starting transfers between devices: none -> 5.06 us  [local(): x_next[ahead] = lax.ppermute(x_next[ahead], 'mem_0', ring)]
    ppermute x0 -> x3, waiting for transfers between devices: none -> 4.32 us  [local(): x_next[ahead] = lax.ppermute(x_next[ahead], 'mem_0', ring)]
    pallas_call x10, Pallas kernels: 16.2 us -> 20.2 us  [call(): pl.pallas_call(kernel, out_shape=shapes if len(shapes) > 1 else shapes[0]...]
    all_to_all x2, starting transfers between devices: 8.55 us -> 11.4 us  [exchange(): return lax.all_to_all(blocks, axis, 0, 0, tiled=True)]
    unnamed x16 -> x10, local copies, waits for them, and re-layouts: 2.23 us -> 0.09 us
    ppermute x4, waiting for transfers between devices: 2.61 us -> 0.53 us  [edges(): return (lax.ppermute(bottom, 'tile', up), lax.ppermute(top, 'tile', down))]
  transfers between devices with their start and end apart: 6 -> 9, of which waited for: 3 -> 5; matrix products, arithmetic and copies ran while one was open for 0% -> 0% of each run, Pallas kernels for 6% -> 9%
where the time goes in v3:
time: 110 us
  blocking collectives  54.4 us (49%)
  starting transfers between devices  25.7 us (23%)
  Pallas kernels  20.2 us (18%)
  waiting for transfers between devices  8.62 us (8%)
    all_to_all x4, blocking collectives, exchange(): return lax.all_to_all(blocks, axis, 0, 0, tiled=True)  54.4 us
    pallas_call x10, Pallas kernels, call(): pl.pallas_call(kernel, out_shape=shapes if len(shapes) > 1 else shapes[0]...  20.2 us
    all_to_all x2, starting transfers between devices, exchange(): return lax.all_to_all(blocks, axis, 0, 0, tiled=True)  11.4 us
    ppermute x4, starting transfers between devices, edges(): return (lax.ppermute(bottom, 'tile', up), lax.ppermute(top, 'tile', down))  9.25 us
    ppermute x3, starting transfers between devices, local(): x_next[ahead] = lax.ppermute(x_next[ahead], 'mem_0', ring)  5.06 us
    ppermute x3, waiting for transfers between devices, local(): x_next[ahead] = lax.ppermute(x_next[ahead], 'mem_0', ring)  4.32 us
    all_to_all x2, waiting for transfers between devices, exchange(): return lax.all_to_all(blocks, axis, 0, 0, tiled=True)  3.77 us
  transfers between devices with their start and end apart: 9, of which 5 were waited for; matrix products, arithmetic and copies ran while one was open for 0% of the time, Pallas kernels for 9%

profile of v3, /device:TPU:1, one launch (start us, length us, event | category | flops | bytes accessed | tf_op | source)
XLA Modules:
  0.0 109.7 jit_solution(922404882005607194)
XLA Ops:
  0.6 2.9 %shard_map.68 = (f32[8,8,1024]{2,1,0:T(8,128)S(1)}, f32[8,8,1024]{2,1,0:T(8,128)S(1)}, f32[8,64,256]{2,1,0:T(8,128)}) custom-call(bf16[256,1024]{1,0:T(8,128)(2,1)} %bitcast.10, f32[128,1024]{1,0:T(8,128)} %bitcast.5), custom_call_target="tpu_custom_call" | custom-call | flops 1000000000 | bytes 1048576 | tf_op jit(solution)/shard_map/pallas_call | solution.py:443
  3.5 2.5 %collective-permute-start = (f32[8,8,1024]{2,1,0:T(8,128)S(1)}, f32[8,8,1024]{2,1,0:T(8,128)S(1)}, u32[]{:S(2)}, u32[]{:S(2)}) collective-permute-start(f32[8,8,1024]{2,1,0:T(8,128)S(1)} %get-tuple-element.29), channel_id=1, source_target_pairs={{0,1},{1,2},{2,3},{3,4},{4,5},{5,6},{6,7},{7,0},{8,9},{9,10},{10,1... | collective-permute-start | bytes 786440 | tf_op jit(solution)/shard_map/ppermute | solution.py:472
  6.1 4.0 %collective-permute-start.1 = (f32[8,8,1024]{2,1,0:T(8,128)S(1)}, f32[8,8,1024]{2,1,0:T(8,128)S(1)}, u32[]{:S(2)}, u32[]{:S(2)}) collective-permute-start(f32[8,8,1024]{2,1,0:T(8,128)S(1)} %get-tuple-element.30), channel_id=1, source_target_pairs={{1,0},{2,1},{3,2},{4,3},{5,4},{6,5},{7,6},{0,7},{9,8},{10,9},{11,1... | collective-permute-start | bytes 786440 | tf_op jit(solution)/shard_map/ppermute | solution.py:472
  10.1 0.0 copy-start
  10.1 0.0 copy-start.3
  10.1 5.3 %all-to-all-start = ((f32[8,64,256]{2,1,0:T(8,128)}), f32[8,64,256]{2,1,0:T(8,128)S(1)}, u32[]{:S(2)}, u32[]{:S(2)}) async-start(f32[8,64,256]{2,1,0:T(8,128)} %get-tuple-element.28.refs_2_), calls=%async_computation | async-start | bytes 1048576 | tf_op jit(solution)/shard_map/all_to_all | solution.py:455
  15.4 0.0 copy-start.4
  15.4 0.1 pad_add_fusion.refs_0_.place_ref
  15.5 0.5 collective-permute-done.refs_4_
  16.0 0.0 collective-permute-done.1.refs_5_
  16.1 0.0 copy-done
  16.1 0.0 copy-done.3
  16.1 0.1 copy-done.4
  16.1 0.0 copy-start.2
  16.1 5.1 %shard_map.69 = (f32[128,1024]{1,0:T(8,128)}, f32[64,256]{1,0:T(8,128)S(1)}) custom-call(s32[2]{0:T(128)S(1)} %pad_add_fusion.refs_0_.place_ref, f32[128,1024]{1,0:T(8,128)S(1)} %bitcast.6, f32[8,64,256]{2,1,0:T(8,128)} %get-tuple-element.28.refs_2_, f32[8,5]{1,0:T(8,128)S(1)} %bitcast.14, f32[8,8,1024]{2,1,0:T(8,128)S(1)} %collective-permute-done.refs_4_, ...), custom_call_target="tpu_custom_call" | custom-call | flops 99999997952 | bytes 2097320 | tf_op jit(solution)/shard_map/pallas_call | solution.py:443
  21.2 0.0 copy-done.2
  21.2 0.0 copy-start.1
  21.2 1.3 %shard_map.70 = (f32[64,512]{1,0:T(8,128)S(1)}, bf16[2,128,192]{2,1,0:T(8,128)(2,1)S(1)}, bf16[1,2,160,128]{3,2,1,0:T(8,128)(2,1)S(1)}, bf16[64,1024]{1,0:T(8,12...) custom-call(s32[2]{0:T(128)S(1)} %pad_add_fusion.refs_0_.place_ref, ...), custom_call_target="tpu_custom_call" | custom-call | flops 1000000000 | bytes 540840 | tf_op jit(solution)/shard_map/pallas_call | solution.py:443
  22.5 1.4 %collective-permute-start.2 = (bf16[64,1024]{1,0:T(8,128)(2,1)S(1)}, bf16[64,1024]{1,0:T(8,128)(2,1)S(1)}, u32[]{:S(2)}, u32[]{:S(2)}) collective-permute-start(bf16[64,1024]{1,0:T(8,128)(2,1)S(1)} %get-tuple-element.35), channel_id=1, source_target_pairs={{0,64},{64,128},{128,192},{192,0},{1,65},{65,129},{129,193},{193,1... | collective-permute-start | bytes 393224 | tf_op jit(solution)/shard_map/ppermute | solution.py:526
  23.9 2.6 %collective-permute-start.3 = (bf16[64,1024]{1,0:T(8,128)(2,1)S(1)}, bf16[64,1024]{1,0:T(8,128)(2,1)S(1)}, u32[]{:S(2)}, u32[]{:S(2)}) collective-permute-start(bf16[64,1024]{1,0:T(8,128)(2,1)S(1)} %get-tuple-element.36), channel_id=1, source_target_pairs={{0,128},{64,192},{128,0},{192,64},{1,129},{65,193},{129,1},{193,65... | collective-permute-start | bytes 393224 | tf_op jit(solution)/shard_map/ppermute | solution.py:526
  26.5 1.1 collective-permute-start.4
  27.6 0.4 collective-permute-done.2.refs_1_.refs_9_
  28.0 3.0 %collective-permute-done.3.refs_2_.refs_10_ = bf16[64,1024]{1,0:T(8,128)(2,1)S(1)} collective-permute-done((bf16[64,1024]{1,0:T(8,128)(2,1)S(1)}, bf16[64,1024]{1,0:T(8,128)(2,1)S(1)}, u32[]{:S(2)}, u32[]{:S(2)}) %collective-permute-start.3) | collective-permute-done | bytes 131104 | tf_op jit(solution)/shard_map/ppermute | solution.py:526
  31.0 0.9 collective-permute-done.4.refs_3_.refs_11_
  31.9 0.0 all-to-all-done.c_ref
  31.9 0.0 copy-done.1
  31.9 2.1 %shard_map.71 = f32[32,32,128]{2,1,0:T(8,128)S(1)} custom-call(bf16[256,1024]{1,0:T(8,128)(2,1)S(1)} %bitcast.13, f32[128,1024]{1,0:T(8,128)} %get-tuple-element.38.fine_hbm, f32[64,256]{1,0:T(8,128)S(1)} %get-tuple-element.39.mean_ref, f32[8,64,256]{2,1,0:T(8,128)S(1)} %all-to-all-done.c_ref, f32[64,512]{1,0:T(8,128)S(1)} %get-tuple-element.40.mix_ref, ...), custom_call_target="tpu_custom_call" | custom-call | flops 1000000000 | bytes 2031616 | tf_op jit(solution)/shard_map/pallas_call | solution.py:443
  34.0 20.4 %all_to_all.30.arrived_ref = f32[32,32,128]{2,1,0:T(8,128)S(1)} all-to-all(f32[32,32,128]{2,1,0:T(8,128)S(1)} %shard_map.71), channel_id=1, replica_groups=mesh['mem_0'=4,'mem_1'=4,'mem_2'=2,'tile'=8] {'mem_0','mem_1','mem_2'}, dimensions={0} | all-to-all | bytes 1048576 | tf_op jit(solution)/shard_map/all_to_all | solution.py:455
  54.5 0.6 shard_map.72
  55.1 8.1 %all_to_all.31.v_ref.refs_2_ = f32[8,32,128]{2,1,0:T(8,128)S(1)} all-to-all(f32[8,32,128]{2,1,0:T(8,128)S(1)} %shard_map.72), channel_id=1, replica_groups=mesh['mem_0'=4,'mem_1'=4,'mem_2'=2,'tile'=8] {'mem_1','mem_2'}, dimensions={0} | all-to-all | bytes 262144 | tf_op jit(solution)/shard_map/all_to_all | solution.py:455
  63.2 1.4 %shard_map.73 = (f32[8,8,1024]{2,1,0:T(8,128)S(1)}, f32[8,8,1024]{2,1,0:T(8,128)S(1)}, f32[8,8,256]{2,1,0:T(8,128)}, f32[64,256]{1,0:T(8,128)S(1)}) custom-call(f32[8,32,128]{2,1,0:T(8,128)S(1)} %all_to_all.31.v_ref.refs_2_, bf16[64,1024]{1,0:T(8,128)(2,1)S(1)} %get-tuple-element.41.refs_0_.refs_8_, ...), custom_call_target="tpu_custom_call" | custom-call | flops 1000000000 | bytes 655360 | tf_op jit(solution)/shard_map/pallas_call | solution.py:443
  64.5 0.9 collective-permute-start.5
  65.4 1.8 %collective-permute-start.6 = (f32[8,8,1024]{2,1,0:T(8,128)S(1)}, f32[8,8,1024]{2,1,0:T(8,128)S(1)}, u32[]{:S(2)}, u32[]{:S(2)}) collective-permute-start(f32[8,8,1024]{2,1,0:T(8,128)S(1)} %get-tuple-element.47), channel_id=1, source_target_pairs={{1,0},{2,1},{3,2},{4,3},{5,4},{6,5},{7,6},{0,7},{9,8},{10,9},{11,1... | collective-permute-start | bytes 786440 | tf_op jit(solution)/shard_map/ppermute | solution.py:472
  67.2 6.0 %all-to-all-start.3 = ((f32[8,8,256]{2,1,0:T(8,128)}), f32[8,8,256]{2,1,0:T(8,128)S(1)}, u32[]{:S(2)}, u32[]{:S(2)}) async-start(f32[8,8,256]{2,1,0:T(8,128)} %get-tuple-element.52), calls=%async_computation.3 | async-start | bytes 131072 | tf_op jit(solution)/shard_map/all_to_all | solution.py:455
  73.3 0.0 collective-permute-done.5.refs_4_
  73.3 0.0 collective-permute-done.6.refs_5_
  73.3 3.5 %shard_map.74 = (f32[32,1024]{1,0:T(8,128)S(1)}, f32[64,256]{1,0:T(8,128)S(1)}, f32[8,128]{1,0:T(8,128)S(1)}) custom-call(s32[2]{0:T(128)S(1)} %pad_add_fusion.refs_0_.place_ref, f32[128,1024]{1,0:T(8,128)S(1)} %bitcast.8, f32[8,32,128]{2,1,0:T(8,128)S(1)} %all_to_all.31.v_ref.refs_2_, f32[64,256]{1,0:T(8,128)S(1)} %get-tuple-element.45.refs_3_, ...), custom_call_target="tpu_custom_call" | custom-call | flops 99999997952 | bytes 1949704 | tf_op jit(solution)/shard_map/pallas_call | solution.py:443
  76.8 3.8 %all-to-all-done.3.c_ref = f32[8,8,256]{2,1,0:T(8,128)S(1)} async-done(((f32[8,8,256]{2,1,0:T(8,128)}), f32[8,8,256]{2,1,0:T(8,128)S(1)}, u32[]{:S(2)}, u32[]{:S(2)}) %all-to-all-start.3) | async-done | bytes 65568 | tf_op jit(solution)/shard_map/all_to_all | solution.py:455
  80.6 0.6 shard_map.75
  81.2 10.3 %all_to_all.32.smoothed_ref = f32[8,24,128]{2,1,0:T(8,128)S(1)} all-to-all(f32[8,24,128]{2,1,0:T(8,128)S(1)} %shard_map.75), channel_id=1, replica_groups=mesh['mem_0'=4,'mem_1'=4,'mem_2'=2,'tile'=8] {'tile'}, dimensions={0} | all-to-all | bytes 196608 | tf_op jit(solution)/shard_map/all_to_all | solution.py:455
  91.5 1.2 %shard_map.76 = f32[32,16,128]{2,1,0:T(8,128)S(1)} custom-call(s32[2]{0:T(128)S(1)} %pad_add_fusion.refs_0_.place_ref, f32[32,1024]{1,0:T(8,128)S(1)} %get-tuple-element.50.fine_ref, f32[64,256]{1,0:T(8,128)S(1)} %get-tuple-element.51.mean_ref, f32[8,24,128]{2,1,0:T(8,128)S(1)} %all_to_all.32.smoothed_ref, f32[8,32,128]{2,1,0:T(8,128)S(1)} %all_to_all.31.v_ref.refs_2_, ...), custom_call_target="tpu_custom_call" | custom-call | flops 1000000000 | bytes 950280 | tf_op jit(solution)/shard_map/pallas_call | solution.py:443
  92.7 15.6 %all_to_all.33.arrived_ref = f32[32,16,128]{2,1,0:T(8,128)S(1)} all-to-all(f32[32,16,128]{2,1,0:T(8,128)S(1)} %shard_map.76), channel_id=1, replica_groups=mesh['mem_0'=4,'mem_1'=4,'mem_2'=2,'tile'=8] {'mem_0','mem_1','mem_2'}, dimensions={0} | all-to-all | bytes 524288 | tf_op jit(solution)/shard_map/all_to_all | solution.py:455
  108.3 1.5 %shard_map.77 = (f32[4,32,32]{2,1,0:T(8,128)}, f32[4,32,32]{2,1,0:T(8,128)}) custom-call(s32[2]{0:T(128)S(1)} %pad_add_fusion.refs_0_.place_ref, f32[32,16,128]{2,1,0:T(8,128)S(1)} %all_to_all.33.arrived_ref, f32[128,1024]{1,0:T(8,128)S(1)} %bitcast.9), custom_call_target="tpu_custom_call" | custom-call | flops 1000000 | bytes 786440 | tf_op jit(solution)/shard_map/pallas_call | solution.py:443
Async XLA Ops:
  3.5 12.5 %collective-permute-start = (f32[8,8,1024]{2,1,0:T(8,128)S(1)}, f32[8,8,1024]{2,1,0:T(8,128)S(1)}, u32[]{:S(2)}, u32[]{:S(2)}) collective-permute-start(f32[8,8,1024]{2,1,0:T(8,128)S(1)} %get-tuple-element.29), channel_id=1, source_target_pairs={{0,1},{1,2},{2,3},{3,4},{4,5},{5,6},{6,7},{7,0},{8,9},{9,10},{10,1... | collective-permute-start | bytes 786440 | tf_op jit(solution)/shard_map/ppermute | solution.py:472
  6.1 10.0 %collective-permute-start.1 = (f32[8,8,1024]{2,1,0:T(8,128)S(1)}, f32[8,8,1024]{2,1,0:T(8,128)S(1)}, u32[]{:S(2)}, u32[]{:S(2)}) collective-permute-start(f32[8,8,1024]{2,1,0:T(8,128)S(1)} %get-tuple-element.30), channel_id=1, source_target_pairs={{1,0},{2,1},{3,2},{4,3},{5,4},{6,5},{7,6},{0,7},{9,8},{10,9},{11,1... | collective-permute-start | bytes 786440 | tf_op jit(solution)/shard_map/ppermute | solution.py:472
  10.1 5.9 %copy-start = (f32[4,32,1024]{2,1,0:T(8,128)S(1)}, f32[4,32,1024]{2,1,0:T(8,128)}, u32[]{:S(2)}) copy-start(f32[4,32,1024]{2,1,0:T(8,128)} %param.6) | copy-start | bytes 1572868
  10.1 5.9 %copy-start.3 = (bf16[2,4,32,1024]{3,2,1,0:T(8,128)(2,1)S(1)}, bf16[2,4,32,1024]{3,2,1,0:T(8,128)(2,1)}, u32[]{:S(2)}) copy-start(bf16[2,4,32,1024]{3,2,1,0:T(8,128)(2,1)} %param.5) | copy-start | bytes 1572868
  10.1 21.8 %all-to-all-start = ((f32[8,64,256]{2,1,0:T(8,128)}), f32[8,64,256]{2,1,0:T(8,128)S(1)}, u32[]{:S(2)}, u32[]{:S(2)}) async-start(f32[8,64,256]{2,1,0:T(8,128)} %get-tuple-element.28.refs_2_), calls=%async_computation | async-start | bytes 1048576 | tf_op jit(solution)/shard_map/all_to_all | solution.py:455
  15.4 0.7 copy-start.4
  16.1 5.1 %copy-start.2 = (f32[64,64]{1,0:T(8,128)S(1)}, f32[64,64]{1,0:T(8,128)}, u32[]{:S(2)}) copy-start(f32[64,64]{1,0:T(8,128)} %lat_ref.3) | copy-start | bytes 49156
  21.2 10.7 %copy-start.1 = (f32[256,256]{1,0:T(8,128)S(1)}, f32[256,256]{1,0:T(8,128)}, u32[]{:S(2)}) copy-start(f32[256,256]{1,0:T(8,128)} %lon_ref.3) | copy-start | bytes 786436
  22.5 5.5 %collective-permute-start.2 = (bf16[64,1024]{1,0:T(8,128)(2,1)S(1)}, bf16[64,1024]{1,0:T(8,128)(2,1)S(1)}, u32[]{:S(2)}, u32[]{:S(2)}) collective-permute-start(bf16[64,1024]{1,0:T(8,128)(2,1)S(1)} %get-tuple-element.35), channel_id=1, source_target_pairs={{0,64},{64,128},{128,192},{192,0},{1,65},{65,129},{129,193},{193,1... | collective-permute-start | bytes 393224 | tf_op jit(solution)/shard_map/ppermute | solution.py:526
  23.9 7.1 %collective-permute-start.3 = (bf16[64,1024]{1,0:T(8,128)(2,1)S(1)}, bf16[64,1024]{1,0:T(8,128)(2,1)S(1)}, u32[]{:S(2)}, u32[]{:S(2)}) collective-permute-start(bf16[64,1024]{1,0:T(8,128)(2,1)S(1)} %get-tuple-element.36), channel_id=1, source_target_pairs={{0,128},{64,192},{128,0},{192,64},{1,129},{65,193},{129,1},{193,65... | collective-permute-start | bytes 393224 | tf_op jit(solution)/shard_map/ppermute | solution.py:526
  26.5 5.4 %collective-permute-start.4 = (bf16[64,1024]{1,0:T(8,128)(2,1)S(1)}, bf16[64,1024]{1,0:T(8,128)(2,1)S(1)}, u32[]{:S(2)}, u32[]{:S(2)}) collective-permute-start(bf16[64,1024]{1,0:T(8,128)(2,1)S(1)} %get-tuple-element.37), channel_id=1, source_target_pairs={{0,192},{64,0},{128,64},{192,128},{1,193},{65,1},{129,65},{193,129... | collective-permute-start | bytes 393224 | tf_op jit(solution)/shard_map/ppermute | solution.py:526
  64.5 8.7 %collective-permute-start.5 = (f32[8,8,1024]{2,1,0:T(8,128)S(1)}, f32[8,8,1024]{2,1,0:T(8,128)S(1)}, u32[]{:S(2)}, u32[]{:S(2)}) collective-permute-start(f32[8,8,1024]{2,1,0:T(8,128)S(1)} %get-tuple-element.46), channel_id=1, source_target_pairs={{0,1},{1,2},{2,3},{3,4},{4,5},{5,6},{6,7},{7,0},{8,9},{9,10},{10,1... | collective-permute-start | bytes 786440 | tf_op jit(solution)/shard_map/ppermute | solution.py:472
  65.4 7.9 %collective-permute-start.6 = (f32[8,8,1024]{2,1,0:T(8,128)S(1)}, f32[8,8,1024]{2,1,0:T(8,128)S(1)}, u32[]{:S(2)}, u32[]{:S(2)}) collective-permute-start(f32[8,8,1024]{2,1,0:T(8,128)S(1)} %get-tuple-element.47), channel_id=1, source_target_pairs={{1,0},{2,1},{3,2},{4,3},{5,4},{6,5},{7,6},{0,7},{9,8},{10,9},{11,1... | collective-permute-start | bytes 786440 | tf_op jit(solution)/shard_map/ppermute | solution.py:472
  67.2 13.4 %all-to-all-start.3 = ((f32[8,8,256]{2,1,0:T(8,128)}), f32[8,8,256]{2,1,0:T(8,128)S(1)}, u32[]{:S(2)}, u32[]{:S(2)}) async-start(f32[8,8,256]{2,1,0:T(8,128)} %get-tuple-element.52), calls=%async_computation.3 | async-start | bytes 131072 | tf_op jit(solution)/shard_map/all_to_all | solution.py:455

commit v4 on v3

--- a/solution.py
+++ b/solution.py
@@ -172,6 +172,14 @@
     return jnp.concatenate([rest, left, middle, right, rest], axis=0)
 
 
+def own_tile():
+    return lax.axis_index("tile")
+
+
+def own_group():
+    return 8 * lax.axis_index("mem_0") + 2 * lax.axis_index("mem_1") + lax.axis_index("mem_2")
+
+
 def taps_of(taps_ref):
     taps = taps_ref[...]
     square = taps * taps
@@ -196,9 +204,9 @@
             band_ref[level, kind] = piece
 
 
-def table_kernel(place_ref, taps_ref, lat_ref, x_ref, *refs):
+def table_kernel(taps_ref, lat_ref, x_ref, *refs):
     mix_ref, rows_ref, band_ref, *x_next_refs = refs
-    tile, own = place_ref[0], place_ref[1] >> 3
+    tile, own = own_tile(), lax.axis_index("mem_0")
 
     def picked(values):
         value = values[3]
@@ -256,14 +264,13 @@
 
 def fine_kernel(last, *refs):
     if last:
-        place_ref, r_ref, *refs = refs
-        v_ref, c_ref, *refs = refs
+        r_ref, v_ref, c_ref, *refs = refs
     else:
-        *refs, fine_ref, c_ref, rows_ref, band_ref, sems = refs
-        place_ref, v_ref, c_hbm, taps_ref, *refs = refs
-        loading = pltpu.make_async_copy(c_hbm.at[0], c_ref, sems.at[0])
-        loading.start()
-        fill_tables(*taps_of(taps_ref), place_ref[0], rows_ref, band_ref)
+        *refs, f_ref, c_ref, rows_ref, band_ref, sem = refs
+        v_ref, c_hbm, taps_ref, *refs = refs
+        load = pltpu.make_async_copy(c_hbm.at[0], c_ref, sem)
+        load.start()
+        fill_tables(*taps_of(taps_ref), own_tile(), rows_ref, band_ref)
     before_ref, after_ref, *refs = refs
     if last:
         rows_ref, band_ref, *refs = refs
@@ -273,9 +280,9 @@
         fine_ref, mean_ref, sums_ref, f_ref = refs
         v = natural(v_ref)
     else:
-        fine_hbm, mean_ref, f_ref = refs
+        fine_ref, mean_ref = refs
         v = v_ref[...]
-        loading.wait()
+        load.wait()
     d = x.astype(F32) * for_each(v) - prolong(c_ref[...])
     highs, lows = [], []
     for part in range(2):
@@ -306,15 +313,10 @@
                     term = x[row : row + ROWS, lanes].astype(F32) * f
                     summed = term if summed is None else summed + term
             fine_ref[ROWS * level : ROWS * level + ROWS, lanes] = summed
-    if not last:
-        copy = pltpu.make_async_copy(fine_ref, fine_hbm, sems.at[1])
-        copy.start()
     means = block_mean(f_ref[...], split2)
     mean_ref[...] = means
-    if not last:
-        copy.wait()
-    else:
-        own = place_ref[1] >> 3
+    if last:
+        own = lax.axis_index("mem_0")
         r = r_ref[pl.ds(pl.multiple_of(ROWS * own, ROWS), ROWS), :]
         products = total(v * fine_ref[...]) - 16.0 * total(c_ref[...] * means)
         sums_ref[...] = lane_sums(
@@ -339,13 +341,9 @@
     return functools.reduce(jnp.add, pieces, fine_ref[...])
 
 
-def partial_kernel(x_ref, fine_hbm, mean_ref, c_ref, mix_ref, lon_ref, out_ref, fine_ref, sem):
-    copy = pltpu.make_async_copy(fine_hbm, fine_ref, sem)
-    copy.start()
+def partial_kernel(x_ref, fine_ref, mean_ref, c_ref, mix_ref, lon_ref, out_ref):
     across = exact_mm(mix_ref[...], c_ref[...].reshape(512, 256))
-    smoothed = exact_mm(across, lon_ref[...]) - mean_ref[...]
-    copy.wait()
-    p = blended(x_ref[...], fine_ref, smoothed)
+    p = blended(x_ref[...], fine_ref, exact_mm(across, lon_ref[...]) - mean_ref[...])
     for tall in range(16):
         for wide in range(8):
             out_ref[2 * tall + wide // 4, 8 * (wide % 4) : 8 * (wide % 4) + 8, :] = p[
@@ -367,7 +365,7 @@
     return shares
 
 
-def last_partial_kernel(place_ref, fine_ref, mean_ref, smoothed_ref, v_ref, *refs):
+def last_partial_kernel(fine_ref, mean_ref, smoothed_ref, v_ref, *refs):
     *x_refs, out_ref, v_packed = refs
     halves = [smoothed_ref[:, 8 * k : 8 * k + 8, :].reshape(64, 128) for k in range(2)]
     p = blended(members_of(x_refs), fine_ref, jnp.concatenate(halves, axis=1) - mean_ref[...])
@@ -377,14 +375,14 @@
     for group, share in enumerate(packed(natural(v_ref))):
         v_packed[group] = share
     i, j = iotas(8, 128)
-    mine = pl.ds(place_ref[1] & 7, 1)
+    mine = pl.ds(own_group() & 7, 1)
     for group in range(GROUPS):
         row = jnp.broadcast_to(v_packed[group, mine, :], (8, 128))
         out_ref[group, 8:16, :] = jnp.where(i == 1, row, sums)
 
 
-def share_kernel(scale, place_ref, arrived_ref, r_ref, out_ref):
-    group = place_ref[1]
+def share_kernel(scale, arrived_ref, r_ref, out_ref):
+    group = own_group()
     share = r_ref[
         pl.ds(pl.multiple_of(8 * (group >> 1), 8), 8),
         pl.ds(pl.multiple_of(512 * (group & 1), 512), 512),
@@ -395,8 +393,8 @@
         out_ref[other] = share
 
 
-def final_kernel(scale, place_ref, arrived_ref, r_ref, x_out, res_out):
-    group = place_ref[1]
+def final_kernel(scale, arrived_ref, r_ref, x_out, res_out):
+    group = own_group()
     lanes = pl.ds(pl.multiple_of(128 * (group >> 2), 128), 128)
     i, j = iotas(8, 128)
     sums = jnp.sum(arrived_ref[:, 8:16, :], axis=0)
@@ -425,7 +423,6 @@
 
 
 VMEM = pl.BlockSpec(memory_space=pltpu.VMEM)
-SMEM = pl.BlockSpec(memory_space=pltpu.SMEM)
 HBM = pl.BlockSpec(memory_space=pltpu.HBM)
 
 
@@ -459,7 +456,6 @@
     count, levels, height, extent = perturbations.shape
     members = count * lax.axis_size(MEM)
     scale = 1.0 / (members - 1)
-    place = jnp.stack([lax.axis_index("tile"), lax.axis_index(MEM)]).astype(jnp.int32)
     x = perturbations.reshape(count * levels * height, extent)
     r = right_side.reshape(levels * height, extent)
     half = ((128, LON), F32)
@@ -472,6 +468,8 @@
         return lax.ppermute(bottom, "tile", up), lax.ppermute(top, "tile", down)
 
     own = ((64, 256), F32)
+    taps = fine_taps.reshape(2 * levels, 5)
+    rows_shape, band_shape = (2, 128, 192), (2, 160, 128)
     top, bottom, c = call(
         first_detail_kernel,
         [edge, edge, ((TILES, 64, 256), F32)],
@@ -486,28 +484,9 @@
             pltpu.SemaphoreType.DMA((8,)),
         ),
     )
+    before, after = edges(top, bottom)
     c_first = exchange(c, "tile")
-    taps = fine_taps.reshape(2 * levels, 5)
-    rows_shape, band_shape = (2, 128, 192), (2, 160, 128)
-    fine_scratch = [pltpu.VMEM((256, LON), F32)]
-    fine, means = call(
-        functools.partial(fine_kernel, False),
-        [half, own],
-        [SMEM, VMEM, HBM] + [VMEM] * 4,
-        (place, r, c, taps, *edges(top, bottom), x),
-        10**11,
-        16,
-        scratch=[
-            *fine_scratch,
-            pltpu.VMEM(*half),
-            pltpu.VMEM(*own),
-            pltpu.VMEM(rows_shape, BF16),
-            pltpu.VMEM((levels, *band_shape), BF16),
-            pltpu.SemaphoreType.DMA((2,)),
-        ],
-        out_specs=[HBM, VMEM],
-    )
-    means, x_again = lax.optimization_barrier((means, x))
+    before, x_again = lax.optimization_barrier((before, x))
     mix, rows_next, band_next, *x_next = call(
         table_kernel,
         [
@@ -516,30 +495,46 @@
             ((1, *band_shape), BF16),
             *[((count * height, extent), BF16)] * 4,
         ],
-        [SMEM] + [VMEM] * 3,
-        (place, taps, coarse_lat, x_again),
-        10**9,
+        [VMEM] * 3,
+        (taps, coarse_lat, x_again),
+        10**11,
         6,
     )
+    before, mix = lax.optimization_barrier((before, mix))
     for ahead in range(1, 4):
         ring = [(i, (i + ahead) % 4) for i in range(4)]
         x_next[ahead] = lax.ppermute(x_next[ahead], "mem_0", ring)
+    fine_scratch = [pltpu.VMEM((256, LON), F32)]
+    fine, means = call(
+        functools.partial(fine_kernel, False),
+        [half, own],
+        [VMEM, HBM] + [VMEM] * 4,
+        (r, c, taps, before, after, x),
+        10**11,
+        16,
+        scratch=[
+            *fine_scratch,
+            pltpu.VMEM(*own),
+            pltpu.VMEM(rows_shape, BF16),
+            pltpu.VMEM((levels, *band_shape), BF16),
+            pltpu.SemaphoreType.DMA,
+        ],
+    )
     fine, x_next = lax.optimization_barrier((fine, x_next))
     shares = call(
         partial_kernel,
         [shared],
-        [VMEM, HBM] + [VMEM] * 4,
+        [VMEM] * 6,
         (x, fine, means, c_first, mix, coarse_lon),
         10**9,
         12,
-        scratch=[pltpu.VMEM(*half), pltpu.SemaphoreType.DMA],
     )
     arrived = exchange(shares, MEM)
     share = call(
         functools.partial(share_kernel, scale),
         [((TILES, 32, 128), F32)],
-        [SMEM, VMEM, VMEM],
-        (place, arrived, r),
+        [VMEM, VMEM],
+        (arrived, r),
         10**6,
         6,
     )
@@ -559,8 +554,8 @@
     fine, means, sums = call(
         functools.partial(fine_kernel, True),
         [level, own, ((8, 128), F32)],
-        [SMEM] + [VMEM] * 11,
-        (place, r, a, c_own, *beside, rows_next, band_next, *x_next),
+        [VMEM] * 11,
+        (r, a, c_own, *beside, rows_next, band_next, *x_next),
         10**11,
         16,
         scratch=fine_scratch,
@@ -577,8 +572,8 @@
     shares = call(
         last_partial_kernel,
         [((GROUPS, 16, 128), F32)],
-        [SMEM] + [VMEM] * 8,
-        (place, fine, means, smoothed, a, *x_next),
+        [VMEM] * 8,
+        (fine, means, smoothed, a, *x_next),
         10**9,
         12,
         scratch=[pltpu.VMEM((GROUPS, 8, 128), F32)],
@@ -589,8 +584,8 @@
         call(
             functools.partial(final_kernel, scale),
             [out, out],
-            [SMEM, VMEM, VMEM],
-            (place, arrived, r),
+            [VMEM, VMEM],
+            (arrived, r),
             10**6,
             6,
         )

time: 110 us -> 106 us (0.964)
  Pallas kernels: 20.2 us -> 17 us
  starting transfers between devices: 25.7 us -> 23.2 us
  waiting for transfers between devices: 8.62 us -> 10.4 us
    ppermute x3, waiting for transfers between devices: 4.32 us -> 0.32 us  [local(): x_next[ahead] = lax.ppermute(x_next[ahead], 'mem_0', ring)]
    all_to_all x2, waiting for transfers between devices: 3.77 us -> 7.55 us  [exchange(): return lax.all_to_all(blocks, axis, 0, 0, tiled=True)]
    pallas_call x10, Pallas kernels: 20.2 us -> 17 us  [call(): pl.pallas_call(kernel, out_shape=shapes if len(shapes) > 1 else shapes[0]...]
    all_to_all x2, starting transfers between devices: 11.4 us -> 8.86 us  [exchange(): return lax.all_to_all(blocks, axis, 0, 0, tiled=True)]
    ppermute x4, waiting for transfers between devices: 0.53 us -> 2.56 us  [edges(): return (lax.ppermute(bottom, 'tile', up), lax.ppermute(top, 'tile', down))]
  transfers between devices with their start and end apart: 9 -> 9, of which waited for: 5 -> 5; matrix products, arithmetic and copies ran while one was open for 0% -> 0% of each run, Pallas kernels for 9% -> 7%
where the time goes in v4:
time: 106 us
  blocking collectives  54.2 us (51%)
  starting transfers between devices  23.2 us (22%)
  Pallas kernels  17 us (16%)
  waiting for transfers between devices  10.4 us (10%)
    all_to_all x4, blocking collectives, exchange(): return lax.all_to_all(blocks, axis, 0, 0, tiled=True)  54.2 us
    pallas_call x10, Pallas kernels, call(): pl.pallas_call(kernel, out_shape=shapes if len(shapes) > 1 else shapes[0]...  17 us
    ppermute x4, starting transfers between devices, edges(): return (lax.ppermute(bottom, 'tile', up), lax.ppermute(top, 'tile', down))  9.25 us
    all_to_all x2, starting transfers between devices, exchange(): return lax.all_to_all(blocks, axis, 0, 0, tiled=True)  8.86 us
    all_to_all x2, waiting for transfers between devices, exchange(): return lax.all_to_all(blocks, axis, 0, 0, tiled=True)  7.55 us
    ppermute x3, starting transfers between devices, local(): x_next[ahead] = lax.ppermute(x_next[ahead], 'mem_0', ring)  5.06 us
    ppermute x4, waiting for transfers between devices, edges(): return (lax.ppermute(bottom, 'tile', up), lax.ppermute(top, 'tile', down))  2.56 us
  transfers between devices with their start and end apart: 9, of which 5 were waited for; matrix products, arithmetic and copies ran while one was open for 0% of the time, Pallas kernels for 7%

profile of v4, /device:TPU:1, one launch (start us, length us, event | category | flops | bytes accessed | tf_op | source)
XLA Modules:
  0.0 105.6 jit_solution(7384190592632856782)
XLA Ops:
  0.6 2.9 %shard_map.68 = (f32[8,8,1024]{2,1,0:T(8,128)S(1)}, f32[8,8,1024]{2,1,0:T(8,128)S(1)}, f32[8,64,256]{2,1,0:T(8,128)}) custom-call(bf16[256,1024]{1,0:T(8,128)(2,1)} %bitcast.8, f32[128,1024]{1,0:T(8,128)} %bitcast.3), custom_call_target="tpu_custom_call" | custom-call | flops 1000000000 | bytes 1048576 | tf_op jit(solution)/shard_map/pallas_call | solution.py:440
  3.5 2.5 %collective-permute-start = (f32[8,8,1024]{2,1,0:T(8,128)S(1)}, f32[8,8,1024]{2,1,0:T(8,128)S(1)}, u32[]{:S(2)}, u32[]{:S(2)}) collective-permute-start(f32[8,8,1024]{2,1,0:T(8,128)S(1)} %get-tuple-element.31), channel_id=1, source_target_pairs={{0,1},{1,2},{2,3},{3,4},{4,5},{5,6},{6,7},{7,0},{8,9},{9,10},{10,1... | collective-permute-start | bytes 786440 | tf_op jit(solution)/shard_map/ppermute | solution.py:468
  6.1 4.0 %collective-permute-start.1 = (f32[8,8,1024]{2,1,0:T(8,128)S(1)}, f32[8,8,1024]{2,1,0:T(8,128)S(1)}, u32[]{:S(2)}, u32[]{:S(2)}) collective-permute-start(f32[8,8,1024]{2,1,0:T(8,128)S(1)} %get-tuple-element.36), channel_id=1, source_target_pairs={{1,0},{2,1},{3,2},{4,3},{5,4},{6,5},{7,6},{0,7},{9,8},{10,9},{11,1... | collective-permute-start | bytes 786440 | tf_op jit(solution)/shard_map/ppermute | solution.py:468
  10.1 0.0 copy-start.2
  10.1 0.0 copy-start.4
  10.1 0.0 copy-start.5
  10.1 5.3 %all-to-all-start = ((f32[8,64,256]{2,1,0:T(8,128)}), f32[8,64,256]{2,1,0:T(8,128)}, u32[]{:S(2)}, u32[]{:S(2)}) async-start(f32[8,64,256]{2,1,0:T(8,128)} %get-tuple-element.30.refs_1_), calls=%async_computation | async-start | bytes 1048576 | tf_op jit(solution)/shard_map/all_to_all | solution.py:452
  15.4 0.6 collective-permute-done.refs_3_
  16.0 0.0 copy-done.2
  16.0 0.0 copy-done.4
  16.0 0.0 copy-done.5
  16.1 0.0 copy-start
  16.1 0.7 shard_map.69
  16.8 1.4 %collective-permute-start.2 = (bf16[64,1024]{1,0:T(8,128)(2,1)S(1)}, bf16[64,1024]{1,0:T(8,128)(2,1)S(1)}, u32[]{:S(2)}, u32[]{:S(2)}) collective-permute-start(bf16[64,1024]{1,0:T(8,128)(2,1)S(1)} %get-tuple-element.39), channel_id=1, source_target_pairs={{0,64},{64,128},{128,192},{192,0},{1,65},{65,129},{129,193},{193,1... | collective-permute-start | bytes 393224 | tf_op jit(solution)/shard_map/ppermute | solution.py:506
  18.2 2.6 %collective-permute-start.3 = (bf16[64,1024]{1,0:T(8,128)(2,1)S(1)}, bf16[64,1024]{1,0:T(8,128)(2,1)S(1)}, u32[]{:S(2)}, u32[]{:S(2)}) collective-permute-start(bf16[64,1024]{1,0:T(8,128)(2,1)S(1)} %get-tuple-element.40), channel_id=1, source_target_pairs={{0,128},{64,192},{128,0},{192,64},{1,129},{65,193},{129,1},{193,65... | collective-permute-start | bytes 393224 | tf_op jit(solution)/shard_map/ppermute | solution.py:506
  20.8 0.0 copy-start.1
  20.8 1.1 %collective-permute-start.4 = (bf16[64,1024]{1,0:T(8,128)(2,1)S(1)}, bf16[64,1024]{1,0:T(8,128)(2,1)S(1)}, u32[]{:S(2)}, u32[]{:S(2)}) collective-permute-start(bf16[64,1024]{1,0:T(8,128)(2,1)S(1)} %get-tuple-element.41), channel_id=1, source_target_pairs={{0,192},{64,0},{128,64},{192,128},{1,193},{65,1},{129,65},{193,129... | collective-permute-start | bytes 393224 | tf_op jit(solution)/shard_map/ppermute | solution.py:506
  21.9 0.0 collective-permute-done.1.refs_4_
  21.9 0.0 copy-done
  21.9 4.2 %shard_map.70 = (f32[128,1024]{1,0:T(8,128)S(1)}, f32[64,256]{1,0:T(8,128)S(1)}) custom-call(f32[128,1024]{1,0:T(8,128)S(1)} %bitcast.4, f32[8,64,256]{2,1,0:T(8,128)} %get-tuple-element.30.refs_1_, f32[8,5]{1,0:T(8,128)S(1)} %bitcast.13, f32[8,8,1024]{2,1,0:T(8,128)S(1)} %collective-permute-done.refs_3_, f32[8,8,1024]{2,1,0:T(8,128)S(1)} %collective-permute-done.1.refs_4_, ...), custom_call_target="tpu_custom_call" | custom-call | flops 99999997952 | bytes 2097312 | tf_op jit(solution)/shard_map/pallas_call | solution.py:440
  26.1 0.0 collective-permute-done.2.refs_1_.refs_8_
  26.1 0.0 collective-permute-done.3.refs_2_.refs_9_
  26.1 0.3 collective-permute-done.4.refs_3_.refs_10_
  26.4 5.5 %all-to-all-done.c_ref = f32[8,64,256]{2,1,0:T(8,128)} async-done(((f32[8,64,256]{2,1,0:T(8,128)}), f32[8,64,256]{2,1,0:T(8,128)}, u32[]{:S(2)}, u32[]{:S(2)}) %all-to-all-start) | async-done | bytes 524320 | tf_op jit(solution)/shard_map/all_to_all | solution.py:452
  32.0 0.0 copy-done.1
  32.0 2.5 %shard_map.71 = f32[32,32,128]{2,1,0:T(8,128)S(1)} custom-call(bf16[256,1024]{1,0:T(8,128)(2,1)S(1)} %bitcast.11, f32[128,1024]{1,0:T(8,128)S(1)} %get-tuple-element.42.fine_ref, f32[64,256]{1,0:T(8,128)S(1)} %get-tuple-element.43.mean_ref, f32[8,64,256]{2,1,0:T(8,128)} %all-to-all-done.c_ref, f32[64,512]{1,0:T(8,128)S(1)} %get-tuple-element.44.mix_ref, ...), custom_call_target="tpu_custom_call" | custom-call | flops 1000000000 | bytes 2031616 | tf_op jit(solution)/shard_map/pallas_call | solution.py:440
  34.5 20.5 %all_to_all.30.arrived_ref = f32[32,32,128]{2,1,0:T(8,128)S(1)} all-to-all(f32[32,32,128]{2,1,0:T(8,128)S(1)} %shard_map.71), channel_id=1, replica_groups=mesh['mem_0'=4,'mem_1'=4,'mem_2'=2,'tile'=8] {'mem_0','mem_1','mem_2'}, dimensions={0} | all-to-all | bytes 1048576 | tf_op jit(solution)/shard_map/all_to_all | solution.py:452
  55.0 8.1 %all_to_all.31.v_ref.refs_1_ = f32[8,32,128]{2,1,0:T(8,128)S(1)} all-to-all(f32[8,32,128]{2,1,0:T(8,128)S(1)} %shard_map.72), channel_id=1, replica_groups=mesh['mem_0'=4,'mem_1'=4,'mem_2'=2,'tile'=8] {'mem_1','mem_2'}, dimensions={0} | all-to-all | bytes 262144 | tf_op jit(solution)/shard_map/all_to_all | solution.py:452
  63.1 1.4 %shard_map.73 = (f32[8,8,1024]{2,1,0:T(8,128)S(1)}, f32[8,8,1024]{2,1,0:T(8,128)S(1)}, f32[8,8,256]{2,1,0:T(8,128)}, f32[64,256]{1,0:T(8,128)S(1)}) custom-call(f32[8,32,128]{2,1,0:T(8,128)S(1)} %all_to_all.31.v_ref.refs_1_, bf16[64,1024]{1,0:T(8,128)(2,1)S(1)} %get-tuple-element.45.refs_0_.refs_7_, ...), custom_call_target="tpu_custom_call" | custom-call | flops 1000000000 | bytes 655360 | tf_op jit(solution)/shard_map/pallas_call | solution.py:440
  64.5 0.3 collective-permute-start.5
  64.8 2.4 %collective-permute-start.6 = (f32[8,8,1024]{2,1,0:T(8,128)S(1)}, f32[8,8,1024]{2,1,0:T(8,128)S(1)}, u32[]{:S(2)}, u32[]{:S(2)}) collective-permute-start(f32[8,8,1024]{2,1,0:T(8,128)S(1)} %get-tuple-element.51), channel_id=1, source_target_pairs={{1,0},{2,1},{3,2},{4,3},{5,4},{6,5},{7,6},{0,7},{9,8},{10,9},{11,1... | collective-permute-start | bytes 786440 | tf_op jit(solution)/shard_map/ppermute | solution.py:468
  67.2 3.5 %all-to-all-start.3 = ((f32[8,8,256]{2,1,0:T(8,128)}), f32[8,8,256]{2,1,0:T(8,128)S(1)}, u32[]{:S(2)}, u32[]{:S(2)}) async-start(f32[8,8,256]{2,1,0:T(8,128)} %get-tuple-element.56), calls=%async_computation.3 | async-start | bytes 131072 | tf_op jit(solution)/shard_map/all_to_all | solution.py:452
  70.7 1.9 %collective-permute-done.5.refs_3_ = f32[8,8,1024]{2,1,0:T(8,128)S(1)} collective-permute-done((f32[8,8,1024]{2,1,0:T(8,128)S(1)}, f32[8,8,1024]{2,1,0:T(8,128)S(1)}, u32[]{:S(2)}, u32[]{:S(2)}) %collective-permute-start.5) | collective-permute-done | bytes 262176 | tf_op jit(solution)/shard_map/ppermute | solution.py:468
  72.6 0.0 collective-permute-done.6.refs_4_
  72.7 0.0 copy-start.3
  72.7 3.0 %shard_map.74 = (f32[32,1024]{1,0:T(8,128)S(1)}, f32[64,256]{1,0:T(8,128)S(1)}, f32[8,128]{1,0:T(8,128)S(1)}) custom-call(f32[128,1024]{1,0:T(8,128)S(1)} %bitcast.6, f32[8,32,128]{2,1,0:T(8,128)S(1)} %all_to_all.31.v_ref.refs_1_, f32[64,256]{1,0:T(8,128)S(1)} %get-tuple-element.49.refs_2_, f32[8,8,1024]{2,1,0:T(8,128)S(1)} %collective-permute-done.5.refs_3_, ...), custom_call_target="tpu_custom_call" | custom-call | flops 99999997952 | bytes 1949696 | tf_op jit(solution)/shard_map/pallas_call | solution.py:440
  75.7 2.0 %all-to-all-done.3.c_ref = f32[8,8,256]{2,1,0:T(8,128)S(1)} async-done(((f32[8,8,256]{2,1,0:T(8,128)}), f32[8,8,256]{2,1,0:T(8,128)S(1)}, u32[]{:S(2)}, u32[]{:S(2)}) %all-to-all-start.3) | async-done | bytes 65568 | tf_op jit(solution)/shard_map/all_to_all | solution.py:452
  77.7 0.0 copy-done.3
  77.7 0.6 shard_map.75
  78.3 10.0 %all_to_all.32.smoothed_ref = f32[8,24,128]{2,1,0:T(8,128)S(1)} all-to-all(f32[8,24,128]{2,1,0:T(8,128)S(1)} %shard_map.75), channel_id=1, replica_groups=mesh['mem_0'=4,'mem_1'=4,'mem_2'=2,'tile'=8] {'tile'}, dimensions={0} | all-to-all | bytes 196608 | tf_op jit(solution)/shard_map/all_to_all | solution.py:452
  88.2 0.7 shard_map.76
  88.9 15.7 %all_to_all.33.arrived_ref = f32[32,16,128]{2,1,0:T(8,128)S(1)} all-to-all(f32[32,16,128]{2,1,0:T(8,128)S(1)} %shard_map.76), channel_id=1, replica_groups=mesh['mem_0'=4,'mem_1'=4,'mem_2'=2,'tile'=8] {'mem_0','mem_1','mem_2'}, dimensions={0} | all-to-all | bytes 524288 | tf_op jit(solution)/shard_map/all_to_all | solution.py:452
  104.7 0.9 shard_map.77
  (1 shorter events, 0.0 us)
Async XLA Ops:
  3.5 12.5 %collective-permute-start = (f32[8,8,1024]{2,1,0:T(8,128)S(1)}, f32[8,8,1024]{2,1,0:T(8,128)S(1)}, u32[]{:S(2)}, u32[]{:S(2)}) collective-permute-start(f32[8,8,1024]{2,1,0:T(8,128)S(1)} %get-tuple-element.31), channel_id=1, source_target_pairs={{0,1},{1,2},{2,3},{3,4},{4,5},{5,6},{6,7},{7,0},{8,9},{9,10},{10,1... | collective-permute-start | bytes 786440 | tf_op jit(solution)/shard_map/ppermute | solution.py:468
  6.1 15.8 %collective-permute-start.1 = (f32[8,8,1024]{2,1,0:T(8,128)S(1)}, f32[8,8,1024]{2,1,0:T(8,128)S(1)}, u32[]{:S(2)}, u32[]{:S(2)}) collective-permute-start(f32[8,8,1024]{2,1,0:T(8,128)S(1)} %get-tuple-element.36), channel_id=1, source_target_pairs={{1,0},{2,1},{3,2},{4,3},{5,4},{6,5},{7,6},{0,7},{9,8},{10,9},{11,1... | collective-permute-start | bytes 786440 | tf_op jit(solution)/shard_map/ppermute | solution.py:468
  10.1 5.9 %copy-start.2 = (f32[64,64]{1,0:T(8,128)S(1)}, f32[64,64]{1,0:T(8,128)}, u32[]{:S(2)}) copy-start(f32[64,64]{1,0:T(8,128)} %lat_ref.3) | copy-start | bytes 49156
  10.1 5.9 %copy-start.4 = (bf16[2,4,32,1024]{3,2,1,0:T(8,128)(2,1)S(1)}, bf16[2,4,32,1024]{3,2,1,0:T(8,128)(2,1)}, u32[]{:S(2)}) copy-start(bf16[2,4,32,1024]{3,2,1,0:T(8,128)(2,1)} %param.5) | copy-start | bytes 1572868
  10.1 5.9 %copy-start.5 = (f32[2,4,5]{2,1,0:T(4,128)S(1)}, f32[2,4,5]{2,1,0:T(4,128)}, u32[]{:S(2)}) copy-start(f32[2,4,5]{2,1,0:T(4,128)} %param.7) | copy-start | bytes 484
  10.1 21.8 %all-to-all-start = ((f32[8,64,256]{2,1,0:T(8,128)}), f32[8,64,256]{2,1,0:T(8,128)}, u32[]{:S(2)}, u32[]{:S(2)}) async-start(f32[8,64,256]{2,1,0:T(8,128)} %get-tuple-element.30.refs_1_), calls=%async_computation | async-start | bytes 1048576 | tf_op jit(solution)/shard_map/all_to_all | solution.py:452
  16.1 5.8 %copy-start = (f32[4,32,1024]{2,1,0:T(8,128)S(1)}, f32[4,32,1024]{2,1,0:T(8,128)}, u32[]{:S(2)}) copy-start(f32[4,32,1024]{2,1,0:T(8,128)} %param.6) | copy-start | bytes 1572868
  16.8 9.3 %collective-permute-start.2 = (bf16[64,1024]{1,0:T(8,128)(2,1)S(1)}, bf16[64,1024]{1,0:T(8,128)(2,1)S(1)}, u32[]{:S(2)}, u32[]{:S(2)}) collective-permute-start(bf16[64,1024]{1,0:T(8,128)(2,1)S(1)} %get-tuple-element.39), channel_id=1, source_target_pairs={{0,64},{64,128},{128,192},{192,0},{1,65},{65,129},{129,193},{193,1... | collective-permute-start | bytes 393224 | tf_op jit(solution)/shard_map/ppermute | solution.py:506
  18.2 7.9 %collective-permute-start.3 = (bf16[64,1024]{1,0:T(8,128)(2,1)S(1)}, bf16[64,1024]{1,0:T(8,128)(2,1)S(1)}, u32[]{:S(2)}, u32[]{:S(2)}) collective-permute-start(bf16[64,1024]{1,0:T(8,128)(2,1)S(1)} %get-tuple-element.40), channel_id=1, source_target_pairs={{0,128},{64,192},{128,0},{192,64},{1,129},{65,193},{129,1},{193,65... | collective-permute-start | bytes 393224 | tf_op jit(solution)/shard_map/ppermute | solution.py:506
  20.8 11.2 %copy-start.1 = (f32[256,256]{1,0:T(8,128)S(1)}, f32[256,256]{1,0:T(8,128)}, u32[]{:S(2)}) copy-start(f32[256,256]{1,0:T(8,128)} %lon_ref.3) | copy-start | bytes 786436
  20.8 5.6 %collective-permute-start.4 = (bf16[64,1024]{1,0:T(8,128)(2,1)S(1)}, bf16[64,1024]{1,0:T(8,128)(2,1)S(1)}, u32[]{:S(2)}, u32[]{:S(2)}) collective-permute-start(bf16[64,1024]{1,0:T(8,128)(2,1)S(1)} %get-tuple-element.41), channel_id=1, source_target_pairs={{0,192},{64,0},{128,64},{192,128},{1,193},{65,1},{129,65},{193,129... | collective-permute-start | bytes 393224 | tf_op jit(solution)/shard_map/ppermute | solution.py:506
  64.5 8.2 %collective-permute-start.5 = (f32[8,8,1024]{2,1,0:T(8,128)S(1)}, f32[8,8,1024]{2,1,0:T(8,128)S(1)}, u32[]{:S(2)}, u32[]{:S(2)}) collective-permute-start(f32[8,8,1024]{2,1,0:T(8,128)S(1)} %get-tuple-element.50), channel_id=1, source_target_pairs={{0,1},{1,2},{2,3},{3,4},{4,5},{5,6},{6,7},{7,0},{8,9},{9,10},{10,1... | collective-permute-start | bytes 786440 | tf_op jit(solution)/shard_map/ppermute | solution.py:468
  64.8 7.9 %collective-permute-start.6 = (f32[8,8,1024]{2,1,0:T(8,128)S(1)}, f32[8,8,1024]{2,1,0:T(8,128)S(1)}, u32[]{:S(2)}, u32[]{:S(2)}) collective-permute-start(f32[8,8,1024]{2,1,0:T(8,128)S(1)} %get-tuple-element.51), channel_id=1, source_target_pairs={{1,0},{2,1},{3,2},{4,3},{5,4},{6,5},{7,6},{0,7},{9,8},{10,9},{11,1... | collective-permute-start | bytes 786440 | tf_op jit(solution)/shard_map/ppermute | solution.py:468
  67.2 10.5 %all-to-all-start.3 = ((f32[8,8,256]{2,1,0:T(8,128)}), f32[8,8,256]{2,1,0:T(8,128)S(1)}, u32[]{:S(2)}, u32[]{:S(2)}) async-start(f32[8,8,256]{2,1,0:T(8,128)} %get-tuple-element.56), calls=%async_computation.3 | async-start | bytes 131072 | tf_op jit(solution)/shard_map/all_to_all | solution.py:452
  72.7 5.0 %copy-start.3 = (f32[64,64]{1,0:T(8,128)S(1)}, f32[64,64]{1,0:T(8,128)}, u32[]{:S(2)}) copy-start(f32[64,64]{1,0:T(8,128)} %lat_ref.3) | copy-start | bytes 49156

commit v5 on v4

--- a/solution.py
+++ b/solution.py
@@ -29,6 +29,10 @@
     return high, (x - high.astype(F32)).astype(BF16)
 
 
+def mm3(a, b):
+    return mm(a[0], b[0]) + mm(a[0], b[1]) + mm(a[1], b[0])
+
+
 def split3(x):
     high = x.astype(BF16)
     rest = x - high.astype(F32)
@@ -55,10 +59,10 @@
     return jnp.where(hit, 1.0, 0.0).astype(BF16)
 
 
-def block_mean(w, split):
-    table = shrink_table(64, 256, False)
-    part = sum(mm(table, piece) for piece in split(w))
-    stacked = jnp.concatenate([part[:, :512], part[:, 512:]], axis=0)
+def block_mean(halves, split):
+    table = shrink_table(32, 128, False)
+    parts = [sum(mm(table, piece) for piece in split(half)) for half in halves]
+    stacked = jnp.concatenate([part[:, k : k + 512] for k in (0, 512) for part in parts], axis=0)
     table = shrink_table(512, 128, True)
     small = sum(mm(piece, table) for piece in split(stacked))
     return jnp.concatenate([small[:64], small[64:]], axis=1)
@@ -91,35 +95,40 @@
 
 
 def for_each(v):
-    return jnp.concatenate([v] * (256 // v.shape[0]), axis=0)
-
-
-def members_of(refs):
-    return refs[0][...] if len(refs) == 1 else jnp.concatenate([ref[...] for ref in refs], axis=0)
+    return jnp.concatenate([v] * (128 // v.shape[0]), axis=0)
+
+
+def halves_of(refs):
+    if len(refs) == 1:
+        return refs[0][:128], refs[0][128:]
+    return [jnp.concatenate([refs[k][...], refs[k + 1][...]], axis=0) for k in (0, 2)]
 
 
 def detail_kernel(v_ref, *refs):
-    detail(members_of(refs[:4]), natural(v_ref), *refs[4:])
+    v = for_each(natural(v_ref))
+    detail([x.astype(F32) * v for x in halves_of(refs[:4])], *refs[4:])
 
 
 def first_detail_kernel(x_hbm, v_hbm, *refs):
     *out_refs, x_ref, v_ref, x_sems, v_sems = refs
-    copies = []
+    v_copies, x_copies = [], []
     for k in range(8):
         rows = pl.ds(16 * k, 16)
-        copies.append(pltpu.make_async_copy(v_hbm.at[rows], v_ref.at[rows], v_sems.at[k]))
+        v_copies.append(pltpu.make_async_copy(v_hbm.at[rows], v_ref.at[rows], v_sems.at[k]))
         rows = pl.ds(32 * k, 32)
-        copies.append(pltpu.make_async_copy(x_hbm.at[rows], x_ref.at[rows], x_sems.at[k]))
-    for copy in copies:
+        x_copies.append(pltpu.make_async_copy(x_hbm.at[rows], x_ref.at[rows], x_sems.at[k]))
+    for copy in v_copies + x_copies:
         copy.start()
-    for copy in copies:
+    for copy in v_copies + x_copies[:4]:
         copy.wait()
-    detail(x_ref[...], v_ref[...], *out_refs)
-
-
-def detail(x, v, top_ref, bottom_ref, c_ref, own_ref=None):
-    w = x.astype(F32) * for_each(v)
-    c = block_mean(w, split3)
+    first = x_ref[:128].astype(F32) * v_ref[...]
+    for copy in x_copies[4:]:
+        copy.wait()
+    detail([first, x_ref[128:].astype(F32) * v_ref[...]], *out_refs)
+
+
+def detail(halves, top_ref, bottom_ref, c_ref, own_ref=None):
+    c = block_mean(halves, split3)
     if own_ref is None:
         for tile in range(TILES):
             c_ref[tile] = c
@@ -128,7 +137,7 @@
         own_ref[...] = c
     spread = prolong(c, edges=True)
     for pair in range(PAIRS):
-        at = ROWS * pair
+        w, at = halves[pair // 4], ROWS * (pair % 4)
         top_ref[pair] = w[at : at + 8] - spread[16 * pair : 16 * pair + 8]
         bottom_ref[pair] = w[at + 24 : at + 32] - spread[16 * pair + 8 : 16 * pair + 16]
 
@@ -204,8 +213,8 @@
             band_ref[level, kind] = piece
 
 
-def table_kernel(taps_ref, lat_ref, x_ref, *refs):
-    mix_ref, rows_ref, band_ref, *x_next_refs = refs
+def table_kernel(taps_ref, lat_ref, lon_ref, x_ref, *refs):
+    mix_ref, lats_ref, lons_ref, rows_ref, band_ref, *x_next_refs = refs
     tile, own = own_tile(), lax.axis_index("mem_0")
 
     def picked(values):
@@ -227,7 +236,9 @@
     mine = lat_ref[pl.ds(pl.multiple_of(8 * tile, 8), 8), :]
     wide = exact_mm(mine, repeat)
     mix = jnp.concatenate([wide] * PAIRS, axis=0)
-    mix_ref[...] = jnp.where((i >> 3) == ((j >> 3) & 7), mix, 0.0)
+    mix = jnp.where((i >> 3) == ((j >> 3) & 7), mix, 0.0)
+    for ref, value in ((mix_ref, mix), (lats_ref, lat_ref[...]), (lons_ref, lon_ref[...])):
+        ref[0], ref[1] = split2(value)
 
 
 def banded(band_ref, level, kind):
@@ -275,7 +286,7 @@
     if last:
         rows_ref, band_ref, *refs = refs
     x_refs, refs = (refs[:4], refs[4:]) if last else (refs[:1], refs[1:])
-    x = members_of(x_refs)
+    halves = halves_of(x_refs)
     if last:
         fine_ref, mean_ref, sums_ref, f_ref = refs
         v = natural(v_ref)
@@ -283,14 +294,16 @@
         fine_ref, mean_ref = refs
         v = v_ref[...]
         load.wait()
-    d = x.astype(F32) * for_each(v) - prolong(c_ref[...])
+    v_rows, spread = for_each(v), prolong(c_ref[...])
     highs, lows = [], []
     for part in range(2):
+        d = halves[part].astype(F32) * v_rows - spread[128 * part : 128 * part + 128]
         rows = []
-        for pair in range(4 * part, 4 * part + 4):
-            rows += [before_ref[pair], d[ROWS * pair : ROWS * pair + ROWS], after_ref[pair]]
+        for k in range(4):
+            pair = 4 * part + k
+            rows += [before_ref[pair], d[ROWS * k : ROWS * k + ROWS], after_ref[pair]]
         high, low = split2(jnp.concatenate(rows, axis=0))
-        passed = mm(rows_ref[0], high) + mm(rows_ref[0], low) + mm(rows_ref[1], high)
+        passed = mm3((rows_ref[0], rows_ref[1]), (high, low))
         high, low = split2(passed)
         highs.append(high)
         lows.append(low)
@@ -300,20 +313,20 @@
         high = windows(highs, height * level, height)
         low = windows(lows, height * level, height)
         table_high, table_low = banded(band_ref, level, 0), banded(band_ref, level, 1)
-        result = mm(high, table_high) + mm(low, table_high) + mm(high, table_low)
+        result = mm3((high, low), (table_high, table_low))
         for block in range(4):
             lanes = slice(256 * block, 256 * block + 256)
             summed = None
             for part in range(2):
                 for inner in range(height // ROWS):
-                    row = 128 * part + height * level + ROWS * inner
+                    row = height * level + ROWS * inner
                     at = height * (2 * block + part) + ROWS * inner
                     f = result[at : at + ROWS]
-                    f_ref[row : row + ROWS, lanes] = f
-                    term = x[row : row + ROWS, lanes].astype(F32) * f
+                    f_ref[128 * part + row : 128 * part + row + ROWS, lanes] = f
+                    term = halves[part][row : row + ROWS, lanes].astype(F32) * f
                     summed = term if summed is None else summed + term
             fine_ref[ROWS * level : ROWS * level + ROWS, lanes] = summed
-    means = block_mean(f_ref[...], split2)
+    means = block_mean((f_ref[:128], f_ref[128:]), split2)
     mean_ref[...] = means
     if last:
         own = lax.axis_index("mem_0")
@@ -324,9 +337,10 @@
         )
 
 
-def smooth_kernel(c_ref, lat_ref, lon_ref, sums_ref, out_ref):
+def smooth_kernel(c_ref, lats_ref, lons_ref, sums_ref, out_ref):
     c = c_ref[...].reshape(64, 256)
-    smoothed = exact_mm(exact_mm(lat_ref[...], c), lon_ref[...])
+    across = mm3((lats_ref[0], lats_ref[1]), split2(c))
+    smoothed = mm3(split2(across), (lons_ref[0], lons_ref[1]))
     sums = sums_ref[...] + lane_sums([(4, 16.0 * total(c * smoothed))])
     for tile in range(TILES):
         out_ref[tile, 0:8, :] = smoothed[8 * tile : 8 * tile + 8, :128]
@@ -334,16 +348,20 @@
         out_ref[tile, 16:24, :] = sums
 
 
-def blended(x, fine_ref, smoothed):
-    product = x.astype(F32) * prolong(smoothed)
-    height = fine_ref.shape[0]
-    pieces = [product[k : k + height] for k in range(0, 256, height)]
-    return functools.reduce(jnp.add, pieces, fine_ref[...])
-
-
-def partial_kernel(x_ref, fine_ref, mean_ref, c_ref, mix_ref, lon_ref, out_ref):
-    across = exact_mm(mix_ref[...], c_ref[...].reshape(512, 256))
-    p = blended(x_ref[...], fine_ref, exact_mm(across, lon_ref[...]) - mean_ref[...])
+def blended(x_refs, fine_ref, smoothed):
+    spread, height = prolong(smoothed), fine_ref.shape[0]
+    result = fine_ref[...]
+    for k, x in enumerate(halves_of(x_refs)):
+        product = x.astype(F32) * spread[128 * k : 128 * k + 128]
+        for row in range(0, 128, height):
+            result = result + product[row : row + height]
+    return result
+
+
+def partial_kernel(x_ref, fine_ref, mean_ref, c_ref, mix_ref, lons_ref, out_ref):
+    across = mm3((mix_ref[0], mix_ref[1]), split2(c_ref[...].reshape(512, 256)))
+    smoothed = mm3(split2(across), (lons_ref[0], lons_ref[1]))
+    p = blended((x_ref,), fine_ref, smoothed - mean_ref[...])
     for tall in range(16):
         for wide in range(8):
             out_ref[2 * tall + wide // 4, 8 * (wide % 4) : 8 * (wide % 4) + 8, :] = p[
@@ -368,17 +386,15 @@
 def last_partial_kernel(fine_ref, mean_ref, smoothed_ref, v_ref, *refs):
     *x_refs, out_ref, v_packed = refs
     halves = [smoothed_ref[:, 8 * k : 8 * k + 8, :].reshape(64, 128) for k in range(2)]
-    p = blended(members_of(x_refs), fine_ref, jnp.concatenate(halves, axis=1) - mean_ref[...])
+    p = blended(x_refs, fine_ref, jnp.concatenate(halves, axis=1) - mean_ref[...])
     sums = jnp.sum(smoothed_ref[:, 16:24, :], axis=0)
-    for group, share in enumerate(packed(p)):
-        out_ref[group, 0:8, :] = share
     for group, share in enumerate(packed(natural(v_ref))):
         v_packed[group] = share
-    i, j = iotas(8, 128)
     mine = pl.ds(own_group() & 7, 1)
-    for group in range(GROUPS):
-        row = jnp.broadcast_to(v_packed[group, mine, :], (8, 128))
-        out_ref[group, 8:16, :] = jnp.where(i == 1, row, sums)
+    for group, share in enumerate(packed(p)):
+        out_ref[10 * group : 10 * group + 8] = share
+        out_ref[10 * group + 8 : 10 * group + 9] = v_packed[group, mine, :]
+        out_ref[10 * group + 9 : 10 * group + 10] = sums[:1]
 
 
 def share_kernel(scale, arrived_ref, r_ref, out_ref):
@@ -397,8 +413,10 @@
     group = own_group()
     lanes = pl.ds(pl.multiple_of(128 * (group >> 2), 128), 128)
     i, j = iotas(8, 128)
-    sums = jnp.sum(arrived_ref[:, 8:16, :], axis=0)
-    rr, ra, aa, af, ac = (total(jnp.where((i == 0) & (j == k), sums, 0.0)) for k in range(5))
+    sums = arrived_ref[9:10]
+    for k in range(1, GROUPS):
+        sums = sums + arrived_ref[10 * k + 9 : 10 * k + 10]
+    rr, ra, aa, af, ac = (total(jnp.where(j[:1] == k, sums, 0.0)) for k in range(5))
     rr, ra, aa = rr / 8, ra / 8, aa / 8
     step = rr / ra
     ab = aa + (af + ac) * scale
@@ -411,8 +429,9 @@
             tile = r_ref[row : row + 8, lanes]
             turned = pltpu.roll(tile, (32 * (k + 4 - (group & 3))) & 127, 1)
             r = jnp.where((j >> 5) == k, turned, r)
-        a = jnp.concatenate([arrived_ref[8 * level + k, 9:10, :] for k in range(8)], axis=0)
-        p = jnp.sum(arrived_ref[8 * level : 8 * level + 8, 0:8, :], axis=0)
+        at = [10 * (8 * level + k) for k in range(8)]
+        a = jnp.concatenate([arrived_ref[k + 8 : k + 9] for k in at], axis=0)
+        p = functools.reduce(jnp.add, [arrived_ref[k : k + 8] for k in at])
         b = a + p * scale
         r_next = r - step * a
         x_new = step * r + next_step * r_next
@@ -487,16 +506,18 @@
     before, after = edges(top, bottom)
     c_first = exchange(c, "tile")
     before, x_again = lax.optimization_barrier((before, x))
-    mix, rows_next, band_next, *x_next = call(
+    mix, lats, lons, rows_next, band_next, *x_next = call(
         table_kernel,
         [
-            ((64, 512), F32),
+            ((2, 64, 512), BF16),
+            ((2, 64, 64), BF16),
+            ((2, 256, 256), BF16),
             (rows_shape, BF16),
             ((1, *band_shape), BF16),
             *[((count * height, extent), BF16)] * 4,
         ],
-        [VMEM] * 3,
-        (taps, coarse_lat, x_again),
+        [VMEM] * 4,
+        (taps, coarse_lat, coarse_lon, x_again),
         10**11,
         6,
     )
@@ -525,7 +546,7 @@
         partial_kernel,
         [shared],
         [VMEM] * 6,
-        (x, fine, means, c_first, mix, coarse_lon),
+        (x, fine, means, c_first, mix, lons),
         10**9,
         12,
     )
@@ -564,21 +585,21 @@
         smooth_kernel,
         [((TILES, 24, 128), F32)],
         [VMEM] * 4,
-        (c, coarse_lat, coarse_lon, sums),
+        (c, lats, lons, sums),
         10**8,
         6,
     )
     smoothed = exchange(smoothed, "tile")
     shares = call(
         last_partial_kernel,
-        [((GROUPS, 16, 128), F32)],
+        [((GROUPS * 10, 128), F32)],
         [VMEM] * 8,
         (fine, means, smoothed, a, *x_next),
         10**9,
         12,
         scratch=[pltpu.VMEM((GROUPS, 8, 128), F32)],
     )
-    arrived = exchange(shares, MEM)
+    arrived = exchange(shares.reshape(GROUPS, 1, 1280), MEM).reshape(shares.shape)
     out = ((levels, height, extent // GROUPS), F32)
     return tuple(
         call(

time: 106 us -> 105 us (level)
  local copies, waits for them, and re-layouts: 0.02 us -> 2.6 us
  waiting for transfers between devices: 10.4 us -> 7.93 us
    unnamed x12 -> x26, local copies, waits for them, and re-layouts: 0.02 us -> 2.6 us
    all_to_all x2, waiting for transfers between devices: 7.55 us -> 5.13 us  [exchange(): return lax.all_to_all(blocks, axis, 0, 0, tiled=True)]
  transfers between devices with their start and end apart: 9 -> 9, of which waited for: 5 -> 5; matrix products, arithmetic and copies ran while one was open for 0% -> 0% of each run, Pallas kernels for 7% -> 8%
where the time goes in v5:
time: 105 us; the launch traced here: 104 us
  blocking collectives  53.4 us (51%)
  starting transfers between devices  23.1 us (22%)
  Pallas kernels  16.6 us (16%)
  waiting for transfers between devices  7.93 us (8%)
  local copies, waits for them, and re-layouts  2.6 us (2%)
    all_to_all x4, blocking collectives, exchange(): return lax.all_to_all(blocks, axis, 0, 0, tiled=True)  53.4 us
    pallas_call x10, Pallas kernels, call(): pl.pallas_call(kernel, out_shape=shapes if len(shapes) > 1 else shapes[0]...  16.6 us
    ppermute x4, starting transfers between devices, edges(): return (lax.ppermute(bottom, 'tile', up), lax.ppermute(top, 'tile', down))  9.25 us
    all_to_all x2, starting transfers between devices, exchange(): return lax.all_to_all(blocks, axis, 0, 0, tiled=True)  8.87 us
    all_to_all x2, waiting for transfers between devices, exchange(): return lax.all_to_all(blocks, axis, 0, 0, tiled=True)  5.13 us
    ppermute x3, starting transfers between devices, local(): x_next[ahead] = lax.ppermute(x_next[ahead], 'mem_0', ring)  4.98 us
    unnamed x26, local copies, waits for them, and re-layouts  2.6 us
    ppermute x4, waiting for transfers between devices, edges(): return (lax.ppermute(bottom, 'tile', up), lax.ppermute(top, 'tile', down))  2.54 us
  transfers between devices with their start and end apart: 9, of which 5 were waited for; matrix products, arithmetic and copies ran while one was open for 0% of the time, Pallas kernels for 8%

profile of v5, /device:TPU:1, one launch (start us, length us, event | category | flops | bytes accessed | tf_op | source)
XLA Modules:
  0.0 104.4 jit_solution(12124088173008657483)
XLA Ops:
  0.6 3.0 %shard_map.68 = (f32[8,8,1024]{2,1,0:T(8,128)S(1)}, f32[8,8,1024]{2,1,0:T(8,128)S(1)}, f32[8,64,256]{2,1,0:T(8,128)}) custom-call(bf16[256,1024]{1,0:T(8,128)(2,1)} %bitcast.12, f32[128,1024]{1,0:T(8,128)} %bitcast.5), custom_call_target="tpu_custom_call" | custom-call | flops 1000000000 | bytes 1048576 | tf_op jit(solution)/shard_map/pallas_call | solution.py:459
  3.6 2.5 %collective-permute-start = (f32[8,8,1024]{2,1,0:T(8,128)S(1)}, f32[8,8,1024]{2,1,0:T(8,128)S(1)}, u32[]{:S(2)}, u32[]{:S(2)}) collective-permute-start(f32[8,8,1024]{2,1,0:T(8,128)S(1)} %get-tuple-element.33), channel_id=1, source_target_pairs={{0,1},{1,2},{2,3},{3,4},{4,5},{5,6},{6,7},{7,0},{8,9},{9,10},{10,1... | collective-permute-start | bytes 786440 | tf_op jit(solution)/shard_map/ppermute | solution.py:487
  6.1 4.0 %collective-permute-start.1 = (f32[8,8,1024]{2,1,0:T(8,128)S(1)}, f32[8,8,1024]{2,1,0:T(8,128)S(1)}, u32[]{:S(2)}, u32[]{:S(2)}) collective-permute-start(f32[8,8,1024]{2,1,0:T(8,128)S(1)} %get-tuple-element.38), channel_id=1, source_target_pairs={{1,0},{2,1},{3,2},{4,3},{5,4},{6,5},{7,6},{0,7},{9,8},{10,9},{11,1... | collective-permute-start | bytes 786440 | tf_op jit(solution)/shard_map/ppermute | solution.py:487
  10.2 0.0 copy-start.1
  10.2 0.0 copy-start.2
  10.2 0.0 copy-start.3
  10.2 0.0 copy-start.4
  10.2 5.3 %all-to-all-start = ((f32[8,64,256]{2,1,0:T(8,128)}), f32[8,64,256]{2,1,0:T(8,128)}, u32[]{:S(2)}, u32[]{:S(2)}) async-start(f32[8,64,256]{2,1,0:T(8,128)} %get-tuple-element.32.refs_1_), calls=%async_computation | async-start | bytes 1048576 | tf_op jit(solution)/shard_map/all_to_all | solution.py:471
  15.5 0.6 collective-permute-done.refs_3_
  16.1 0.0 copy-done.1
  16.1 0.0 copy-done.2
  16.1 0.0 copy-done.3
  16.1 0.0 copy-done.4
  16.1 0.0 copy-start
  16.1 0.7 shard_map.69
  16.9 0.0 copy-start.5
  16.9 0.6 copy-done.5
  17.5 0.0 copy-start.7
  17.5 0.7 copy-done.7
  18.2 0.0 copy-start.9
  18.2 0.6 copy-done.9
  18.8 0.0 copy-start.11
  18.8 0.6 copy-done.11
  19.5 1.3 %collective-permute-start.2 = (bf16[64,1024]{1,0:T(8,128)(2,1)S(1)}, bf16[64,1024]{1,0:T(8,128)(2,1)S(1)}, u32[]{:S(2)}, u32[]{:S(2)}) collective-permute-start(bf16[64,1024]{1,0:T(8,128)(2,1)S(1)} %get-tuple-element.41), channel_id=1, source_target_pairs={{0,64},{64,128},{128,192},{192,0},{1,65},{65,129},{129,193},{193,1... | collective-permute-start | bytes 393224 | tf_op jit(solution)/shard_map/ppermute | solution.py:527
  20.7 2.6 %collective-permute-start.3 = (bf16[64,1024]{1,0:T(8,128)(2,1)S(1)}, bf16[64,1024]{1,0:T(8,128)(2,1)S(1)}, u32[]{:S(2)}, u32[]{:S(2)}) collective-permute-start(bf16[64,1024]{1,0:T(8,128)(2,1)S(1)} %get-tuple-element.42), channel_id=1, source_target_pairs={{0,128},{64,192},{128,0},{192,64},{1,129},{65,193},{129,1},{193,65... | collective-permute-start | bytes 393224 | tf_op jit(solution)/shard_map/ppermute | solution.py:527
  23.4 0.0 copy-start.6
  23.4 1.1 %collective-permute-start.4 = (bf16[64,1024]{1,0:T(8,128)(2,1)S(1)}, bf16[64,1024]{1,0:T(8,128)(2,1)S(1)}, u32[]{:S(2)}, u32[]{:S(2)}) collective-permute-start(bf16[64,1024]{1,0:T(8,128)(2,1)S(1)} %get-tuple-element.43), channel_id=1, source_target_pairs={{0,192},{64,0},{128,64},{192,128},{1,193},{65,1},{129,65},{193,129... | collective-permute-start | bytes 393224 | tf_op jit(solution)/shard_map/ppermute | solution.py:527
  24.4 0.0 collective-permute-done.1.refs_4_
  24.4 0.0 copy-done
  24.4 4.2 %shard_map.70 = (f32[128,1024]{1,0:T(8,128)S(1)}, f32[64,256]{1,0:T(8,128)S(1)}) custom-call(f32[128,1024]{1,0:T(8,128)S(1)} %bitcast.6, f32[8,64,256]{2,1,0:T(8,128)} %get-tuple-element.32.refs_1_, f32[8,5]{1,0:T(8,128)S(1)} %bitcast.17, f32[8,8,1024]{2,1,0:T(8,128)S(1)} %collective-permute-done.refs_3_, f32[8,8,1024]{2,1,0:T(8,128)S(1)} %collective-permute-done.1.refs_4_, ...), custom_call_target="tpu_custom_call" | custom-call | flops 99999997952 | bytes 2097312 | tf_op jit(solution)/shard_map/pallas_call | solution.py:459
  28.6 0.0 collective-permute-done.2.refs_1_.refs_8_
  28.6 0.0 collective-permute-done.3.refs_2_.refs_9_
  28.6 0.3 collective-permute-done.4.refs_3_.refs_10_
  28.9 3.1 %all-to-all-done.c_ref = f32[8,64,256]{2,1,0:T(8,128)} async-done(((f32[8,64,256]{2,1,0:T(8,128)}), f32[8,64,256]{2,1,0:T(8,128)}, u32[]{:S(2)}, u32[]{:S(2)}) %all-to-all-start) | async-done | bytes 524320 | tf_op jit(solution)/shard_map/all_to_all | solution.py:471
  32.0 0.0 copy-done.6
  32.0 2.2 %shard_map.71 = f32[32,32,128]{2,1,0:T(8,128)S(1)} custom-call(bf16[256,1024]{1,0:T(8,128)(2,1)S(1)} %bitcast.15, f32[128,1024]{1,0:T(8,128)S(1)} %get-tuple-element.44.fine_ref, f32[64,256]{1,0:T(8,128)S(1)} %get-tuple-element.45.mean_ref, f32[8,64,256]{2,1,0:T(8,128)} %all-to-all-done.c_ref, bf16[2,64,512]{2,1,0:T(8,128)(2,1)S(1)} %copy-done.6, ...), custom_call_target="tpu_custom_call" | custom-call | flops 1000000000 | bytes 2031616 | tf_op jit(solution)/shard_map/pallas_call | solution.py:459
  34.2 20.5 %all_to_all.30.arrived_ref = f32[32,32,128]{2,1,0:T(8,128)S(1)} all-to-all(f32[32,32,128]{2,1,0:T(8,128)S(1)} %shard_map.71), channel_id=1, replica_groups=mesh['mem_0'=4,'mem_1'=4,'mem_2'=2,'tile'=8] {'mem_0','mem_1','mem_2'}, dimensions={0} | all-to-all | bytes 1048576 | tf_op jit(solution)/shard_map/all_to_all | solution.py:471
  54.8 0.0 copy-start.8
  54.8 8.2 %all_to_all.31.v_ref.refs_1_ = f32[8,32,128]{2,1,0:T(8,128)S(1)} all-to-all(f32[8,32,128]{2,1,0:T(8,128)S(1)} %shard_map.72), channel_id=1, replica_groups=mesh['mem_0'=4,'mem_1'=4,'mem_2'=2,'tile'=8] {'mem_1','mem_2'}, dimensions={0} | all-to-all | bytes 262144 | tf_op jit(solution)/shard_map/all_to_all | solution.py:471
  63.0 0.0 copy-done.8
  63.0 0.0 copy-start.12
  63.0 1.4 %shard_map.73 = (f32[8,8,1024]{2,1,0:T(8,128)S(1)}, f32[8,8,1024]{2,1,0:T(8,128)S(1)}, f32[8,8,256]{2,1,0:T(8,128)}, f32[64,256]{1,0:T(8,128)S(1)}) custom-call(f32[8,32,128]{2,1,0:T(8,128)S(1)} %all_to_all.31.v_ref.refs_1_, bf16[64,1024]{1,0:T(8,128)(2,1)S(1)} %copy-done.8, bf16[64,1024]{1,0:T(8,128)(2,1)S(1)} %collective-permute-done.2.refs_1_.refs_8_, ...), custom_call_target="tpu_custom_call" | custom-call | flops 1000000000 | bytes 655360 | tf_op jit(solution)/shard_map/pallas_call | solution.py:459
  64.4 0.0 copy-start.10
  64.4 0.3 collective-permute-start.5
  64.7 2.4 %collective-permute-start.6 = (f32[8,8,1024]{2,1,0:T(8,128)S(1)}, f32[8,8,1024]{2,1,0:T(8,128)S(1)}, u32[]{:S(2)}, u32[]{:S(2)}) collective-permute-start(f32[8,8,1024]{2,1,0:T(8,128)S(1)} %get-tuple-element.54), channel_id=1, source_target_pairs={{1,0},{2,1},{3,2},{4,3},{5,4},{6,5},{7,6},{0,7},{9,8},{10,9},{11,1... | collective-permute-start | bytes 786440 | tf_op jit(solution)/shard_map/ppermute | solution.py:487
  67.0 3.5 %all-to-all-start.3 = ((f32[8,8,256]{2,1,0:T(8,128)}), f32[8,8,256]{2,1,0:T(8,128)S(1)}, u32[]{:S(2)}, u32[]{:S(2)}) async-start(f32[8,8,256]{2,1,0:T(8,128)} %get-tuple-element.59), calls=%async_computation.3 | async-start | bytes 131072 | tf_op jit(solution)/shard_map/all_to_all | solution.py:471
  70.6 1.9 %collective-permute-done.5.refs_3_ = f32[8,8,1024]{2,1,0:T(8,128)S(1)} collective-permute-done((f32[8,8,1024]{2,1,0:T(8,128)S(1)}, f32[8,8,1024]{2,1,0:T(8,128)S(1)}, u32[]{:S(2)}, u32[]{:S(2)}) %collective-permute-start.5) | collective-permute-done | bytes 262176 | tf_op jit(solution)/shard_map/ppermute | solution.py:487
  72.5 0.0 collective-permute-done.6.refs_4_
  72.5 0.0 copy-done.12
  72.5 0.0 copy-done.10
  72.5 3.0 %shard_map.74 = (f32[32,1024]{1,0:T(8,128)S(1)}, f32[64,256]{1,0:T(8,128)S(1)}, f32[8,128]{1,0:T(8,128)S(1)}) custom-call(f32[128,1024]{1,0:T(8,128)S(1)} %bitcast.8, f32[8,32,128]{2,1,0:T(8,128)S(1)} %all_to_all.31.v_ref.refs_1_, f32[64,256]{1,0:T(8,128)S(1)} %get-tuple-element.52.refs_2_, f32[8,8,1024]{2,1,0:T(8,128)S(1)} %collective-permute-done.5.refs_3_, ...), custom_call_target="tpu_custom_call" | custom-call | flops 99999997952 | bytes 1949696 | tf_op jit(solution)/shard_map/pallas_call | solution.py:459
  75.6 2.0 %all-to-all-done.3.c_ref = f32[8,8,256]{2,1,0:T(8,128)S(1)} async-done(((f32[8,8,256]{2,1,0:T(8,128)}), f32[8,8,256]{2,1,0:T(8,128)S(1)}, u32[]{:S(2)}, u32[]{:S(2)}) %all-to-all-start.3) | async-done | bytes 65568 | tf_op jit(solution)/shard_map/all_to_all | solution.py:471
  77.5 0.5 shard_map.75
  78.0 10.0 %all_to_all.32.smoothed_ref = f32[8,24,128]{2,1,0:T(8,128)S(1)} all-to-all(f32[8,24,128]{2,1,0:T(8,128)S(1)} %shard_map.75), channel_id=1, replica_groups=mesh['mem_0'=4,'mem_1'=4,'mem_2'=2,'tile'=8] {'tile'}, dimensions={0} | all-to-all | bytes 196608 | tf_op jit(solution)/shard_map/all_to_all | solution.py:471
  88.0 0.7 shard_map.76
  88.7 14.8 %all_to_all.33 = f32[32,1,1280]{2,1,0:T(1,128)S(1)} all-to-all(f32[32,1,1280]{2,1,0:T(1,128)S(1)} %bitcast.11), channel_id=1, replica_groups=mesh['mem_0'=4,'mem_1'=4,'mem_2'=2,'tile'=8] {'mem_0','mem_1','mem_2'}, dimensions={0} | all-to-all | bytes 327680 | tf_op jit(solution)/shard_map/all_to_all | solution.py:471
  103.5 0.9 shard_map.77
  (1 shorter events, 0.0 us)
Async XLA Ops:
  3.6 12.5 %collective-permute-start = (f32[8,8,1024]{2,1,0:T(8,128)S(1)}, f32[8,8,1024]{2,1,0:T(8,128)S(1)}, u32[]{:S(2)}, u32[]{:S(2)}) collective-permute-start(f32[8,8,1024]{2,1,0:T(8,128)S(1)} %get-tuple-element.33), channel_id=1, source_target_pairs={{0,1},{1,2},{2,3},{3,4},{4,5},{5,6},{6,7},{7,0},{8,9},{9,10},{10,1... | collective-permute-start | bytes 786440 | tf_op jit(solution)/shard_map/ppermute | solution.py:487
  6.1 18.3 %collective-permute-start.1 = (f32[8,8,1024]{2,1,0:T(8,128)S(1)}, f32[8,8,1024]{2,1,0:T(8,128)S(1)}, u32[]{:S(2)}, u32[]{:S(2)}) collective-permute-start(f32[8,8,1024]{2,1,0:T(8,128)S(1)} %get-tuple-element.38), channel_id=1, source_target_pairs={{1,0},{2,1},{3,2},{4,3},{5,4},{6,5},{7,6},{0,7},{9,8},{10,9},{11,1... | collective-permute-start | bytes 786440 | tf_op jit(solution)/shard_map/ppermute | solution.py:487
  10.2 5.9 %copy-start.1 = (bf16[2,4,32,1024]{3,2,1,0:T(8,128)(2,1)S(1)}, bf16[2,4,32,1024]{3,2,1,0:T(8,128)(2,1)}, u32[]{:S(2)}) copy-start(bf16[2,4,32,1024]{3,2,1,0:T(8,128)(2,1)} %param.5) | copy-start | bytes 1572868
  10.2 5.9 %copy-start.2 = (f32[256,256]{1,0:T(8,128)S(1)}, f32[256,256]{1,0:T(8,128)}, u32[]{:S(2)}) copy-start(f32[256,256]{1,0:T(8,128)} %lon_ref.1) | copy-start | bytes 786436
  10.2 5.9 %copy-start.3 = (f32[64,64]{1,0:T(8,128)S(1)}, f32[64,64]{1,0:T(8,128)}, u32[]{:S(2)}) copy-start(f32[64,64]{1,0:T(8,128)} %lat_ref.1) | copy-start | bytes 49156
  10.2 5.9 %copy-start.4 = (f32[2,4,5]{2,1,0:T(4,128)S(1)}, f32[2,4,5]{2,1,0:T(4,128)}, u32[]{:S(2)}) copy-start(f32[2,4,5]{2,1,0:T(4,128)} %param.7) | copy-start | bytes 484
  10.2 21.9 %all-to-all-start = ((f32[8,64,256]{2,1,0:T(8,128)}), f32[8,64,256]{2,1,0:T(8,128)}, u32[]{:S(2)}, u32[]{:S(2)}) async-start(f32[8,64,256]{2,1,0:T(8,128)} %get-tuple-element.32.refs_1_), calls=%async_computation | async-start | bytes 1048576 | tf_op jit(solution)/shard_map/all_to_all | solution.py:471
  16.1 8.3 %copy-start = (f32[4,32,1024]{2,1,0:T(8,128)S(1)}, f32[4,32,1024]{2,1,0:T(8,128)}, u32[]{:S(2)}) copy-start(f32[4,32,1024]{2,1,0:T(8,128)} %param.6) | copy-start | bytes 1572868
  16.9 0.6 copy-start.5
  17.5 0.7 copy-start.7
  18.2 0.6 copy-start.9
  18.8 0.6 copy-start.11
  19.5 9.2 %collective-permute-start.2 = (bf16[64,1024]{1,0:T(8,128)(2,1)S(1)}, bf16[64,1024]{1,0:T(8,128)(2,1)S(1)}, u32[]{:S(2)}, u32[]{:S(2)}) collective-permute-start(bf16[64,1024]{1,0:T(8,128)(2,1)S(1)} %get-tuple-element.41), channel_id=1, source_target_pairs={{0,64},{64,128},{128,192},{192,0},{1,65},{65,129},{129,193},{193,1... | collective-permute-start | bytes 393224 | tf_op jit(solution)/shard_map/ppermute | solution.py:527
  20.7 7.9 %collective-permute-start.3 = (bf16[64,1024]{1,0:T(8,128)(2,1)S(1)}, bf16[64,1024]{1,0:T(8,128)(2,1)S(1)}, u32[]{:S(2)}, u32[]{:S(2)}) collective-permute-start(bf16[64,1024]{1,0:T(8,128)(2,1)S(1)} %get-tuple-element.42), channel_id=1, source_target_pairs={{0,128},{64,192},{128,0},{192,64},{1,129},{65,193},{129,1},{193,65... | collective-permute-start | bytes 393224 | tf_op jit(solution)/shard_map/ppermute | solution.py:527
  23.4 8.7 %copy-start.6 = (bf16[2,64,512]{2,1,0:T(8,128)(2,1)S(1)}, bf16[2,64,512]{2,1,0:T(8,128)(2,1)}, u32[]{:S(2)}) copy-start(bf16[2,64,512]{2,1,0:T(8,128)(2,1)} %copy-done.5) | copy-start | bytes 393220
  23.4 5.5 %collective-permute-start.4 = (bf16[64,1024]{1,0:T(8,128)(2,1)S(1)}, bf16[64,1024]{1,0:T(8,128)(2,1)S(1)}, u32[]{:S(2)}, u32[]{:S(2)}) collective-permute-start(bf16[64,1024]{1,0:T(8,128)(2,1)S(1)} %get-tuple-element.43), channel_id=1, source_target_pairs={{0,192},{64,0},{128,64},{192,128},{1,193},{65,1},{129,65},{193,129... | collective-permute-start | bytes 393224 | tf_op jit(solution)/shard_map/ppermute | solution.py:527
  54.8 8.2 %copy-start.8 = (bf16[64,1024]{1,0:T(8,128)(2,1)S(1)}, bf16[64,1024]{1,0:T(8,128)(2,1)}, u32[]{:S(2)}) copy-start(bf16[64,1024]{1,0:T(8,128)(2,1)} %copy-done.7) | copy-start | bytes 393220
  63.0 9.5 %copy-start.12 = (bf16[1,2,160,128]{3,2,1,0:T(8,128)(2,1)S(1)}, bf16[1,2,160,128]{3,2,1,0:T(8,128)(2,1)}, u32[]{:S(2)}) copy-start(bf16[1,2,160,128]{3,2,1,0:T(8,128)(2,1)} %copy-done.11) | copy-start | bytes 245764
  64.4 8.2 %copy-start.10 = (bf16[2,128,192]{2,1,0:T(8,128)(2,1)S(1)}, bf16[2,128,192]{2,1,0:T(8,128)(2,1)}, u32[]{:S(2)}) copy-start(bf16[2,128,192]{2,1,0:T(8,128)(2,1)} %copy-done.9) | copy-start | bytes 294916
  64.4 8.2 %collective-permute-start.5 = (f32[8,8,1024]{2,1,0:T(8,128)S(1)}, f32[8,8,1024]{2,1,0:T(8,128)S(1)}, u32[]{:S(2)}, u32[]{:S(2)}) collective-permute-start(f32[8,8,1024]{2,1,0:T(8,128)S(1)} %get-tuple-element.53), channel_id=1, source_target_pairs={{0,1},{1,2},{2,3},{3,4},{4,5},{5,6},{6,7},{7,0},{8,9},{9,10},{10,1... | collective-permute-start | bytes 786440 | tf_op jit(solution)/shard_map/ppermute | solution.py:487
  64.7 7.9 %collective-permute-start.6 = (f32[8,8,1024]{2,1,0:T(8,128)S(1)}, f32[8,8,1024]{2,1,0:T(8,128)S(1)}, u32[]{:S(2)}, u32[]{:S(2)}) collective-permute-start(f32[8,8,1024]{2,1,0:T(8,128)S(1)} %get-tuple-element.54), channel_id=1, source_target_pairs={{1,0},{2,1},{3,2},{4,3},{5,4},{6,5},{7,6},{0,7},{9,8},{10,9},{11,1... | collective-permute-start | bytes 786440 | tf_op jit(solution)/shard_map/ppermute | solution.py:487
  67.0 10.5 %all-to-all-start.3 = ((f32[8,8,256]{2,1,0:T(8,128)}), f32[8,8,256]{2,1,0:T(8,128)S(1)}, u32[]{:S(2)}, u32[]{:S(2)}) async-start(f32[8,8,256]{2,1,0:T(8,128)} %get-tuple-element.59), calls=%async_computation.3 | async-start | bytes 131072 | tf_op jit(solution)/shard_map/all_to_all | solution.py:471

commit v6 on v5

--- a/solution.py
+++ b/solution.py
@@ -213,9 +213,31 @@
             band_ref[level, kind] = piece
 
 
-def table_kernel(taps_ref, lat_ref, lon_ref, x_ref, *refs):
-    mix_ref, lats_ref, lons_ref, rows_ref, band_ref, *x_next_refs = refs
-    tile, own = own_tile(), lax.axis_index("mem_0")
+def table_kernel(x_hbm, r_hbm, taps_ref, lat_ref, lon_ref, *refs):
+    *refs, lats_ref, rows_ref, band_ref, lanes_ref, sems = refs
+    mix_ref, lons_ref, share_ref, level_ref, packed_ref, *refs = refs
+    x_next_refs, hbm_refs = refs[:4], refs[4:]
+    tile, own, group = own_tile(), lax.axis_index("mem_0"), own_group()
+    lanes = pl.ds(pl.multiple_of(128 * (group >> 2), 128), 128)
+    pieces = [
+        (r_hbm.at[:, lanes], lanes_ref),
+        (r_hbm.at[pl.ds(pl.multiple_of(ROWS * own, ROWS), ROWS)], level_ref),
+    ]
+    for k in range(4):
+        at = pl.multiple_of(512 * (group & 1) + 128 * k, 128)
+        rows = pl.ds(pl.multiple_of(8 * (group >> 1), 8), 8)
+        pieces.append((r_hbm.at[rows, pl.ds(at, 128)], share_ref.at[pl.ds(8 * k, 8)]))
+    for ahead, x_next_ref in enumerate(x_next_refs):
+        for member in range(2):
+            row = pl.multiple_of(ROWS * (4 * member + ((own + ahead) & 3)), ROWS)
+            target = x_next_ref.at[pl.ds(ROWS * member, ROWS)]
+            pieces.append((x_hbm.at[pl.ds(row, ROWS)], target))
+    loads = [
+        pltpu.make_async_copy(source, target, sems.at[3 + k])
+        for k, (source, target) in enumerate(pieces)
+    ]
+    for load in loads:
+        load.start()
 
     def picked(values):
         value = values[3]
@@ -225,20 +247,34 @@
 
     lat, lon = ([[picked(tap)] * 4 for tap in taps] for taps in taps_of(taps_ref))
     fill_tables(lat, lon, tile, rows_ref, band_ref)
-    for ahead, x_next_ref in enumerate(x_next_refs):
-        for member in range(2):
-            row = ROWS * (4 * member + ((own + ahead) & 3))
-            x_next_ref[ROWS * member : ROWS * member + ROWS] = x_ref[
-                pl.ds(pl.multiple_of(row, ROWS), ROWS), :
-            ]
+    lats_ref[0], lats_ref[1] = split2(lat_ref[...])
+    copies = [
+        pltpu.make_async_copy(source, target, sems.at[k])
+        for k, (source, target) in enumerate(zip((lats_ref, rows_ref, band_ref), hbm_refs))
+    ]
+    for copy in copies:
+        copy.start()
     i, j = iotas(64, 512)
     repeat = jnp.where((i >> 3) == (j >> 6), jnp.where((i & 7) == (j & 7), 1.0, 0.0), 0.0)
     mine = lat_ref[pl.ds(pl.multiple_of(8 * tile, 8), 8), :]
     wide = exact_mm(mine, repeat)
     mix = jnp.concatenate([wide] * PAIRS, axis=0)
     mix = jnp.where((i >> 3) == ((j >> 3) & 7), mix, 0.0)
-    for ref, value in ((mix_ref, mix), (lats_ref, lat_ref[...]), (lons_ref, lon_ref[...])):
-        ref[0], ref[1] = split2(value)
+    mix_ref[0], mix_ref[1] = split2(mix)
+    lons_ref[0], lons_ref[1] = split2(lon_ref[...])
+    for load in loads:
+        load.wait()
+    j = lax.broadcasted_iota(jnp.int32, (8, 128), 1)
+    for level in range(4):
+        packed_r = jnp.zeros((8, 128), F32)
+        for k in range(4):
+            row = ROWS * level + 8 * k
+            shift = (32 * (k + 4 - (group & 3))) & 127
+            turned = pltpu.roll(lanes_ref[row : row + 8], shift, 1)
+            packed_r = jnp.where((j >> 5) == k, turned, packed_r)
+        packed_ref[level] = packed_r
+    for copy in copies:
+        copy.wait()
 
 
 def banded(band_ref, level, kind):
@@ -277,23 +313,30 @@
     if last:
         r_ref, v_ref, c_ref, *refs = refs
     else:
-        *refs, f_ref, c_ref, rows_ref, band_ref, sem = refs
-        v_ref, c_hbm, taps_ref, *refs = refs
-        load = pltpu.make_async_copy(c_hbm.at[0], c_ref, sem)
-        load.start()
+        *refs, f_ref, c_ref, v_ref, x_ref, rows_ref, band_ref, sems = refs
+        v_hbm, c_hbm, x_hbm, taps_ref, *refs = refs
+        loads = [
+            pltpu.make_async_copy(source, target, sems.at[k])
+            for k, (source, target) in enumerate(
+                ((c_hbm.at[0], c_ref), (v_hbm, v_ref), (x_hbm, x_ref))
+            )
+        ]
+        for load in loads:
+            load.start()
         fill_tables(*taps_of(taps_ref), own_tile(), rows_ref, band_ref)
     before_ref, after_ref, *refs = refs
     if last:
         rows_ref, band_ref, *refs = refs
-    x_refs, refs = (refs[:4], refs[4:]) if last else (refs[:1], refs[1:])
-    halves = halves_of(x_refs)
+    x_refs, refs = (refs[:4], refs[4:]) if last else ((x_ref,), refs)
     if last:
         fine_ref, mean_ref, sums_ref, f_ref = refs
         v = natural(v_ref)
     else:
         fine_ref, mean_ref = refs
+        for load in loads:
+            load.wait()
         v = v_ref[...]
-        load.wait()
+    halves = halves_of(x_refs)
     v_rows, spread = for_each(v), prolong(c_ref[...])
     highs, lows = [], []
     for part in range(2):
@@ -329,8 +372,7 @@
     means = block_mean((f_ref[:128], f_ref[128:]), split2)
     mean_ref[...] = means
     if last:
-        own = lax.axis_index("mem_0")
-        r = r_ref[pl.ds(pl.multiple_of(ROWS * own, ROWS), ROWS), :]
+        r = r_ref[...]
         products = total(v * fine_ref[...]) - 16.0 * total(c_ref[...] * means)
         sums_ref[...] = lane_sums(
             ((0, total(r * r)), (1, total(r * v)), (2, total(v * v)), (3, products))
@@ -348,8 +390,10 @@
         out_ref[tile, 16:24, :] = sums
 
 
-def blended(x_refs, fine_ref, smoothed):
+def blended(x_refs, fine_ref, smoothed, loads=()):
     spread, height = prolong(smoothed), fine_ref.shape[0]
+    for load in loads:
+        load.wait()
     result = fine_ref[...]
     for k, x in enumerate(halves_of(x_refs)):
         product = x.astype(F32) * spread[128 * k : 128 * k + 128]
@@ -358,10 +402,26 @@
     return result
 
 
-def partial_kernel(x_ref, fine_ref, mean_ref, c_ref, mix_ref, lons_ref, out_ref):
-    across = mm3((mix_ref[0], mix_ref[1]), split2(c_ref[...].reshape(512, 256)))
-    smoothed = mm3(split2(across), (lons_ref[0], lons_ref[1]))
-    p = blended((x_ref,), fine_ref, smoothed - mean_ref[...])
+def partial_kernel(x_hbm, c_hbm, fine_ref, mean_ref, mix_ref, lons_ref, out_ref, *refs):
+    x_ref, c_ref, sems = refs
+    spans = [(c_hbm, c_ref, k, 1) for k in range(TILES)]
+    spans += [(x_hbm, x_ref, 64 * k, 64) for k in range(4)]
+    loads = [
+        pltpu.make_async_copy(source.at[pl.ds(at, size)], target.at[pl.ds(at, size)], sems.at[k])
+        for k, (source, target, at, size) in enumerate(spans)
+    ]
+    for load in loads:
+        load.start()
+    across = None
+    for part in range(2):
+        for load in loads[4 * part : 4 * part + 4]:
+            load.wait()
+        lanes = slice(256 * part, 256 * part + 256)
+        c = c_ref[4 * part : 4 * part + 4].reshape(256, 256)
+        term = mm3((mix_ref[0, :, lanes], mix_ref[1, :, lanes]), split2(c))
+        across = term if across is None else across + term
+    smoothed = mm3(split2(across), (lons_ref[0], lons_ref[1])) - mean_ref[...]
+    p = blended((x_ref,), fine_ref, smoothed, loads[8:])
     for tall in range(16):
         for wide in range(8):
             out_ref[2 * tall + wide // 4, 8 * (wide % 4) : 8 * (wide % 4) + 8, :] = p[
@@ -398,20 +458,12 @@
 
 
 def share_kernel(scale, arrived_ref, r_ref, out_ref):
-    group = own_group()
-    share = r_ref[
-        pl.ds(pl.multiple_of(8 * (group >> 1), 8), 8),
-        pl.ds(pl.multiple_of(512 * (group & 1), 512), 512),
-    ]
-    share = jnp.concatenate([share[:, 128 * k : 128 * k + 128] for k in range(4)], axis=0)
-    share = share + jnp.sum(arrived_ref[...], axis=0) * scale
+    share = r_ref[...] + jnp.sum(arrived_ref[...], axis=0) * scale
     for other in range(out_ref.shape[0]):
         out_ref[other] = share
 
 
 def final_kernel(scale, arrived_ref, r_ref, x_out, res_out):
-    group = own_group()
-    lanes = pl.ds(pl.multiple_of(128 * (group >> 2), 128), 128)
     i, j = iotas(8, 128)
     sums = arrived_ref[9:10]
     for k in range(1, GROUPS):
@@ -423,12 +475,7 @@
     squares = step * step * aa - rr
     next_step = squares / ((ra - step * aa) - step * (aa - step * ab))
     for level in range(4):
-        r = jnp.zeros((8, 128), F32)
-        for k in range(4):
-            row = ROWS * level + 8 * k
-            tile = r_ref[row : row + 8, lanes]
-            turned = pltpu.roll(tile, (32 * (k + 4 - (group & 3))) & 127, 1)
-            r = jnp.where((j >> 5) == k, turned, r)
+        r = r_ref[level]
         at = [10 * (8 * level + k) for k in range(8)]
         a = jnp.concatenate([arrived_ref[k + 8 : k + 9] for k in at], axis=0)
         p = functools.reduce(jnp.add, [arrived_ref[k : k + 8] for k in at])
@@ -506,21 +553,31 @@
     before, after = edges(top, bottom)
     c_first = exchange(c, "tile")
     before, x_again = lax.optimization_barrier((before, x))
-    mix, lats, lons, rows_next, band_next, *x_next = call(
+    next_tables = [((2, 64, 64), BF16), (rows_shape, BF16), ((1, *band_shape), BF16)]
+    level = ((height, LON), F32)
+    outs = [
+        ((2, 64, 512), BF16),
+        ((2, 256, 256), BF16),
+        ((32, 128), F32),
+        level,
+        ((levels, 8, 128), F32),
+        *[((count * height, extent), BF16)] * 4,
+    ]
+    mix, lons, r_share, r_level, r_packed, *x_next = call(
         table_kernel,
-        [
-            ((2, 64, 512), BF16),
-            ((2, 64, 64), BF16),
-            ((2, 256, 256), BF16),
-            (rows_shape, BF16),
-            ((1, *band_shape), BF16),
-            *[((count * height, extent), BF16)] * 4,
-        ],
-        [VMEM] * 4,
-        (taps, coarse_lat, coarse_lon, x_again),
+        outs + next_tables,
+        [HBM] * 2 + [VMEM] * 3,
+        (x_again, r, taps, coarse_lat, coarse_lon),
         10**11,
         6,
-    )
+        scratch=[
+            *(pltpu.VMEM(*shape) for shape in next_tables),
+            pltpu.VMEM((128, 128), F32),
+            pltpu.SemaphoreType.DMA((17,)),
+        ],
+        out_specs=[VMEM] * len(outs) + [HBM] * 3,
+    )
+    *x_next, lats, rows_next, band_next = x_next
     before, mix = lax.optimization_barrier((before, mix))
     for ahead in range(1, 4):
         ring = [(i, (i + ahead) % 4) for i in range(4)]
@@ -529,33 +586,40 @@
     fine, means = call(
         functools.partial(fine_kernel, False),
         [half, own],
-        [VMEM, HBM] + [VMEM] * 4,
-        (r, c, taps, before, after, x),
+        [HBM] * 3 + [VMEM] * 3,
+        (r, c, x, taps, before, after),
         10**11,
         16,
         scratch=[
             *fine_scratch,
             pltpu.VMEM(*own),
+            pltpu.VMEM(r.shape, F32),
+            pltpu.VMEM(x.shape, BF16),
             pltpu.VMEM(rows_shape, BF16),
             pltpu.VMEM((levels, *band_shape), BF16),
-            pltpu.SemaphoreType.DMA,
+            pltpu.SemaphoreType.DMA((3,)),
         ],
     )
     fine, x_next = lax.optimization_barrier((fine, x_next))
     shares = call(
         partial_kernel,
         [shared],
-        [VMEM] * 6,
-        (x, fine, means, c_first, mix, lons),
+        [HBM] * 2 + [VMEM] * 4,
+        (x, c_first, fine, means, mix, lons),
         10**9,
         12,
+        scratch=[
+            pltpu.VMEM(x.shape, BF16),
+            pltpu.VMEM(c.shape, F32),
+            pltpu.SemaphoreType.DMA((12,)),
+        ],
     )
     arrived = exchange(shares, MEM)
     share = call(
         functools.partial(share_kernel, scale),
         [((TILES, 32, 128), F32)],
         [VMEM, VMEM],
-        (arrived, r),
+        (arrived, r_share),
         10**6,
         6,
     )
@@ -571,12 +635,11 @@
     )
     beside = edges(top, bottom)
     c = exchange(c, "tile")
-    level = ((height, LON), F32)
     fine, means, sums = call(
         functools.partial(fine_kernel, True),
         [level, own, ((8, 128), F32)],
         [VMEM] * 11,
-        (r, a, c_own, *beside, rows_next, band_next, *x_next),
+        (r_level, a, c_own, *beside, rows_next, band_next, *x_next),
         10**11,
         16,
         scratch=fine_scratch,
@@ -606,7 +669,7 @@
             functools.partial(final_kernel, scale),
             [out, out],
             [VMEM, VMEM],
-            (arrived, r),
+            (arrived, r_packed),
             10**6,
             6,
         )

time: 105 us -> 105 us (level)
  local copies, waits for them, and re-layouts: 2.6 us -> 0.02 us
  Pallas kernels: 16.6 us -> 18.5 us
    unnamed x26 -> x12, local copies, waits for them, and re-layouts: 2.6 us -> 0.02 us
    pallas_call x10, Pallas kernels: 16.6 us -> 18.5 us  [call(): pl.pallas_call(kernel, out_shape=shapes if len(shapes) > 1 else shapes[0]...]
  transfers between devices with their start and end apart: 9 -> 9, of which waited for: 5 -> 4; matrix products, arithmetic and copies ran while one was open for 0% -> 0% of each run, Pallas kernels for 8% -> 9%
where the time goes in v6:
time: 105 us; the launch traced here: 104 us
  blocking collectives  53.3 us (51%)
  starting transfers between devices  23.2 us (22%)
  Pallas kernels  18.5 us (18%)
  waiting for transfers between devices  8.61 us (8%)
    all_to_all x4, blocking collectives, exchange(): return lax.all_to_all(blocks, axis, 0, 0, tiled=True)  53.3 us
    pallas_call x10, Pallas kernels, call(): pl.pallas_call(kernel, out_shape=shapes if len(shapes) > 1 else shapes[0]...  18.5 us
    ppermute x4, starting transfers between devices, edges(): return (lax.ppermute(bottom, 'tile', up), lax.ppermute(top, 'tile', down))  9.25 us
    all_to_all x2, starting transfers between devices, exchange(): return lax.all_to_all(blocks, axis, 0, 0, tiled=True)  8.86 us
    all_to_all x2, waiting for transfers between devices, exchange(): return lax.all_to_all(blocks, axis, 0, 0, tiled=True)  6.04 us
    ppermute x3, starting transfers between devices, local(): x_next[ahead] = lax.ppermute(x_next[ahead], 'mem_0', ring)  5.05 us
    ppermute x4, waiting for transfers between devices, edges(): return (lax.ppermute(bottom, 'tile', up), lax.ppermute(top, 'tile', down))  2.56 us
  transfers between devices with their start and end apart: 9, of which 4 were waited for; matrix products, arithmetic and copies ran while one was open for 0% of the time, Pallas kernels for 9%

profile of v6, /device:TPU:1, one launch (start us, length us, event | category | flops | bytes accessed | tf_op | source)
XLA Modules:
  0.0 104.3 jit_solution(17238125055976292820)
XLA Ops:
  0.6 2.9 %shard_map.68 = (f32[8,8,1024]{2,1,0:T(8,128)S(1)}, f32[8,8,1024]{2,1,0:T(8,128)S(1)}, f32[8,64,256]{2,1,0:T(8,128)}) custom-call(bf16[256,1024]{1,0:T(8,128)(2,1)} %bitcast.12, f32[128,1024]{1,0:T(8,128)} %bitcast.9), custom_call_target="tpu_custom_call" | custom-call | flops 1000000000 | bytes 1048576 | tf_op jit(solution)/shard_map/pallas_call | solution.py:506
  3.6 2.5 %collective-permute-start = (f32[8,8,1024]{2,1,0:T(8,128)S(1)}, f32[8,8,1024]{2,1,0:T(8,128)S(1)}, u32[]{:S(2)}, u32[]{:S(2)}) collective-permute-start(f32[8,8,1024]{2,1,0:T(8,128)S(1)} %get-tuple-element.35), channel_id=1, source_target_pairs={{0,1},{1,2},{2,3},{3,4},{4,5},{5,6},{6,7},{7,0},{8,9},{9,10},{10,1... | collective-permute-start | bytes 786440 | tf_op jit(solution)/shard_map/ppermute | solution.py:534
  6.1 4.0 %collective-permute-start.1 = (f32[8,8,1024]{2,1,0:T(8,128)S(1)}, f32[8,8,1024]{2,1,0:T(8,128)S(1)}, u32[]{:S(2)}, u32[]{:S(2)}) collective-permute-start(f32[8,8,1024]{2,1,0:T(8,128)S(1)} %get-tuple-element.42), channel_id=1, source_target_pairs={{1,0},{2,1},{3,2},{4,3},{5,4},{6,5},{7,6},{0,7},{9,8},{10,9},{11,1... | collective-permute-start | bytes 786440 | tf_op jit(solution)/shard_map/ppermute | solution.py:534
  10.1 0.0 copy-start.1
  10.1 0.0 copy-start.2
  10.1 0.0 copy-start.3
  10.1 5.3 %all-to-all-start = ((f32[8,64,256]{2,1,0:T(8,128)}), f32[8,64,256]{2,1,0:T(8,128)}, u32[]{:S(2)}, u32[]{:S(2)}) async-start(f32[8,64,256]{2,1,0:T(8,128)} %get-tuple-element.38.refs_1_), calls=%async_computation | async-start | bytes 1048576 | tf_op jit(solution)/shard_map/all_to_all | solution.py:518
  15.5 0.6 collective-permute-done.refs_4_
  16.1 0.0 copy-done.1
  16.1 0.0 copy-done.2
  16.1 0.0 copy-done.3
  16.1 2.1 %shard_map.69 = (bf16[2,64,512]{2,1,0:T(8,128)(2,1)S(1)}, bf16[2,256,256]{2,1,0:T(8,128)(2,1)S(1)}, f32[32,128]{1,0:T(8,128)S(1)}, f32[32,1024]{1,0:T(8,128)S(1)...) custom-call(bf16[256,1024]{1,0:T(8,128)(2,1)} %bitcast.13, ...), custom_call_target="tpu_custom_call" | custom-call | flops 99999997952 | bytes 1327264 | tf_op jit(solution)/shard_map/pallas_call | solution.py:506
  18.2 1.4 %collective-permute-start.2 = (bf16[64,1024]{1,0:T(8,128)(2,1)S(1)}, bf16[64,1024]{1,0:T(8,128)(2,1)S(1)}, u32[]{:S(2)}, u32[]{:S(2)}) collective-permute-start(bf16[64,1024]{1,0:T(8,128)(2,1)S(1)} %get-tuple-element.45), channel_id=1, source_target_pairs={{0,64},{64,128},{128,192},{192,0},{1,65},{65,129},{129,193},{193,1... | collective-permute-start | bytes 393224 | tf_op jit(solution)/shard_map/ppermute | solution.py:584
  19.6 2.6 %collective-permute-start.3 = (bf16[64,1024]{1,0:T(8,128)(2,1)S(1)}, bf16[64,1024]{1,0:T(8,128)(2,1)S(1)}, u32[]{:S(2)}, u32[]{:S(2)}) collective-permute-start(bf16[64,1024]{1,0:T(8,128)(2,1)S(1)} %get-tuple-element.46), channel_id=1, source_target_pairs={{0,128},{64,192},{128,0},{192,64},{1,129},{65,193},{129,1},{193,65... | collective-permute-start | bytes 393224 | tf_op jit(solution)/shard_map/ppermute | solution.py:584
  22.2 1.1 %collective-permute-start.4 = (bf16[64,1024]{1,0:T(8,128)(2,1)S(1)}, bf16[64,1024]{1,0:T(8,128)(2,1)S(1)}, u32[]{:S(2)}, u32[]{:S(2)}) collective-permute-start(bf16[64,1024]{1,0:T(8,128)(2,1)S(1)} %get-tuple-element.47), channel_id=1, source_target_pairs={{0,192},{64,0},{128,64},{192,128},{1,193},{65,1},{129,65},{193,129... | collective-permute-start | bytes 393224 | tf_op jit(solution)/shard_map/ppermute | solution.py:584
  23.3 0.0 collective-permute-done.1.refs_5_
  23.3 4.6 %shard_map.70 = (f32[128,1024]{1,0:T(8,128)S(1)}, f32[64,256]{1,0:T(8,128)S(1)}) custom-call(f32[128,1024]{1,0:T(8,128)} %bitcast.11, f32[8,64,256]{2,1,0:T(8,128)} %get-tuple-element.38.refs_1_, bf16[256,1024]{1,0:T(8,128)(2,1)} %bitcast.14, f32[8,5]{1,0:T(8,128)S(1)} %bitcast.8, f32[8,8,1024]{2,1,0:T(8,128)S(1)} %collective-permute-done.refs_4_, ...), custom_call_target="tpu_custom_call" | custom-call | flops 99999997952 | bytes 2097312 | tf_op jit(solution)/shard_map/pallas_call | solution.py:506
  27.9 0.0 collective-permute-done.2.refs_1_.refs_8_
  27.9 0.0 collective-permute-done.3.refs_2_.refs_9_
  27.9 0.0 collective-permute-done.4.refs_3_.refs_10_
  27.9 4.1 %all-to-all-done.c_hbm = f32[8,64,256]{2,1,0:T(8,128)} async-done(((f32[8,64,256]{2,1,0:T(8,128)}), f32[8,64,256]{2,1,0:T(8,128)}, u32[]{:S(2)}, u32[]{:S(2)}) %all-to-all-start) | async-done | bytes 524320 | tf_op jit(solution)/shard_map/all_to_all | solution.py:518
  32.0 2.3 %shard_map.71 = f32[32,32,128]{2,1,0:T(8,128)S(1)} custom-call(bf16[256,1024]{1,0:T(8,128)(2,1)} %bitcast.15, f32[8,64,256]{2,1,0:T(8,128)} %all-to-all-done.c_hbm, f32[128,1024]{1,0:T(8,128)S(1)} %get-tuple-element.48.fine_ref, f32[64,256]{1,0:T(8,128)S(1)} %get-tuple-element.49.mean_ref, bf16[2,64,512]{2,1,0:T(8,128)(2,1)S(1)} %get-tuple-element.50.mix_ref, ...), custom_call_target="tpu_custom_call" | custom-call | flops 1000000000 | bytes 2031616 | tf_op jit(solution)/shard_map/pallas_call | solution.py:506
  34.3 20.5 %all_to_all.30.arrived_ref = f32[32,32,128]{2,1,0:T(8,128)S(1)} all-to-all(f32[32,32,128]{2,1,0:T(8,128)S(1)} %shard_map.71), channel_id=1, replica_groups=mesh['mem_0'=4,'mem_1'=4,'mem_2'=2,'tile'=8] {'mem_0','mem_1','mem_2'}, dimensions={0} | all-to-all | bytes 1048576 | tf_op jit(solution)/shard_map/all_to_all | solution.py:518
  54.9 8.1 %all_to_all.31.v_ref.refs_1_ = f32[8,32,128]{2,1,0:T(8,128)S(1)} all-to-all(f32[8,32,128]{2,1,0:T(8,128)S(1)} %shard_map.72), channel_id=1, replica_groups=mesh['mem_0'=4,'mem_1'=4,'mem_2'=2,'tile'=8] {'mem_1','mem_2'}, dimensions={0} | all-to-all | bytes 262144 | tf_op jit(solution)/shard_map/all_to_all | solution.py:518
  63.0 0.0 copy-start.5
  63.0 1.4 %shard_map.73 = (f32[8,8,1024]{2,1,0:T(8,128)S(1)}, f32[8,8,1024]{2,1,0:T(8,128)S(1)}, f32[8,8,256]{2,1,0:T(8,128)}, f32[64,256]{1,0:T(8,128)S(1)}) custom-call(f32[8,32,128]{2,1,0:T(8,128)S(1)} %all_to_all.31.v_ref.refs_1_, bf16[64,1024]{1,0:T(8,128)(2,1)S(1)} %get-tuple-element.53.refs_0_.refs_7_, ...), custom_call_target="tpu_custom_call" | custom-call | flops 1000000000 | bytes 655360 | tf_op jit(solution)/shard_map/pallas_call | solution.py:506
  64.3 0.0 copy-start.4
  64.3 0.3 collective-permute-start.5
  64.6 2.4 %collective-permute-start.6 = (f32[8,8,1024]{2,1,0:T(8,128)S(1)}, f32[8,8,1024]{2,1,0:T(8,128)S(1)}, u32[]{:S(2)}, u32[]{:S(2)}) collective-permute-start(f32[8,8,1024]{2,1,0:T(8,128)S(1)} %get-tuple-element.59), channel_id=1, source_target_pairs={{1,0},{2,1},{3,2},{4,3},{5,4},{6,5},{7,6},{0,7},{9,8},{10,9},{11,1... | collective-permute-start | bytes 786440 | tf_op jit(solution)/shard_map/ppermute | solution.py:534
  67.0 3.5 %all-to-all-start.3 = ((f32[8,8,256]{2,1,0:T(8,128)}), f32[8,8,256]{2,1,0:T(8,128)S(1)}, u32[]{:S(2)}, u32[]{:S(2)}) async-start(f32[8,8,256]{2,1,0:T(8,128)} %get-tuple-element.64), calls=%async_computation.3 | async-start | bytes 131072 | tf_op jit(solution)/shard_map/all_to_all | solution.py:518
  70.5 1.9 %collective-permute-done.5.refs_3_ = f32[8,8,1024]{2,1,0:T(8,128)S(1)} collective-permute-done((f32[8,8,1024]{2,1,0:T(8,128)S(1)}, f32[8,8,1024]{2,1,0:T(8,128)S(1)}, u32[]{:S(2)}, u32[]{:S(2)}) %collective-permute-start.5) | collective-permute-done | bytes 262176 | tf_op jit(solution)/shard_map/ppermute | solution.py:534
  72.5 0.0 collective-permute-done.6.refs_4_
  72.5 0.0 copy-done.5
  72.5 0.0 copy-done.4
  72.5 0.0 copy-start
  72.5 3.0 %shard_map.74 = (f32[32,1024]{1,0:T(8,128)S(1)}, f32[64,256]{1,0:T(8,128)S(1)}, f32[8,128]{1,0:T(8,128)S(1)}) custom-call(f32[32,1024]{1,0:T(8,128)S(1)} %get-tuple-element.37.refs_0_, f32[8,32,128]{2,1,0:T(8,128)S(1)} %all_to_all.31.v_ref.refs_1_, f32[64,256]{1,0:T(8,128)S(1)} %get-tuple-element.57.refs_2_, ...), custom_call_target="tpu_custom_call" | custom-call | flops 99999997952 | bytes 1556480 | tf_op jit(solution)/shard_map/pallas_call | solution.py:506
  75.5 2.0 %all-to-all-done.3.c_ref = f32[8,8,256]{2,1,0:T(8,128)S(1)} async-done(((f32[8,8,256]{2,1,0:T(8,128)}), f32[8,8,256]{2,1,0:T(8,128)S(1)}, u32[]{:S(2)}, u32[]{:S(2)}) %all-to-all-start.3) | async-done | bytes 65568 | tf_op jit(solution)/shard_map/all_to_all | solution.py:518
  77.5 0.0 copy-done
  77.5 0.5 shard_map.75
  78.0 10.0 %all_to_all.32.smoothed_ref = f32[8,24,128]{2,1,0:T(8,128)S(1)} all-to-all(f32[8,24,128]{2,1,0:T(8,128)S(1)} %shard_map.75), channel_id=1, replica_groups=mesh['mem_0'=4,'mem_1'=4,'mem_2'=2,'tile'=8] {'tile'}, dimensions={0} | all-to-all | bytes 196608 | tf_op jit(solution)/shard_map/all_to_all | solution.py:518
  87.9 0.7 shard_map.76
  88.6 14.8 %all_to_all.33 = f32[32,1,1280]{2,1,0:T(1,128)S(1)} all-to-all(f32[32,1,1280]{2,1,0:T(1,128)S(1)} %bitcast.6), channel_id=1, replica_groups=mesh['mem_0'=4,'mem_1'=4,'mem_2'=2,'tile'=8] {'mem_0','mem_1','mem_2'}, dimensions={0} | all-to-all | bytes 327680 | tf_op jit(solution)/shard_map/all_to_all | solution.py:518
  103.4 0.9 shard_map.77
  (1 shorter events, 0.0 us)
Async XLA Ops:
  3.6 12.5 %collective-permute-start = (f32[8,8,1024]{2,1,0:T(8,128)S(1)}, f32[8,8,1024]{2,1,0:T(8,128)S(1)}, u32[]{:S(2)}, u32[]{:S(2)}) collective-permute-start(f32[8,8,1024]{2,1,0:T(8,128)S(1)} %get-tuple-element.35), channel_id=1, source_target_pairs={{0,1},{1,2},{2,3},{3,4},{4,5},{5,6},{6,7},{7,0},{8,9},{9,10},{10,1... | collective-permute-start | bytes 786440 | tf_op jit(solution)/shard_map/ppermute | solution.py:534
  6.1 17.2 %collective-permute-start.1 = (f32[8,8,1024]{2,1,0:T(8,128)S(1)}, f32[8,8,1024]{2,1,0:T(8,128)S(1)}, u32[]{:S(2)}, u32[]{:S(2)}) collective-permute-start(f32[8,8,1024]{2,1,0:T(8,128)S(1)} %get-tuple-element.42), channel_id=1, source_target_pairs={{1,0},{2,1},{3,2},{4,3},{5,4},{6,5},{7,6},{0,7},{9,8},{10,9},{11,1... | collective-permute-start | bytes 786440 | tf_op jit(solution)/shard_map/ppermute | solution.py:534
  10.1 5.9 %copy-start.1 = (f32[256,256]{1,0:T(8,128)S(1)}, f32[256,256]{1,0:T(8,128)}, u32[]{:S(2)}) copy-start(f32[256,256]{1,0:T(8,128)} %lon_ref.1) | copy-start | bytes 786436
  10.1 5.9 %copy-start.2 = (f32[64,64]{1,0:T(8,128)S(1)}, f32[64,64]{1,0:T(8,128)}, u32[]{:S(2)}) copy-start(f32[64,64]{1,0:T(8,128)} %lat_ref.1) | copy-start | bytes 49156
  10.1 5.9 %copy-start.3 = (f32[2,4,5]{2,1,0:T(4,128)S(1)}, f32[2,4,5]{2,1,0:T(4,128)}, u32[]{:S(2)}) copy-start(f32[2,4,5]{2,1,0:T(4,128)} %param.7) | copy-start | bytes 484
  10.1 21.8 %all-to-all-start = ((f32[8,64,256]{2,1,0:T(8,128)}), f32[8,64,256]{2,1,0:T(8,128)}, u32[]{:S(2)}, u32[]{:S(2)}) async-start(f32[8,64,256]{2,1,0:T(8,128)} %get-tuple-element.38.refs_1_), calls=%async_computation | async-start | bytes 1048576 | tf_op jit(solution)/shard_map/all_to_all | solution.py:518
  18.2 9.6 %collective-permute-start.2 = (bf16[64,1024]{1,0:T(8,128)(2,1)S(1)}, bf16[64,1024]{1,0:T(8,128)(2,1)S(1)}, u32[]{:S(2)}, u32[]{:S(2)}) collective-permute-start(bf16[64,1024]{1,0:T(8,128)(2,1)S(1)} %get-tuple-element.45), channel_id=1, source_target_pairs={{0,64},{64,128},{128,192},{192,0},{1,65},{65,129},{129,193},{193,1... | collective-permute-start | bytes 393224 | tf_op jit(solution)/shard_map/ppermute | solution.py:584
  19.6 8.3 %collective-permute-start.3 = (bf16[64,1024]{1,0:T(8,128)(2,1)S(1)}, bf16[64,1024]{1,0:T(8,128)(2,1)S(1)}, u32[]{:S(2)}, u32[]{:S(2)}) collective-permute-start(bf16[64,1024]{1,0:T(8,128)(2,1)S(1)} %get-tuple-element.46), channel_id=1, source_target_pairs={{0,128},{64,192},{128,0},{192,64},{1,129},{65,193},{129,1},{193,65... | collective-permute-start | bytes 393224 | tf_op jit(solution)/shard_map/ppermute | solution.py:584
  22.2 5.7 %collective-permute-start.4 = (bf16[64,1024]{1,0:T(8,128)(2,1)S(1)}, bf16[64,1024]{1,0:T(8,128)(2,1)S(1)}, u32[]{:S(2)}, u32[]{:S(2)}) collective-permute-start(bf16[64,1024]{1,0:T(8,128)(2,1)S(1)} %get-tuple-element.47), channel_id=1, source_target_pairs={{0,192},{64,0},{128,64},{192,128},{1,193},{65,1},{129,65},{193,129... | collective-permute-start | bytes 393224 | tf_op jit(solution)/shard_map/ppermute | solution.py:584
  63.0 9.5 %copy-start.5 = (bf16[1,2,160,128]{3,2,1,0:T(8,128)(2,1)S(1)}, bf16[1,2,160,128]{3,2,1,0:T(8,128)(2,1)}, u32[]{:S(2)}) copy-start(bf16[1,2,160,128]{3,2,1,0:T(8,128)(2,1)} %get-tuple-element.61.refs_6_) | copy-start | bytes 245764
  64.3 8.2 %copy-start.4 = (bf16[2,128,192]{2,1,0:T(8,128)(2,1)S(1)}, bf16[2,128,192]{2,1,0:T(8,128)(2,1)}, u32[]{:S(2)}) copy-start(bf16[2,128,192]{2,1,0:T(8,128)(2,1)} %get-tuple-element.60.refs_5_) | copy-start | bytes 294916
  64.3 8.2 %collective-permute-start.5 = (f32[8,8,1024]{2,1,0:T(8,128)S(1)}, f32[8,8,1024]{2,1,0:T(8,128)S(1)}, u32[]{:S(2)}, u32[]{:S(2)}) collective-permute-start(f32[8,8,1024]{2,1,0:T(8,128)S(1)} %get-tuple-element.58), channel_id=1, source_target_pairs={{0,1},{1,2},{2,3},{3,4},{4,5},{5,6},{6,7},{7,0},{8,9},{9,10},{10,1... | collective-permute-start | bytes 786440 | tf_op jit(solution)/shard_map/ppermute | solution.py:534
  64.6 7.9 %collective-permute-start.6 = (f32[8,8,1024]{2,1,0:T(8,128)S(1)}, f32[8,8,1024]{2,1,0:T(8,128)S(1)}, u32[]{:S(2)}, u32[]{:S(2)}) collective-permute-start(f32[8,8,1024]{2,1,0:T(8,128)S(1)} %get-tuple-element.59), channel_id=1, source_target_pairs={{1,0},{2,1},{3,2},{4,3},{5,4},{6,5},{7,6},{0,7},{9,8},{10,9},{11,1... | collective-permute-start | bytes 786440 | tf_op jit(solution)/shard_map/ppermute | solution.py:534
  67.0 10.5 %all-to-all-start.3 = ((f32[8,8,256]{2,1,0:T(8,128)}), f32[8,8,256]{2,1,0:T(8,128)S(1)}, u32[]{:S(2)}, u32[]{:S(2)}) async-start(f32[8,8,256]{2,1,0:T(8,128)} %get-tuple-element.64), calls=%async_computation.3 | async-start | bytes 131072 | tf_op jit(solution)/shard_map/all_to_all | solution.py:518
  72.5 5.0 %copy-start = (bf16[2,64,64]{2,1,0:T(8,128)(2,1)S(1)}, bf16[2,64,64]{2,1,0:T(8,128)(2,1)}, u32[]{:S(2)}) copy-start(bf16[2,64,64]{2,1,0:T(8,128)(2,1)} %get-tuple-element.65.lats_ref) | copy-start | bytes 49156

commit v7 on v6

--- a/solution.py
+++ b/solution.py
@@ -33,13 +33,6 @@
     return mm(a[0], b[0]) + mm(a[0], b[1]) + mm(a[1], b[0])
 
 
-def split3(x):
-    high = x.astype(BF16)
-    rest = x - high.astype(F32)
-    mid = rest.astype(BF16)
-    return high, mid, (rest - mid.astype(F32)).astype(BF16)
-
-
 def iotas(rows, cols):
     return (
         lax.broadcasted_iota(jnp.int32, (rows, cols), 0),
@@ -59,12 +52,15 @@
     return jnp.where(hit, 1.0, 0.0).astype(BF16)
 
 
-def block_mean(halves, split):
-    table = shrink_table(32, 128, False)
-    parts = [sum(mm(table, piece) for piece in split(half)) for half in halves]
+def lat_mean(field):
+    table = shrink_table(field.shape[0] // 4, field.shape[0], False)
+    return sum(mm(table, piece) for piece in split2(field))
+
+
+def lon_mean(parts):
     stacked = jnp.concatenate([part[:, k : k + 512] for k in (0, 512) for part in parts], axis=0)
     table = shrink_table(512, 128, True)
-    small = sum(mm(piece, table) for piece in split(stacked))
+    small = sum(mm(piece, table) for piece in split2(stacked))
     return jnp.concatenate([small[:64], small[64:]], axis=1)
 
 
@@ -105,41 +101,64 @@
 
 
 def detail_kernel(v_ref, *refs):
+    *x_refs, top_ref, bottom_ref, c_ref, own_ref = refs
     v = for_each(natural(v_ref))
-    detail([x.astype(F32) * v for x in halves_of(refs[:4])], *refs[4:])
-
-
-def first_detail_kernel(x_hbm, v_hbm, *refs):
-    *out_refs, x_ref, v_ref, x_sems, v_sems = refs
-    v_copies, x_copies = [], []
-    for k in range(8):
-        rows = pl.ds(16 * k, 16)
-        v_copies.append(pltpu.make_async_copy(v_hbm.at[rows], v_ref.at[rows], v_sems.at[k]))
-        rows = pl.ds(32 * k, 32)
-        x_copies.append(pltpu.make_async_copy(x_hbm.at[rows], x_ref.at[rows], x_sems.at[k]))
-    for copy in v_copies + x_copies:
+    halves = [x.astype(F32) * v for x in halves_of(x_refs)]
+    c = lon_mean([lat_mean(half) for half in halves])
+    c_ref[...] = c.reshape(PAIRS, 8, 256)
+    own_ref[...] = c
+    fields = [half[ROWS * k : ROWS * k + ROWS] for half in halves for k in range(4)]
+    fill_edges(fields, c, top_ref, bottom_ref)
+
+
+def first_detail_kernel(x_hbm, v_hbm, top_ref, bottom_ref, c_hbm, *refs):
+    x_ref, v_ref, c_ref, x_sems, v_sems, c_sems = refs
+    pieces = {}
+    for pair in range(2):
+        rows = [pl.ds(64 * pair + 32 * k, 32) for k in range(2)]
+        pieces[pair] = [
+            pltpu.make_async_copy(v_hbm.at[row], v_ref.at[row], v_sems.at[2 * pair + k])
+            for k, row in enumerate(rows)
+        ]
+        for member in range(2):
+            rows = [pl.ds(128 * member + 64 * pair + 32 * k, 32) for k in range(2)]
+            pieces[pair] += [
+                pltpu.make_async_copy(
+                    x_hbm.at[row], x_ref.at[row], x_sems.at[4 * pair + 2 * member + k]
+                )
+                for k, row in enumerate(rows)
+            ]
+    for pair in range(2):
+        for copy in pieces[pair]:
+            copy.start()
+    fields, parts = [None] * PAIRS, [None] * 4
+    for pair in range(2):
+        for copy in pieces[pair]:
+            copy.wait()
+        v = v_ref[64 * pair : 64 * pair + 64]
+        for member in range(2):
+            at = 128 * member + 64 * pair
+            w = x_ref[at : at + 64].astype(F32) * v
+            parts[2 * member + pair] = lat_mean(w)
+            for k in range(2):
+                fields[4 * member + 2 * pair + k] = w[ROWS * k : ROWS * k + ROWS]
+    c = lon_mean(parts)
+    c_ref[...] = c
+    copies = [
+        pltpu.make_async_copy(c_ref, c_hbm.at[tile], c_sems.at[tile]) for tile in range(TILES)
+    ]
+    for copy in copies:
         copy.start()
-    for copy in v_copies + x_copies[:4]:
+    fill_edges(fields, c, top_ref, bottom_ref)
+    for copy in copies:
         copy.wait()
-    first = x_ref[:128].astype(F32) * v_ref[...]
-    for copy in x_copies[4:]:
-        copy.wait()
-    detail([first, x_ref[128:].astype(F32) * v_ref[...]], *out_refs)
-
-
-def detail(halves, top_ref, bottom_ref, c_ref, own_ref=None):
-    c = block_mean(halves, split3)
-    if own_ref is None:
-        for tile in range(TILES):
-            c_ref[tile] = c
-    else:
-        c_ref[...] = c.reshape(PAIRS, 8, 256)
-        own_ref[...] = c
+
+
+def fill_edges(fields, c, top_ref, bottom_ref):
     spread = prolong(c, edges=True)
-    for pair in range(PAIRS):
-        w, at = halves[pair // 4], ROWS * (pair % 4)
-        top_ref[pair] = w[at : at + 8] - spread[16 * pair : 16 * pair + 8]
-        bottom_ref[pair] = w[at + 24 : at + 32] - spread[16 * pair + 8 : 16 * pair + 16]
+    for pair, w in enumerate(fields):
+        top_ref[pair] = w[:8] - spread[16 * pair : 16 * pair + 8]
+        bottom_ref[pair] = w[24:] - spread[16 * pair + 8 : 16 * pair + 16]
 
 
 def row_table(taps, tile):
@@ -369,7 +388,7 @@
                     term = halves[part][row : row + ROWS, lanes].astype(F32) * f
                     summed = term if summed is None else summed + term
             fine_ref[ROWS * level : ROWS * level + ROWS, lanes] = summed
-    means = block_mean((f_ref[:128], f_ref[128:]), split2)
+    means = lon_mean([lat_mean(f_ref[128 * k : 128 * k + 128]) for k in range(2)])
     mean_ref[...] = means
     if last:
         r = r_ref[...]
@@ -546,9 +565,12 @@
         scratch=(
             pltpu.VMEM((256, LON), BF16),
             pltpu.VMEM((128, LON), F32),
+            pltpu.VMEM(*own),
             pltpu.SemaphoreType.DMA((8,)),
-            pltpu.SemaphoreType.DMA((8,)),
+            pltpu.SemaphoreType.DMA((4,)),
+            pltpu.SemaphoreType.DMA((TILES,)),
         ),
+        out_specs=[VMEM, VMEM, HBM],
     )
     before, after = edges(top, bottom)
     c_first = exchange(c, "tile")

time: 105 us -> 104 us (level)
  no operation moved by 1% of the time
where the time goes in v7:
time: 104 us
  blocking collectives  53.3 us (51%)
  starting transfers between devices  23.2 us (22%)
  Pallas kernels  18.1 us (17%)
  waiting for transfers between devices  8.63 us (8%)
    all_to_all x4, blocking collectives, exchange(): return lax.all_to_all(blocks, axis, 0, 0, tiled=True)  53.3 us
    pallas_call x10, Pallas kernels, call(): pl.pallas_call(kernel, out_shape=shapes if len(shapes) > 1 else shapes[0]...  18.1 us
    ppermute x4, starting transfers between devices, edges(): return (lax.ppermute(bottom, 'tile', up), lax.ppermute(top, 'tile', down))  9.25 us
    all_to_all x2, starting transfers between devices, exchange(): return lax.all_to_all(blocks, axis, 0, 0, tiled=True)  8.86 us
    all_to_all x2, waiting for transfers between devices, exchange(): return lax.all_to_all(blocks, axis, 0, 0, tiled=True)  6.05 us
    ppermute x3, starting transfers between devices, local(): x_next[ahead] = lax.ppermute(x_next[ahead], 'mem_0', ring)  5.06 us
    ppermute x4, waiting for transfers between devices, edges(): return (lax.ppermute(bottom, 'tile', up), lax.ppermute(top, 'tile', down))  2.57 us
  transfers between devices with their start and end apart: 9, of which 4 were waited for; matrix products, arithmetic and copies ran while one was open for 0% of the time, Pallas kernels for 9%

profile of v7, /device:TPU:1, one launch (start us, length us, event | category | flops | bytes accessed | tf_op | source)
XLA Modules:
  0.0 104.0 jit_solution(5414482824430289387)
XLA Ops:
  0.6 2.8 %shard_map.68 = (f32[8,8,1024]{2,1,0:T(8,128)S(1)}, f32[8,8,1024]{2,1,0:T(8,128)S(1)}, f32[8,64,256]{2,1,0:T(8,128)}) custom-call(bf16[256,1024]{1,0:T(8,128)(2,1)} %bitcast.12, f32[128,1024]{1,0:T(8,128)} %bitcast.9), custom_call_target="tpu_custom_call" | custom-call | flops 1000000000 | bytes 1048576 | tf_op jit(solution)/shard_map/pallas_call | solution.py:525
  3.4 2.5 %collective-permute-start = (f32[8,8,1024]{2,1,0:T(8,128)S(1)}, f32[8,8,1024]{2,1,0:T(8,128)S(1)}, u32[]{:S(2)}, u32[]{:S(2)}) collective-permute-start(f32[8,8,1024]{2,1,0:T(8,128)S(1)} %get-tuple-element.35), channel_id=1, source_target_pairs={{0,1},{1,2},{2,3},{3,4},{4,5},{5,6},{6,7},{7,0},{8,9},{9,10},{10,1... | collective-permute-start | bytes 786440 | tf_op jit(solution)/shard_map/ppermute | solution.py:553
  5.9 4.0 %collective-permute-start.1 = (f32[8,8,1024]{2,1,0:T(8,128)S(1)}, f32[8,8,1024]{2,1,0:T(8,128)S(1)}, u32[]{:S(2)}, u32[]{:S(2)}) collective-permute-start(f32[8,8,1024]{2,1,0:T(8,128)S(1)} %get-tuple-element.42), channel_id=1, source_target_pairs={{1,0},{2,1},{3,2},{4,3},{5,4},{6,5},{7,6},{0,7},{9,8},{10,9},{11,1... | collective-permute-start | bytes 786440 | tf_op jit(solution)/shard_map/ppermute | solution.py:553
  10.0 0.0 copy-start.1
  10.0 0.0 copy-start.2
  10.0 0.0 copy-start.3
  10.0 5.3 %all-to-all-start = ((f32[8,64,256]{2,1,0:T(8,128)}), f32[8,64,256]{2,1,0:T(8,128)}, u32[]{:S(2)}, u32[]{:S(2)}) async-start(f32[8,64,256]{2,1,0:T(8,128)} %get-tuple-element.38.refs_1_), calls=%async_computation | async-start | bytes 1048576 | tf_op jit(solution)/shard_map/all_to_all | solution.py:537
  15.3 0.6 collective-permute-done.refs_4_
  15.9 0.0 copy-done.1
  15.9 0.0 copy-done.2
  15.9 0.0 copy-done.3
  15.9 2.1 %shard_map.69 = (bf16[2,64,512]{2,1,0:T(8,128)(2,1)S(1)}, bf16[2,256,256]{2,1,0:T(8,128)(2,1)S(1)}, f32[32,128]{1,0:T(8,128)S(1)}, f32[32,1024]{1,0:T(8,128)S(1)...) custom-call(bf16[256,1024]{1,0:T(8,128)(2,1)} %bitcast.13, ...), custom_call_target="tpu_custom_call" | custom-call | flops 99999997952 | bytes 1327264 | tf_op jit(solution)/shard_map/pallas_call | solution.py:525
  18.1 1.4 %collective-permute-start.2 = (bf16[64,1024]{1,0:T(8,128)(2,1)S(1)}, bf16[64,1024]{1,0:T(8,128)(2,1)S(1)}, u32[]{:S(2)}, u32[]{:S(2)}) collective-permute-start(bf16[64,1024]{1,0:T(8,128)(2,1)S(1)} %get-tuple-element.45), channel_id=1, source_target_pairs={{0,64},{64,128},{128,192},{192,0},{1,65},{65,129},{129,193},{193,1... | collective-permute-start | bytes 393224 | tf_op jit(solution)/shard_map/ppermute | solution.py:606
  19.4 2.6 %collective-permute-start.3 = (bf16[64,1024]{1,0:T(8,128)(2,1)S(1)}, bf16[64,1024]{1,0:T(8,128)(2,1)S(1)}, u32[]{:S(2)}, u32[]{:S(2)}) collective-permute-start(bf16[64,1024]{1,0:T(8,128)(2,1)S(1)} %get-tuple-element.46), channel_id=1, source_target_pairs={{0,128},{64,192},{128,0},{192,64},{1,129},{65,193},{129,1},{193,65... | collective-permute-start | bytes 393224 | tf_op jit(solution)/shard_map/ppermute | solution.py:606
  22.1 1.1 %collective-permute-start.4 = (bf16[64,1024]{1,0:T(8,128)(2,1)S(1)}, bf16[64,1024]{1,0:T(8,128)(2,1)S(1)}, u32[]{:S(2)}, u32[]{:S(2)}) collective-permute-start(bf16[64,1024]{1,0:T(8,128)(2,1)S(1)} %get-tuple-element.47), channel_id=1, source_target_pairs={{0,192},{64,0},{128,64},{192,128},{1,193},{65,1},{129,65},{193,129... | collective-permute-start | bytes 393224 | tf_op jit(solution)/shard_map/ppermute | solution.py:606
  23.1 0.0 collective-permute-done.1.refs_5_
  23.1 4.6 %shard_map.70 = (f32[128,1024]{1,0:T(8,128)S(1)}, f32[64,256]{1,0:T(8,128)S(1)}) custom-call(f32[128,1024]{1,0:T(8,128)} %bitcast.11, f32[8,64,256]{2,1,0:T(8,128)} %get-tuple-element.38.refs_1_, bf16[256,1024]{1,0:T(8,128)(2,1)} %bitcast.14, f32[8,5]{1,0:T(8,128)S(1)} %bitcast.8, f32[8,8,1024]{2,1,0:T(8,128)S(1)} %collective-permute-done.refs_4_, ...), custom_call_target="tpu_custom_call" | custom-call | flops 99999997952 | bytes 2097312 | tf_op jit(solution)/shard_map/pallas_call | solution.py:525
  27.7 0.0 collective-permute-done.2.refs_1_.refs_8_
  27.7 0.0 collective-permute-done.3.refs_2_.refs_9_
  27.7 0.0 collective-permute-done.4.refs_3_.refs_10_
  27.7 4.1 %all-to-all-done.c_hbm = f32[8,64,256]{2,1,0:T(8,128)} async-done(((f32[8,64,256]{2,1,0:T(8,128)}), f32[8,64,256]{2,1,0:T(8,128)}, u32[]{:S(2)}, u32[]{:S(2)}) %all-to-all-start) | async-done | bytes 524320 | tf_op jit(solution)/shard_map/all_to_all | solution.py:537
  31.8 2.3 %shard_map.71 = f32[32,32,128]{2,1,0:T(8,128)S(1)} custom-call(bf16[256,1024]{1,0:T(8,128)(2,1)} %bitcast.15, f32[8,64,256]{2,1,0:T(8,128)} %all-to-all-done.c_hbm, f32[128,1024]{1,0:T(8,128)S(1)} %get-tuple-element.48.fine_ref, f32[64,256]{1,0:T(8,128)S(1)} %get-tuple-element.49.mean_ref, bf16[2,64,512]{2,1,0:T(8,128)(2,1)S(1)} %get-tuple-element.50.mix_ref, ...), custom_call_target="tpu_custom_call" | custom-call | flops 1000000000 | bytes 2031616 | tf_op jit(solution)/shard_map/pallas_call | solution.py:525
  34.2 20.5 %all_to_all.30.arrived_ref = f32[32,32,128]{2,1,0:T(8,128)S(1)} all-to-all(f32[32,32,128]{2,1,0:T(8,128)S(1)} %shard_map.71), channel_id=1, replica_groups=mesh['mem_0'=4,'mem_1'=4,'mem_2'=2,'tile'=8] {'mem_0','mem_1','mem_2'}, dimensions={0} | all-to-all | bytes 1048576 | tf_op jit(solution)/shard_map/all_to_all | solution.py:537
  54.7 8.1 %all_to_all.31.v_ref.refs_1_ = f32[8,32,128]{2,1,0:T(8,128)S(1)} all-to-all(f32[8,32,128]{2,1,0:T(8,128)S(1)} %shard_map.72), channel_id=1, replica_groups=mesh['mem_0'=4,'mem_1'=4,'mem_2'=2,'tile'=8] {'mem_1','mem_2'}, dimensions={0} | all-to-all | bytes 262144 | tf_op jit(solution)/shard_map/all_to_all | solution.py:537
  62.8 0.0 copy-start.5
  62.8 1.2 %shard_map.73 = (f32[8,8,1024]{2,1,0:T(8,128)S(1)}, f32[8,8,1024]{2,1,0:T(8,128)S(1)}, f32[8,8,256]{2,1,0:T(8,128)}, f32[64,256]{1,0:T(8,128)S(1)}) custom-call(f32[8,32,128]{2,1,0:T(8,128)S(1)} %all_to_all.31.v_ref.refs_1_, bf16[64,1024]{1,0:T(8,128)(2,1)S(1)} %get-tuple-element.53.refs_0_.refs_7_, ...), custom_call_target="tpu_custom_call" | custom-call | flops 1000000000 | bytes 655360 | tf_op jit(solution)/shard_map/pallas_call | solution.py:525
  64.0 0.0 copy-start.4
  64.0 0.3 collective-permute-start.5
  64.3 2.4 %collective-permute-start.6 = (f32[8,8,1024]{2,1,0:T(8,128)S(1)}, f32[8,8,1024]{2,1,0:T(8,128)S(1)}, u32[]{:S(2)}, u32[]{:S(2)}) collective-permute-start(f32[8,8,1024]{2,1,0:T(8,128)S(1)} %get-tuple-element.59), channel_id=1, source_target_pairs={{1,0},{2,1},{3,2},{4,3},{5,4},{6,5},{7,6},{0,7},{9,8},{10,9},{11,1... | collective-permute-start | bytes 786440 | tf_op jit(solution)/shard_map/ppermute | solution.py:553
  66.7 3.5 %all-to-all-start.3 = ((f32[8,8,256]{2,1,0:T(8,128)}), f32[8,8,256]{2,1,0:T(8,128)S(1)}, u32[]{:S(2)}, u32[]{:S(2)}) async-start(f32[8,8,256]{2,1,0:T(8,128)} %get-tuple-element.64), calls=%async_computation.3 | async-start | bytes 131072 | tf_op jit(solution)/shard_map/all_to_all | solution.py:537
  70.2 2.0 %collective-permute-done.5.refs_3_ = f32[8,8,1024]{2,1,0:T(8,128)S(1)} collective-permute-done((f32[8,8,1024]{2,1,0:T(8,128)S(1)}, f32[8,8,1024]{2,1,0:T(8,128)S(1)}, u32[]{:S(2)}, u32[]{:S(2)}) %collective-permute-start.5) | collective-permute-done | bytes 262176 | tf_op jit(solution)/shard_map/ppermute | solution.py:553
  72.2 0.0 collective-permute-done.6.refs_4_
  72.2 0.0 copy-done.5
  72.2 0.0 copy-done.4
  72.2 0.0 copy-start
  72.2 3.0 %shard_map.74 = (f32[32,1024]{1,0:T(8,128)S(1)}, f32[64,256]{1,0:T(8,128)S(1)}, f32[8,128]{1,0:T(8,128)S(1)}) custom-call(f32[32,1024]{1,0:T(8,128)S(1)} %get-tuple-element.37.refs_0_, f32[8,32,128]{2,1,0:T(8,128)S(1)} %all_to_all.31.v_ref.refs_1_, f32[64,256]{1,0:T(8,128)S(1)} %get-tuple-element.57.refs_2_, ...), custom_call_target="tpu_custom_call" | custom-call | flops 99999997952 | bytes 1556480 | tf_op jit(solution)/shard_map/pallas_call | solution.py:525
  75.2 2.0 %all-to-all-done.3.c_ref = f32[8,8,256]{2,1,0:T(8,128)S(1)} async-done(((f32[8,8,256]{2,1,0:T(8,128)}), f32[8,8,256]{2,1,0:T(8,128)S(1)}, u32[]{:S(2)}, u32[]{:S(2)}) %all-to-all-start.3) | async-done | bytes 65568 | tf_op jit(solution)/shard_map/all_to_all | solution.py:537
  77.2 0.0 copy-done
  77.2 0.5 shard_map.75
  77.7 10.0 %all_to_all.32.smoothed_ref = f32[8,24,128]{2,1,0:T(8,128)S(1)} all-to-all(f32[8,24,128]{2,1,0:T(8,128)S(1)} %shard_map.75), channel_id=1, replica_groups=mesh['mem_0'=4,'mem_1'=4,'mem_2'=2,'tile'=8] {'tile'}, dimensions={0} | all-to-all | bytes 196608 | tf_op jit(solution)/shard_map/all_to_all | solution.py:537
  87.6 0.7 shard_map.76
  88.3 14.8 %all_to_all.33 = f32[32,1,1280]{2,1,0:T(1,128)S(1)} all-to-all(f32[32,1,1280]{2,1,0:T(1,128)S(1)} %bitcast.6), channel_id=1, replica_groups=mesh['mem_0'=4,'mem_1'=4,'mem_2'=2,'tile'=8] {'mem_0','mem_1','mem_2'}, dimensions={0} | all-to-all | bytes 327680 | tf_op jit(solution)/shard_map/all_to_all | solution.py:537
  103.1 0.9 shard_map.77
  (1 shorter events, 0.0 us)
Async XLA Ops:
  3.4 12.5 %collective-permute-start = (f32[8,8,1024]{2,1,0:T(8,128)S(1)}, f32[8,8,1024]{2,1,0:T(8,128)S(1)}, u32[]{:S(2)}, u32[]{:S(2)}) collective-permute-start(f32[8,8,1024]{2,1,0:T(8,128)S(1)} %get-tuple-element.35), channel_id=1, source_target_pairs={{0,1},{1,2},{2,3},{3,4},{4,5},{5,6},{6,7},{7,0},{8,9},{9,10},{10,1... | collective-permute-start | bytes 786440 | tf_op jit(solution)/shard_map/ppermute | solution.py:553
  5.9 17.2 %collective-permute-start.1 = (f32[8,8,1024]{2,1,0:T(8,128)S(1)}, f32[8,8,1024]{2,1,0:T(8,128)S(1)}, u32[]{:S(2)}, u32[]{:S(2)}) collective-permute-start(f32[8,8,1024]{2,1,0:T(8,128)S(1)} %get-tuple-element.42), channel_id=1, source_target_pairs={{1,0},{2,1},{3,2},{4,3},{5,4},{6,5},{7,6},{0,7},{9,8},{10,9},{11,1... | collective-permute-start | bytes 786440 | tf_op jit(solution)/shard_map/ppermute | solution.py:553
  10.0 5.9 %copy-start.1 = (f32[256,256]{1,0:T(8,128)S(1)}, f32[256,256]{1,0:T(8,128)}, u32[]{:S(2)}) copy-start(f32[256,256]{1,0:T(8,128)} %lon_ref.1) | copy-start | bytes 786436
  10.0 5.9 %copy-start.2 = (f32[64,64]{1,0:T(8,128)S(1)}, f32[64,64]{1,0:T(8,128)}, u32[]{:S(2)}) copy-start(f32[64,64]{1,0:T(8,128)} %lat_ref.1) | copy-start | bytes 49156
  10.0 5.9 %copy-start.3 = (f32[2,4,5]{2,1,0:T(4,128)S(1)}, f32[2,4,5]{2,1,0:T(4,128)}, u32[]{:S(2)}) copy-start(f32[2,4,5]{2,1,0:T(4,128)} %param.7) | copy-start | bytes 484
  10.0 21.8 %all-to-all-start = ((f32[8,64,256]{2,1,0:T(8,128)}), f32[8,64,256]{2,1,0:T(8,128)}, u32[]{:S(2)}, u32[]{:S(2)}) async-start(f32[8,64,256]{2,1,0:T(8,128)} %get-tuple-element.38.refs_1_), calls=%async_computation | async-start | bytes 1048576 | tf_op jit(solution)/shard_map/all_to_all | solution.py:537
  18.1 9.6 %collective-permute-start.2 = (bf16[64,1024]{1,0:T(8,128)(2,1)S(1)}, bf16[64,1024]{1,0:T(8,128)(2,1)S(1)}, u32[]{:S(2)}, u32[]{:S(2)}) collective-permute-start(bf16[64,1024]{1,0:T(8,128)(2,1)S(1)} %get-tuple-element.45), channel_id=1, source_target_pairs={{0,64},{64,128},{128,192},{192,0},{1,65},{65,129},{129,193},{193,1... | collective-permute-start | bytes 393224 | tf_op jit(solution)/shard_map/ppermute | solution.py:606
  19.4 8.3 %collective-permute-start.3 = (bf16[64,1024]{1,0:T(8,128)(2,1)S(1)}, bf16[64,1024]{1,0:T(8,128)(2,1)S(1)}, u32[]{:S(2)}, u32[]{:S(2)}) collective-permute-start(bf16[64,1024]{1,0:T(8,128)(2,1)S(1)} %get-tuple-element.46), channel_id=1, source_target_pairs={{0,128},{64,192},{128,0},{192,64},{1,129},{65,193},{129,1},{193,65... | collective-permute-start | bytes 393224 | tf_op jit(solution)/shard_map/ppermute | solution.py:606
  22.1 5.7 %collective-permute-start.4 = (bf16[64,1024]{1,0:T(8,128)(2,1)S(1)}, bf16[64,1024]{1,0:T(8,128)(2,1)S(1)}, u32[]{:S(2)}, u32[]{:S(2)}) collective-permute-start(bf16[64,1024]{1,0:T(8,128)(2,1)S(1)} %get-tuple-element.47), channel_id=1, source_target_pairs={{0,192},{64,0},{128,64},{192,128},{1,193},{65,1},{129,65},{193,129... | collective-permute-start | bytes 393224 | tf_op jit(solution)/shard_map/ppermute | solution.py:606
  62.8 9.4 %copy-start.5 = (bf16[1,2,160,128]{3,2,1,0:T(8,128)(2,1)S(1)}, bf16[1,2,160,128]{3,2,1,0:T(8,128)(2,1)}, u32[]{:S(2)}) copy-start(bf16[1,2,160,128]{3,2,1,0:T(8,128)(2,1)} %get-tuple-element.61.refs_6_) | copy-start | bytes 245764
  64.0 8.2 %copy-start.4 = (bf16[2,128,192]{2,1,0:T(8,128)(2,1)S(1)}, bf16[2,128,192]{2,1,0:T(8,128)(2,1)}, u32[]{:S(2)}) copy-start(bf16[2,128,192]{2,1,0:T(8,128)(2,1)} %get-tuple-element.60.refs_5_) | copy-start | bytes 294916
  64.0 8.2 %collective-permute-start.5 = (f32[8,8,1024]{2,1,0:T(8,128)S(1)}, f32[8,8,1024]{2,1,0:T(8,128)S(1)}, u32[]{:S(2)}, u32[]{:S(2)}) collective-permute-start(f32[8,8,1024]{2,1,0:T(8,128)S(1)} %get-tuple-element.58), channel_id=1, source_target_pairs={{0,1},{1,2},{2,3},{3,4},{4,5},{5,6},{6,7},{7,0},{8,9},{9,10},{10,1... | collective-permute-start | bytes 786440 | tf_op jit(solution)/shard_map/ppermute | solution.py:553
  64.3 7.9 %collective-permute-start.6 = (f32[8,8,1024]{2,1,0:T(8,128)S(1)}, f32[8,8,1024]{2,1,0:T(8,128)S(1)}, u32[]{:S(2)}, u32[]{:S(2)}) collective-permute-start(f32[8,8,1024]{2,1,0:T(8,128)S(1)} %get-tuple-element.59), channel_id=1, source_target_pairs={{1,0},{2,1},{3,2},{4,3},{5,4},{6,5},{7,6},{0,7},{9,8},{10,9},{11,1... | collective-permute-start | bytes 786440 | tf_op jit(solution)/shard_map/ppermute | solution.py:553
  66.7 10.5 %all-to-all-start.3 = ((f32[8,8,256]{2,1,0:T(8,128)}), f32[8,8,256]{2,1,0:T(8,128)S(1)}, u32[]{:S(2)}, u32[]{:S(2)}) async-start(f32[8,8,256]{2,1,0:T(8,128)} %get-tuple-element.64), calls=%async_computation.3 | async-start | bytes 131072 | tf_op jit(solution)/shard_map/all_to_all | solution.py:537
  72.2 5.0 %copy-start = (bf16[2,64,64]{2,1,0:T(8,128)(2,1)S(1)}, bf16[2,64,64]{2,1,0:T(8,128)(2,1)}, u32[]{:S(2)}) copy-start(bf16[2,64,64]{2,1,0:T(8,128)(2,1)} %get-tuple-element.65.lats_ref) | copy-start | bytes 49156

commit v8 on v7

--- a/solution.py
+++ b/solution.py
@@ -101,23 +101,26 @@
 
 
 def detail_kernel(v_ref, *refs):
-    *x_refs, top_ref, bottom_ref, c_ref, own_ref = refs
+    *x_refs, top_ref, bottom_ref, c_hbm, own_ref, c_ref, sem = refs
     v = for_each(natural(v_ref))
     halves = [x.astype(F32) * v for x in halves_of(x_refs)]
     c = lon_mean([lat_mean(half) for half in halves])
     c_ref[...] = c.reshape(PAIRS, 8, 256)
+    copy = pltpu.make_async_copy(c_ref, c_hbm, sem)
+    copy.start()
     own_ref[...] = c
     fields = [half[ROWS * k : ROWS * k + ROWS] for half in halves for k in range(4)]
     fill_edges(fields, c, top_ref, bottom_ref)
+    copy.wait()
 
 
 def first_detail_kernel(x_hbm, v_hbm, top_ref, bottom_ref, c_hbm, *refs):
     x_ref, v_ref, c_ref, x_sems, v_sems, c_sems = refs
     pieces = {}
     for pair in range(2):
-        rows = [pl.ds(64 * pair + 32 * k, 32) for k in range(2)]
+        rows = [pl.ds(64 * pair + 16 * k, 16) for k in range(4)]
         pieces[pair] = [
-            pltpu.make_async_copy(v_hbm.at[row], v_ref.at[row], v_sems.at[2 * pair + k])
+            pltpu.make_async_copy(v_hbm.at[row], v_ref.at[row], v_sems.at[4 * pair + k])
             for k, row in enumerate(rows)
         ]
         for member in range(2):
@@ -409,10 +412,8 @@
         out_ref[tile, 16:24, :] = sums
 
 
-def blended(x_refs, fine_ref, smoothed, loads=()):
+def blended(x_refs, fine_ref, smoothed):
     spread, height = prolong(smoothed), fine_ref.shape[0]
-    for load in loads:
-        load.wait()
     result = fine_ref[...]
     for k, x in enumerate(halves_of(x_refs)):
         product = x.astype(F32) * spread[128 * k : 128 * k + 128]
@@ -421,10 +422,9 @@
     return result
 
 
-def partial_kernel(x_hbm, c_hbm, fine_ref, mean_ref, mix_ref, lons_ref, out_ref, *refs):
-    x_ref, c_ref, sems = refs
+def partial_kernel(x_ref, c_hbm, fine_ref, mean_ref, mix_ref, lons_ref, out_ref, *refs):
+    c_ref, sems = refs
     spans = [(c_hbm, c_ref, k, 1) for k in range(TILES)]
-    spans += [(x_hbm, x_ref, 64 * k, 64) for k in range(4)]
     loads = [
         pltpu.make_async_copy(source.at[pl.ds(at, size)], target.at[pl.ds(at, size)], sems.at[k])
         for k, (source, target, at, size) in enumerate(spans)
@@ -440,7 +440,7 @@
         term = mm3((mix_ref[0, :, lanes], mix_ref[1, :, lanes]), split2(c))
         across = term if across is None else across + term
     smoothed = mm3(split2(across), (lons_ref[0], lons_ref[1])) - mean_ref[...]
-    p = blended((x_ref,), fine_ref, smoothed, loads[8:])
+    p = blended((x_ref,), fine_ref, smoothed)
     for tall in range(16):
         for wide in range(8):
             out_ref[2 * tall + wide // 4, 8 * (wide % 4) : 8 * (wide % 4) + 8, :] = p[
@@ -567,7 +567,7 @@
             pltpu.VMEM((128, LON), F32),
             pltpu.VMEM(*own),
             pltpu.SemaphoreType.DMA((8,)),
-            pltpu.SemaphoreType.DMA((4,)),
+            pltpu.SemaphoreType.DMA((8,)),
             pltpu.SemaphoreType.DMA((TILES,)),
         ),
         out_specs=[VMEM, VMEM, HBM],
@@ -626,14 +626,13 @@
     shares = call(
         partial_kernel,
         [shared],
-        [HBM] * 2 + [VMEM] * 4,
+        [VMEM, HBM] + [VMEM] * 4,
         (x, c_first, fine, means, mix, lons),
         10**9,
         12,
         scratch=[
-            pltpu.VMEM(x.shape, BF16),
             pltpu.VMEM(c.shape, F32),
-            pltpu.SemaphoreType.DMA((12,)),
+            pltpu.SemaphoreType.DMA((TILES,)),
         ],
     )
     arrived = exchange(shares, MEM)
@@ -654,6 +653,8 @@
         (a, *x_next),
         10**9,
         12,
+        scratch=[pltpu.VMEM((PAIRS, 8, 256), F32), pltpu.SemaphoreType.DMA],
+        out_specs=[VMEM, VMEM, HBM, VMEM],
     )
     beside = edges(top, bottom)
     c = exchange(c, "tile")

time: 104 us -> 104 us (level)
  no operation moved by 1% of the time
where the time goes in v8:
time: 104 us
  blocking collectives  53.3 us (51%)
  starting transfers between devices  23.2 us (22%)
  Pallas kernels  18 us (17%)
  waiting for transfers between devices  8.61 us (8%)
    all_to_all x4, blocking collectives, exchange(): return lax.all_to_all(blocks, axis, 0, 0, tiled=True)  53.3 us
    pallas_call x10, Pallas kernels, call(): pl.pallas_call(kernel, out_shape=shapes if len(shapes) > 1 else shapes[0]...  18 us
    ppermute x4, starting transfers between devices, edges(): return (lax.ppermute(bottom, 'tile', up), lax.ppermute(top, 'tile', down))  9.33 us
    all_to_all x2, starting transfers between devices, exchange(): return lax.all_to_all(blocks, axis, 0, 0, tiled=True)  8.86 us
    all_to_all x2, waiting for transfers between devices, exchange(): return lax.all_to_all(blocks, axis, 0, 0, tiled=True)  6.04 us
    ppermute x3, starting transfers between devices, local(): x_next[ahead] = lax.ppermute(x_next[ahead], 'mem_0', ring)  5.06 us
    ppermute x4, waiting for transfers between devices, edges(): return (lax.ppermute(bottom, 'tile', up), lax.ppermute(top, 'tile', down))  2.56 us
  transfers between devices with their start and end apart: 9, of which 4 were waited for; matrix products, arithmetic and copies ran while one was open for 0% of the time, Pallas kernels for 9%

profile of v8, /device:TPU:1, one launch (start us, length us, event | category | flops | bytes accessed | tf_op | source)
XLA Modules:
  0.0 103.9 jit_solution(3047935730720015142)
XLA Ops:
  0.6 2.7 %shard_map.68 = (f32[8,8,1024]{2,1,0:T(8,128)S(1)}, f32[8,8,1024]{2,1,0:T(8,128)S(1)}, f32[8,64,256]{2,1,0:T(8,128)}) custom-call(bf16[256,1024]{1,0:T(8,128)(2,1)} %bitcast.7, f32[128,1024]{1,0:T(8,128)} %bitcast.13), custom_call_target="tpu_custom_call" | custom-call | flops 1000000000 | bytes 1048576 | tf_op jit(solution)/shard_map/pallas_call | solution.py:525
  3.4 2.5 %collective-permute-start = (f32[8,8,1024]{2,1,0:T(8,128)S(1)}, f32[8,8,1024]{2,1,0:T(8,128)S(1)}, u32[]{:S(2)}, u32[]{:S(2)}) collective-permute-start(f32[8,8,1024]{2,1,0:T(8,128)S(1)} %get-tuple-element.35), channel_id=1, source_target_pairs={{0,1},{1,2},{2,3},{3,4},{4,5},{5,6},{6,7},{7,0},{8,9},{9,10},{10,1... | collective-permute-start | bytes 786440 | tf_op jit(solution)/shard_map/ppermute | solution.py:553
  5.9 4.0 %collective-permute-start.1 = (f32[8,8,1024]{2,1,0:T(8,128)S(1)}, f32[8,8,1024]{2,1,0:T(8,128)S(1)}, u32[]{:S(2)}, u32[]{:S(2)}) collective-permute-start(f32[8,8,1024]{2,1,0:T(8,128)S(1)} %get-tuple-element.42), channel_id=1, source_target_pairs={{1,0},{2,1},{3,2},{4,3},{5,4},{6,5},{7,6},{0,7},{9,8},{10,9},{11,1... | collective-permute-start | bytes 786440 | tf_op jit(solution)/shard_map/ppermute | solution.py:553
  9.9 0.0 copy-start.2
  9.9 0.0 copy-start.3
  9.9 0.0 copy-start.4
  9.9 5.3 %all-to-all-start = ((f32[8,64,256]{2,1,0:T(8,128)}), f32[8,64,256]{2,1,0:T(8,128)}, u32[]{:S(2)}, u32[]{:S(2)}) async-start(f32[8,64,256]{2,1,0:T(8,128)} %get-tuple-element.38.refs_1_), calls=%async_computation | async-start | bytes 1048576 | tf_op jit(solution)/shard_map/all_to_all | solution.py:537
  15.3 0.6 collective-permute-done.refs_4_
  15.9 0.0 copy-done.2
  15.9 0.0 copy-done.3
  15.9 0.0 copy-done.4
  15.9 2.1 %shard_map.69 = (bf16[2,64,512]{2,1,0:T(8,128)(2,1)S(1)}, bf16[2,256,256]{2,1,0:T(8,128)(2,1)S(1)}, f32[32,128]{1,0:T(8,128)S(1)}, f32[32,1024]{1,0:T(8,128)S(1)...) custom-call(bf16[256,1024]{1,0:T(8,128)(2,1)} %bitcast.8, ...), custom_call_target="tpu_custom_call" | custom-call | flops 99999997952 | bytes 1327264 | tf_op jit(solution)/shard_map/pallas_call | solution.py:525
  18.0 1.4 %collective-permute-start.2 = (bf16[64,1024]{1,0:T(8,128)(2,1)S(1)}, bf16[64,1024]{1,0:T(8,128)(2,1)S(1)}, u32[]{:S(2)}, u32[]{:S(2)}) collective-permute-start(bf16[64,1024]{1,0:T(8,128)(2,1)S(1)} %get-tuple-element.45), channel_id=1, source_target_pairs={{0,64},{64,128},{128,192},{192,0},{1,65},{65,129},{129,193},{193,1... | collective-permute-start | bytes 393224 | tf_op jit(solution)/shard_map/ppermute | solution.py:606
  19.4 2.6 %collective-permute-start.3 = (bf16[64,1024]{1,0:T(8,128)(2,1)S(1)}, bf16[64,1024]{1,0:T(8,128)(2,1)S(1)}, u32[]{:S(2)}, u32[]{:S(2)}) collective-permute-start(bf16[64,1024]{1,0:T(8,128)(2,1)S(1)} %get-tuple-element.46), channel_id=1, source_target_pairs={{0,128},{64,192},{128,0},{192,64},{1,129},{65,193},{129,1},{193,65... | collective-permute-start | bytes 393224 | tf_op jit(solution)/shard_map/ppermute | solution.py:606
  22.0 0.0 copy-start.1
  22.0 1.1 %collective-permute-start.4 = (bf16[64,1024]{1,0:T(8,128)(2,1)S(1)}, bf16[64,1024]{1,0:T(8,128)(2,1)S(1)}, u32[]{:S(2)}, u32[]{:S(2)}) collective-permute-start(bf16[64,1024]{1,0:T(8,128)(2,1)S(1)} %get-tuple-element.47), channel_id=1, source_target_pairs={{0,192},{64,0},{128,64},{192,128},{1,193},{65,1},{129,65},{193,129... | collective-permute-start | bytes 393224 | tf_op jit(solution)/shard_map/ppermute | solution.py:606
  23.1 0.0 collective-permute-done.1.refs_5_
  23.1 4.6 %shard_map.70 = (f32[128,1024]{1,0:T(8,128)S(1)}, f32[64,256]{1,0:T(8,128)S(1)}) custom-call(f32[128,1024]{1,0:T(8,128)} %bitcast.15, f32[8,64,256]{2,1,0:T(8,128)} %get-tuple-element.38.refs_1_, bf16[256,1024]{1,0:T(8,128)(2,1)} %bitcast.9, f32[8,5]{1,0:T(8,128)S(1)} %bitcast.12, f32[8,8,1024]{2,1,0:T(8,128)S(1)} %collective-permute-done.refs_4_, ...), custom_call_target="tpu_custom_call" | custom-call | flops 99999997952 | bytes 2097312 | tf_op jit(solution)/shard_map/pallas_call | solution.py:525
  27.7 0.0 collective-permute-done.2.refs_1_.refs_8_
  27.7 0.0 collective-permute-done.3.refs_2_.refs_9_
  27.7 0.0 collective-permute-done.4.refs_3_.refs_10_
  27.7 4.1 %all-to-all-done.c_hbm = f32[8,64,256]{2,1,0:T(8,128)} async-done(((f32[8,64,256]{2,1,0:T(8,128)}), f32[8,64,256]{2,1,0:T(8,128)}, u32[]{:S(2)}, u32[]{:S(2)}) %all-to-all-start) | async-done | bytes 524320 | tf_op jit(solution)/shard_map/all_to_all | solution.py:537
  31.8 0.0 copy-done.1
  31.8 2.2 %shard_map.71 = f32[32,32,128]{2,1,0:T(8,128)S(1)} custom-call(bf16[256,1024]{1,0:T(8,128)(2,1)S(1)} %bitcast.10, f32[8,64,256]{2,1,0:T(8,128)} %all-to-all-done.c_hbm, f32[128,1024]{1,0:T(8,128)S(1)} %get-tuple-element.48.fine_ref, f32[64,256]{1,0:T(8,128)S(1)} %get-tuple-element.49.mean_ref, bf16[2,64,512]{2,1,0:T(8,128)(2,1)S(1)} %get-tuple-element.50.mix_ref, ...), custom_call_target="tpu_custom_call" | custom-call | flops 1000000000 | bytes 2031616 | tf_op jit(solution)/shard_map/pallas_call | solution.py:525
  34.0 20.5 %all_to_all.30.arrived_ref = f32[32,32,128]{2,1,0:T(8,128)S(1)} all-to-all(f32[32,32,128]{2,1,0:T(8,128)S(1)} %shard_map.71), channel_id=1, replica_groups=mesh['mem_0'=4,'mem_1'=4,'mem_2'=2,'tile'=8] {'mem_0','mem_1','mem_2'}, dimensions={0} | all-to-all | bytes 1048576 | tf_op jit(solution)/shard_map/all_to_all | solution.py:537
  54.5 8.1 %all_to_all.31.v_ref.refs_1_ = f32[8,32,128]{2,1,0:T(8,128)S(1)} all-to-all(f32[8,32,128]{2,1,0:T(8,128)S(1)} %shard_map.72), channel_id=1, replica_groups=mesh['mem_0'=4,'mem_1'=4,'mem_2'=2,'tile'=8] {'mem_1','mem_2'}, dimensions={0} | all-to-all | bytes 262144 | tf_op jit(solution)/shard_map/all_to_all | solution.py:537
  62.6 0.0 copy-start.6
  62.6 1.2 %shard_map.73 = (f32[8,8,1024]{2,1,0:T(8,128)S(1)}, f32[8,8,1024]{2,1,0:T(8,128)S(1)}, f32[8,8,256]{2,1,0:T(8,128)}, f32[64,256]{1,0:T(8,128)S(1)}) custom-call(f32[8,32,128]{2,1,0:T(8,128)S(1)} %all_to_all.31.v_ref.refs_1_, bf16[64,1024]{1,0:T(8,128)(2,1)S(1)} %get-tuple-element.53.refs_0_.refs_7_, ...), custom_call_target="tpu_custom_call" | custom-call | flops 1000000000 | bytes 655360 | tf_op jit(solution)/shard_map/pallas_call | solution.py:525
  63.8 0.0 copy-start.5
  63.9 0.4 collective-permute-start.5
  64.2 2.4 %collective-permute-start.6 = (f32[8,8,1024]{2,1,0:T(8,128)S(1)}, f32[8,8,1024]{2,1,0:T(8,128)S(1)}, u32[]{:S(2)}, u32[]{:S(2)}) collective-permute-start(f32[8,8,1024]{2,1,0:T(8,128)S(1)} %get-tuple-element.59), channel_id=1, source_target_pairs={{1,0},{2,1},{3,2},{4,3},{5,4},{6,5},{7,6},{0,7},{9,8},{10,9},{11,1... | collective-permute-start | bytes 786440 | tf_op jit(solution)/shard_map/ppermute | solution.py:553
  66.6 3.5 %all-to-all-start.3 = ((f32[8,8,256]{2,1,0:T(8,128)}), f32[8,8,256]{2,1,0:T(8,128)S(1)}, u32[]{:S(2)}, u32[]{:S(2)}) async-start(f32[8,8,256]{2,1,0:T(8,128)} %get-tuple-element.64), calls=%async_computation.3 | async-start | bytes 131072 | tf_op jit(solution)/shard_map/all_to_all | solution.py:537
  70.1 1.9 %collective-permute-done.5.refs_3_ = f32[8,8,1024]{2,1,0:T(8,128)S(1)} collective-permute-done((f32[8,8,1024]{2,1,0:T(8,128)S(1)}, f32[8,8,1024]{2,1,0:T(8,128)S(1)}, u32[]{:S(2)}, u32[]{:S(2)}) %collective-permute-start.5) | collective-permute-done | bytes 262176 | tf_op jit(solution)/shard_map/ppermute | solution.py:553
  72.1 0.0 collective-permute-done.6.refs_4_
  72.1 0.0 copy-done.6
  72.1 0.0 copy-done.5
  72.1 0.0 copy-start
  72.1 3.0 %shard_map.74 = (f32[32,1024]{1,0:T(8,128)S(1)}, f32[64,256]{1,0:T(8,128)S(1)}, f32[8,128]{1,0:T(8,128)S(1)}) custom-call(f32[32,1024]{1,0:T(8,128)S(1)} %get-tuple-element.37.refs_0_, f32[8,32,128]{2,1,0:T(8,128)S(1)} %all_to_all.31.v_ref.refs_1_, f32[64,256]{1,0:T(8,128)S(1)} %get-tuple-element.57.refs_2_, ...), custom_call_target="tpu_custom_call" | custom-call | flops 99999997952 | bytes 1556480 | tf_op jit(solution)/shard_map/pallas_call | solution.py:525
  75.1 2.0 %all-to-all-done.3.c_ref = f32[8,8,256]{2,1,0:T(8,128)S(1)} async-done(((f32[8,8,256]{2,1,0:T(8,128)}), f32[8,8,256]{2,1,0:T(8,128)S(1)}, u32[]{:S(2)}, u32[]{:S(2)}) %all-to-all-start.3) | async-done | bytes 65568 | tf_op jit(solution)/shard_map/all_to_all | solution.py:537
  77.1 0.0 copy-done
  77.1 0.5 shard_map.75
  77.6 10.0 %all_to_all.32.smoothed_ref = f32[8,24,128]{2,1,0:T(8,128)S(1)} all-to-all(f32[8,24,128]{2,1,0:T(8,128)S(1)} %shard_map.75), channel_id=1, replica_groups=mesh['mem_0'=4,'mem_1'=4,'mem_2'=2,'tile'=8] {'tile'}, dimensions={0} | all-to-all | bytes 196608 | tf_op jit(solution)/shard_map/all_to_all | solution.py:537
  87.5 0.7 shard_map.76
  88.2 14.8 %all_to_all.33 = f32[32,1,1280]{2,1,0:T(1,128)S(1)} all-to-all(f32[32,1,1280]{2,1,0:T(1,128)S(1)} %bitcast.6), channel_id=1, replica_groups=mesh['mem_0'=4,'mem_1'=4,'mem_2'=2,'tile'=8] {'mem_0','mem_1','mem_2'}, dimensions={0} | all-to-all | bytes 327680 | tf_op jit(solution)/shard_map/all_to_all | solution.py:537
  103.0 0.9 shard_map.77
  (1 shorter events, 0.0 us)
Async XLA Ops:
  3.4 12.5 %collective-permute-start = (f32[8,8,1024]{2,1,0:T(8,128)S(1)}, f32[8,8,1024]{2,1,0:T(8,128)S(1)}, u32[]{:S(2)}, u32[]{:S(2)}) collective-permute-start(f32[8,8,1024]{2,1,0:T(8,128)S(1)} %get-tuple-element.35), channel_id=1, source_target_pairs={{0,1},{1,2},{2,3},{3,4},{4,5},{5,6},{6,7},{7,0},{8,9},{9,10},{10,1... | collective-permute-start | bytes 786440 | tf_op jit(solution)/shard_map/ppermute | solution.py:553
  5.9 17.2 %collective-permute-start.1 = (f32[8,8,1024]{2,1,0:T(8,128)S(1)}, f32[8,8,1024]{2,1,0:T(8,128)S(1)}, u32[]{:S(2)}, u32[]{:S(2)}) collective-permute-start(f32[8,8,1024]{2,1,0:T(8,128)S(1)} %get-tuple-element.42), channel_id=1, source_target_pairs={{1,0},{2,1},{3,2},{4,3},{5,4},{6,5},{7,6},{0,7},{9,8},{10,9},{11,1... | collective-permute-start | bytes 786440 | tf_op jit(solution)/shard_map/ppermute | solution.py:553
  9.9 5.9 %copy-start.2 = (f32[256,256]{1,0:T(8,128)S(1)}, f32[256,256]{1,0:T(8,128)}, u32[]{:S(2)}) copy-start(f32[256,256]{1,0:T(8,128)} %lon_ref.1) | copy-start | bytes 786436
  9.9 5.9 %copy-start.3 = (f32[64,64]{1,0:T(8,128)S(1)}, f32[64,64]{1,0:T(8,128)}, u32[]{:S(2)}) copy-start(f32[64,64]{1,0:T(8,128)} %lat_ref.1) | copy-start | bytes 49156
  9.9 5.9 %copy-start.4 = (f32[2,4,5]{2,1,0:T(4,128)S(1)}, f32[2,4,5]{2,1,0:T(4,128)}, u32[]{:S(2)}) copy-start(f32[2,4,5]{2,1,0:T(4,128)} %param.7) | copy-start | bytes 484
  9.9 21.8 %all-to-all-start = ((f32[8,64,256]{2,1,0:T(8,128)}), f32[8,64,256]{2,1,0:T(8,128)}, u32[]{:S(2)}, u32[]{:S(2)}) async-start(f32[8,64,256]{2,1,0:T(8,128)} %get-tuple-element.38.refs_1_), calls=%async_computation | async-start | bytes 1048576 | tf_op jit(solution)/shard_map/all_to_all | solution.py:537
  18.0 9.6 %collective-permute-start.2 = (bf16[64,1024]{1,0:T(8,128)(2,1)S(1)}, bf16[64,1024]{1,0:T(8,128)(2,1)S(1)}, u32[]{:S(2)}, u32[]{:S(2)}) collective-permute-start(bf16[64,1024]{1,0:T(8,128)(2,1)S(1)} %get-tuple-element.45), channel_id=1, source_target_pairs={{0,64},{64,128},{128,192},{192,0},{1,65},{65,129},{129,193},{193,1... | collective-permute-start | bytes 393224 | tf_op jit(solution)/shard_map/ppermute | solution.py:606
  19.4 8.3 %collective-permute-start.3 = (bf16[64,1024]{1,0:T(8,128)(2,1)S(1)}, bf16[64,1024]{1,0:T(8,128)(2,1)S(1)}, u32[]{:S(2)}, u32[]{:S(2)}) collective-permute-start(bf16[64,1024]{1,0:T(8,128)(2,1)S(1)} %get-tuple-element.46), channel_id=1, source_target_pairs={{0,128},{64,192},{128,0},{192,64},{1,129},{65,193},{129,1},{193,65... | collective-permute-start | bytes 393224 | tf_op jit(solution)/shard_map/ppermute | solution.py:606
  22.0 9.8 %copy-start.1 = (bf16[2,4,32,1024]{3,2,1,0:T(8,128)(2,1)S(1)}, bf16[2,4,32,1024]{3,2,1,0:T(8,128)(2,1)}, u32[]{:S(2)}) copy-start(bf16[2,4,32,1024]{3,2,1,0:T(8,128)(2,1)} %param.5) | copy-start | bytes 1572868
  22.0 5.7 %collective-permute-start.4 = (bf16[64,1024]{1,0:T(8,128)(2,1)S(1)}, bf16[64,1024]{1,0:T(8,128)(2,1)S(1)}, u32[]{:S(2)}, u32[]{:S(2)}) collective-permute-start(bf16[64,1024]{1,0:T(8,128)(2,1)S(1)} %get-tuple-element.47), channel_id=1, source_target_pairs={{0,192},{64,0},{128,64},{192,128},{1,193},{65,1},{129,65},{193,129... | collective-permute-start | bytes 393224 | tf_op jit(solution)/shard_map/ppermute | solution.py:606
  62.6 9.5 %copy-start.6 = (bf16[1,2,160,128]{3,2,1,0:T(8,128)(2,1)S(1)}, bf16[1,2,160,128]{3,2,1,0:T(8,128)(2,1)}, u32[]{:S(2)}) copy-start(bf16[1,2,160,128]{3,2,1,0:T(8,128)(2,1)} %get-tuple-element.61.refs_6_) | copy-start | bytes 245764
  63.8 8.3 %copy-start.5 = (bf16[2,128,192]{2,1,0:T(8,128)(2,1)S(1)}, bf16[2,128,192]{2,1,0:T(8,128)(2,1)}, u32[]{:S(2)}) copy-start(bf16[2,128,192]{2,1,0:T(8,128)(2,1)} %get-tuple-element.60.refs_5_) | copy-start | bytes 294916
  63.9 8.2 %collective-permute-start.5 = (f32[8,8,1024]{2,1,0:T(8,128)S(1)}, f32[8,8,1024]{2,1,0:T(8,128)S(1)}, u32[]{:S(2)}, u32[]{:S(2)}) collective-permute-start(f32[8,8,1024]{2,1,0:T(8,128)S(1)} %get-tuple-element.58), channel_id=1, source_target_pairs={{0,1},{1,2},{2,3},{3,4},{4,5},{5,6},{6,7},{7,0},{8,9},{9,10},{10,1... | collective-permute-start | bytes 786440 | tf_op jit(solution)/shard_map/ppermute | solution.py:553
  64.2 7.9 %collective-permute-start.6 = (f32[8,8,1024]{2,1,0:T(8,128)S(1)}, f32[8,8,1024]{2,1,0:T(8,128)S(1)}, u32[]{:S(2)}, u32[]{:S(2)}) collective-permute-start(f32[8,8,1024]{2,1,0:T(8,128)S(1)} %get-tuple-element.59), channel_id=1, source_target_pairs={{1,0},{2,1},{3,2},{4,3},{5,4},{6,5},{7,6},{0,7},{9,8},{10,9},{11,1... | collective-permute-start | bytes 786440 | tf_op jit(solution)/shard_map/ppermute | solution.py:553
  66.6 10.5 %all-to-all-start.3 = ((f32[8,8,256]{2,1,0:T(8,128)}), f32[8,8,256]{2,1,0:T(8,128)S(1)}, u32[]{:S(2)}, u32[]{:S(2)}) async-start(f32[8,8,256]{2,1,0:T(8,128)} %get-tuple-element.64), calls=%async_computation.3 | async-start | bytes 131072 | tf_op jit(solution)/shard_map/all_to_all | solution.py:537
  72.1 5.0 %copy-start = (bf16[2,64,64]{2,1,0:T(8,128)(2,1)S(1)}, bf16[2,64,64]{2,1,0:T(8,128)(2,1)}, u32[]{:S(2)}) copy-start(bf16[2,64,64]{2,1,0:T(8,128)(2,1)} %get-tuple-element.65.lats_ref) | copy-start | bytes 49156

commit v9 on v7

--- a/solution.py
+++ b/solution.py
@@ -348,7 +348,7 @@
         rows_ref, band_ref, *refs = refs
     x_refs, refs = (refs[:4], refs[4:]) if last else ((x_ref,), refs)
     if last:
-        fine_ref, mean_ref, sums_ref, f_ref = refs
+        fine_ref, mean_ref, sums_ref, lines_ref, f_ref, v_packed = refs
         v = natural(v_ref)
     else:
         fine_ref, mean_ref = refs
@@ -391,6 +391,11 @@
     means = lon_mean([lat_mean(f_ref[128 * k : 128 * k + 128]) for k in range(2)])
     mean_ref[...] = means
     if last:
+        for group, share in enumerate(packed(v)):
+            v_packed[group] = share
+        mine = pl.ds(own_group() & 7, 1)
+        for group in range(GROUPS):
+            lines_ref[group : group + 1] = v_packed[group, mine, :]
         r = r_ref[...]
         products = total(v * fine_ref[...]) - 16.0 * total(c_ref[...] * means)
         sums_ref[...] = lane_sums(
@@ -462,17 +467,14 @@
     return shares
 
 
-def last_partial_kernel(fine_ref, mean_ref, smoothed_ref, v_ref, *refs):
-    *x_refs, out_ref, v_packed = refs
+def last_partial_kernel(fine_ref, mean_ref, smoothed_ref, lines_ref, *refs):
+    *x_refs, out_ref = refs
     halves = [smoothed_ref[:, 8 * k : 8 * k + 8, :].reshape(64, 128) for k in range(2)]
     p = blended(x_refs, fine_ref, jnp.concatenate(halves, axis=1) - mean_ref[...])
     sums = jnp.sum(smoothed_ref[:, 16:24, :], axis=0)
-    for group, share in enumerate(packed(natural(v_ref))):
-        v_packed[group] = share
-    mine = pl.ds(own_group() & 7, 1)
     for group, share in enumerate(packed(p)):
         out_ref[10 * group : 10 * group + 8] = share
-        out_ref[10 * group + 8 : 10 * group + 9] = v_packed[group, mine, :]
+        out_ref[10 * group + 8 : 10 * group + 9] = lines_ref[group : group + 1]
         out_ref[10 * group + 9 : 10 * group + 10] = sums[:1]
 
 
@@ -657,14 +659,14 @@
     )
     beside = edges(top, bottom)
     c = exchange(c, "tile")
-    fine, means, sums = call(
+    fine, means, sums, lines = call(
         functools.partial(fine_kernel, True),
-        [level, own, ((8, 128), F32)],
+        [level, own, ((8, 128), F32), ((GROUPS, 128), F32)],
         [VMEM] * 11,
         (r_level, a, c_own, *beside, rows_next, band_next, *x_next),
         10**11,
         16,
-        scratch=fine_scratch,
+        scratch=fine_scratch + [pltpu.VMEM((GROUPS, 8, 128), F32)],
     )
     smoothed = call(
         smooth_kernel,
@@ -679,10 +681,9 @@
         last_partial_kernel,
         [((GROUPS * 10, 128), F32)],
         [VMEM] * 8,
-        (fine, means, smoothed, a, *x_next),
+        (fine, means, smoothed, lines, *x_next),
         10**9,
         12,
-        scratch=[pltpu.VMEM((GROUPS, 8, 128), F32)],
     )
     arrived = exchange(shares.reshape(GROUPS, 1, 1280), MEM).reshape(shares.shape)
     out = ((levels, height, extent // GROUPS), F32)

time: 104 us -> 104 us (level)
  no operation moved by 1% of the time
where the time goes in v9:
time: 104 us
  blocking collectives  53.3 us (51%)
  starting transfers between devices  23.2 us (22%)
  Pallas kernels  18.1 us (17%)
  waiting for transfers between devices  8.61 us (8%)
    all_to_all x4, blocking collectives, exchange(): return lax.all_to_all(blocks, axis, 0, 0, tiled=True)  53.3 us
    pallas_call x10, Pallas kernels, call(): pl.pallas_call(kernel, out_shape=shapes if len(shapes) > 1 else shapes[0]...  18.1 us
    ppermute x4, starting transfers between devices, edges(): return (lax.ppermute(bottom, 'tile', up), lax.ppermute(top, 'tile', down))  9.25 us
    all_to_all x2, starting transfers between devices, exchange(): return lax.all_to_all(blocks, axis, 0, 0, tiled=True)  8.86 us
    all_to_all x2, waiting for transfers between devices, exchange(): return lax.all_to_all(blocks, axis, 0, 0, tiled=True)  6.04 us
    ppermute x3, starting transfers between devices, local(): x_next[ahead] = lax.ppermute(x_next[ahead], 'mem_0', ring)  5.06 us
    ppermute x4, waiting for transfers between devices, edges(): return (lax.ppermute(bottom, 'tile', up), lax.ppermute(top, 'tile', down))  2.57 us
  transfers between devices with their start and end apart: 9, of which 4 were waited for; matrix products, arithmetic and copies ran while one was open for 0% of the time, Pallas kernels for 9%

profile of v9, /device:TPU:1, one launch (start us, length us, event | category | flops | bytes accessed | tf_op | source)
XLA Modules:
  0.0 104.0 jit_solution(15945193066961103864)
XLA Ops:
  0.6 2.8 %shard_map.68 = (f32[8,8,1024]{2,1,0:T(8,128)S(1)}, f32[8,8,1024]{2,1,0:T(8,128)S(1)}, f32[8,64,256]{2,1,0:T(8,128)}) custom-call(bf16[256,1024]{1,0:T(8,128)(2,1)} %bitcast.12, f32[128,1024]{1,0:T(8,128)} %bitcast.9), custom_call_target="tpu_custom_call" | custom-call | flops 1000000000 | bytes 1048576 | tf_op jit(solution)/shard_map/pallas_call | solution.py:527
  3.4 2.5 %collective-permute-start = (f32[8,8,1024]{2,1,0:T(8,128)S(1)}, f32[8,8,1024]{2,1,0:T(8,128)S(1)}, u32[]{:S(2)}, u32[]{:S(2)}) collective-permute-start(f32[8,8,1024]{2,1,0:T(8,128)S(1)} %get-tuple-element.36), channel_id=1, source_target_pairs={{0,1},{1,2},{2,3},{3,4},{4,5},{5,6},{6,7},{7,0},{8,9},{9,10},{10,1... | collective-permute-start | bytes 786440 | tf_op jit(solution)/shard_map/ppermute | solution.py:555
  5.9 4.0 %collective-permute-start.1 = (f32[8,8,1024]{2,1,0:T(8,128)S(1)}, f32[8,8,1024]{2,1,0:T(8,128)S(1)}, u32[]{:S(2)}, u32[]{:S(2)}) collective-permute-start(f32[8,8,1024]{2,1,0:T(8,128)S(1)} %get-tuple-element.43), channel_id=1, source_target_pairs={{1,0},{2,1},{3,2},{4,3},{5,4},{6,5},{7,6},{0,7},{9,8},{10,9},{11,1... | collective-permute-start | bytes 786440 | tf_op jit(solution)/shard_map/ppermute | solution.py:555
  10.0 0.0 copy-start.1
  10.0 0.0 copy-start.2
  10.0 0.0 copy-start.3
  10.0 5.3 %all-to-all-start = ((f32[8,64,256]{2,1,0:T(8,128)}), f32[8,64,256]{2,1,0:T(8,128)}, u32[]{:S(2)}, u32[]{:S(2)}) async-start(f32[8,64,256]{2,1,0:T(8,128)} %get-tuple-element.39.refs_1_), calls=%async_computation | async-start | bytes 1048576 | tf_op jit(solution)/shard_map/all_to_all | solution.py:539
  15.3 0.6 collective-permute-done.refs_4_
  15.9 0.0 copy-done.1
  15.9 0.0 copy-done.2
  15.9 0.0 copy-done.3
  15.9 2.1 %shard_map.69 = (bf16[2,64,512]{2,1,0:T(8,128)(2,1)S(1)}, bf16[2,256,256]{2,1,0:T(8,128)(2,1)S(1)}, f32[32,128]{1,0:T(8,128)S(1)}, f32[32,1024]{1,0:T(8,128)S(1)...) custom-call(bf16[256,1024]{1,0:T(8,128)(2,1)} %bitcast.13, ...), custom_call_target="tpu_custom_call" | custom-call | flops 99999997952 | bytes 1327264 | tf_op jit(solution)/shard_map/pallas_call | solution.py:527
  18.1 1.4 %collective-permute-start.2 = (bf16[64,1024]{1,0:T(8,128)(2,1)S(1)}, bf16[64,1024]{1,0:T(8,128)(2,1)S(1)}, u32[]{:S(2)}, u32[]{:S(2)}) collective-permute-start(bf16[64,1024]{1,0:T(8,128)(2,1)S(1)} %get-tuple-element.46), channel_id=1, source_target_pairs={{0,64},{64,128},{128,192},{192,0},{1,65},{65,129},{129,193},{193,1... | collective-permute-start | bytes 393224 | tf_op jit(solution)/shard_map/ppermute | solution.py:608
  19.4 2.6 %collective-permute-start.3 = (bf16[64,1024]{1,0:T(8,128)(2,1)S(1)}, bf16[64,1024]{1,0:T(8,128)(2,1)S(1)}, u32[]{:S(2)}, u32[]{:S(2)}) collective-permute-start(bf16[64,1024]{1,0:T(8,128)(2,1)S(1)} %get-tuple-element.47), channel_id=1, source_target_pairs={{0,128},{64,192},{128,0},{192,64},{1,129},{65,193},{129,1},{193,65... | collective-permute-start | bytes 393224 | tf_op jit(solution)/shard_map/ppermute | solution.py:608
  22.1 1.1 %collective-permute-start.4 = (bf16[64,1024]{1,0:T(8,128)(2,1)S(1)}, bf16[64,1024]{1,0:T(8,128)(2,1)S(1)}, u32[]{:S(2)}, u32[]{:S(2)}) collective-permute-start(bf16[64,1024]{1,0:T(8,128)(2,1)S(1)} %get-tuple-element.48), channel_id=1, source_target_pairs={{0,192},{64,0},{128,64},{192,128},{1,193},{65,1},{129,65},{193,129... | collective-permute-start | bytes 393224 | tf_op jit(solution)/shard_map/ppermute | solution.py:608
  23.1 0.0 collective-permute-done.1.refs_5_
  23.1 4.6 %shard_map.70 = (f32[128,1024]{1,0:T(8,128)S(1)}, f32[64,256]{1,0:T(8,128)S(1)}) custom-call(f32[128,1024]{1,0:T(8,128)} %bitcast.11, f32[8,64,256]{2,1,0:T(8,128)} %get-tuple-element.39.refs_1_, bf16[256,1024]{1,0:T(8,128)(2,1)} %bitcast.14, f32[8,5]{1,0:T(8,128)S(1)} %bitcast.8, f32[8,8,1024]{2,1,0:T(8,128)S(1)} %collective-permute-done.refs_4_, ...), custom_call_target="tpu_custom_call" | custom-call | flops 99999997952 | bytes 2097312 | tf_op jit(solution)/shard_map/pallas_call | solution.py:527
  27.7 0.0 collective-permute-done.2.refs_1_.refs_8_
  27.7 0.0 collective-permute-done.3.refs_2_.refs_9_
  27.7 0.0 collective-permute-done.4.refs_3_.refs_10_
  27.7 4.1 %all-to-all-done.c_hbm = f32[8,64,256]{2,1,0:T(8,128)} async-done(((f32[8,64,256]{2,1,0:T(8,128)}), f32[8,64,256]{2,1,0:T(8,128)}, u32[]{:S(2)}, u32[]{:S(2)}) %all-to-all-start) | async-done | bytes 524320 | tf_op jit(solution)/shard_map/all_to_all | solution.py:539
  31.8 2.3 %shard_map.71 = f32[32,32,128]{2,1,0:T(8,128)S(1)} custom-call(bf16[256,1024]{1,0:T(8,128)(2,1)} %bitcast.15, f32[8,64,256]{2,1,0:T(8,128)} %all-to-all-done.c_hbm, f32[128,1024]{1,0:T(8,128)S(1)} %get-tuple-element.49.fine_ref, f32[64,256]{1,0:T(8,128)S(1)} %get-tuple-element.50.mean_ref, bf16[2,64,512]{2,1,0:T(8,128)(2,1)S(1)} %get-tuple-element.51.mix_ref, ...), custom_call_target="tpu_custom_call" | custom-call | flops 1000000000 | bytes 2031616 | tf_op jit(solution)/shard_map/pallas_call | solution.py:527
  34.2 20.5 %all_to_all.30.arrived_ref = f32[32,32,128]{2,1,0:T(8,128)S(1)} all-to-all(f32[32,32,128]{2,1,0:T(8,128)S(1)} %shard_map.71), channel_id=1, replica_groups=mesh['mem_0'=4,'mem_1'=4,'mem_2'=2,'tile'=8] {'mem_0','mem_1','mem_2'}, dimensions={0} | all-to-all | bytes 1048576 | tf_op jit(solution)/shard_map/all_to_all | solution.py:539
  54.7 8.1 %all_to_all.31.v_ref.refs_1_ = f32[8,32,128]{2,1,0:T(8,128)S(1)} all-to-all(f32[8,32,128]{2,1,0:T(8,128)S(1)} %shard_map.72), channel_id=1, replica_groups=mesh['mem_0'=4,'mem_1'=4,'mem_2'=2,'tile'=8] {'mem_1','mem_2'}, dimensions={0} | all-to-all | bytes 262144 | tf_op jit(solution)/shard_map/all_to_all | solution.py:539
  62.8 0.0 copy-start.5
  62.8 1.2 %shard_map.73 = (f32[8,8,1024]{2,1,0:T(8,128)S(1)}, f32[8,8,1024]{2,1,0:T(8,128)S(1)}, f32[8,8,256]{2,1,0:T(8,128)}, f32[64,256]{1,0:T(8,128)S(1)}) custom-call(f32[8,32,128]{2,1,0:T(8,128)S(1)} %all_to_all.31.v_ref.refs_1_, bf16[64,1024]{1,0:T(8,128)(2,1)S(1)} %get-tuple-element.54.refs_0_.refs_7_, ...), custom_call_target="tpu_custom_call" | custom-call | flops 1000000000 | bytes 655360 | tf_op jit(solution)/shard_map/pallas_call | solution.py:527
  64.0 0.0 copy-start.4
  64.0 0.3 collective-permute-start.5
  64.3 2.4 %collective-permute-start.6 = (f32[8,8,1024]{2,1,0:T(8,128)S(1)}, f32[8,8,1024]{2,1,0:T(8,128)S(1)}, u32[]{:S(2)}, u32[]{:S(2)}) collective-permute-start(f32[8,8,1024]{2,1,0:T(8,128)S(1)} %get-tuple-element.60), channel_id=1, source_target_pairs={{1,0},{2,1},{3,2},{4,3},{5,4},{6,5},{7,6},{0,7},{9,8},{10,9},{11,1... | collective-permute-start | bytes 786440 | tf_op jit(solution)/shard_map/ppermute | solution.py:555
  66.7 3.5 %all-to-all-start.3 = ((f32[8,8,256]{2,1,0:T(8,128)}), f32[8,8,256]{2,1,0:T(8,128)S(1)}, u32[]{:S(2)}, u32[]{:S(2)}) async-start(f32[8,8,256]{2,1,0:T(8,128)} %get-tuple-element.65), calls=%async_computation.3 | async-start | bytes 131072 | tf_op jit(solution)/shard_map/all_to_all | solution.py:539
  70.2 2.0 %collective-permute-done.5.refs_3_ = f32[8,8,1024]{2,1,0:T(8,128)S(1)} collective-permute-done((f32[8,8,1024]{2,1,0:T(8,128)S(1)}, f32[8,8,1024]{2,1,0:T(8,128)S(1)}, u32[]{:S(2)}, u32[]{:S(2)}) %collective-permute-start.5) | collective-permute-done | bytes 262176 | tf_op jit(solution)/shard_map/ppermute | solution.py:555
  72.2 0.0 collective-permute-done.6.refs_4_
  72.2 0.0 copy-done.5
  72.2 0.0 copy-done.4
  72.2 0.0 copy-start
  72.2 3.0 %shard_map.74 = (f32[32,1024]{1,0:T(8,128)S(1)}, f32[64,256]{1,0:T(8,128)S(1)}, f32[8,128]{1,0:T(8,128)S(1)}, f32[32,128]{1,0:T(8,128)S(1)}) custom-call(f32[32,1024]{1,0:T(8,128)S(1)} %get-tuple-element.38.refs_0_, f32[8,32,128]{2,1,0:T(8,128)S(1)} %all_to_all.31.v_ref.refs_1_, f32[64,256]{1,0:T(8,128)S(1)} %get-tuple-element.58.refs_2_, ...), custom_call_target="tpu_custom_call" | custom-call | flops 99999997952 | bytes 1556480 | tf_op jit(solution)/shard_map/pallas_call | solution.py:527
  75.2 2.0 %all-to-all-done.3.c_ref = f32[8,8,256]{2,1,0:T(8,128)S(1)} async-done(((f32[8,8,256]{2,1,0:T(8,128)}), f32[8,8,256]{2,1,0:T(8,128)S(1)}, u32[]{:S(2)}, u32[]{:S(2)}) %all-to-all-start.3) | async-done | bytes 65568 | tf_op jit(solution)/shard_map/all_to_all | solution.py:539
  77.2 0.0 copy-done
  77.2 0.5 shard_map.75
  77.7 10.0 %all_to_all.32.smoothed_ref = f32[8,24,128]{2,1,0:T(8,128)S(1)} all-to-all(f32[8,24,128]{2,1,0:T(8,128)S(1)} %shard_map.75), channel_id=1, replica_groups=mesh['mem_0'=4,'mem_1'=4,'mem_2'=2,'tile'=8] {'tile'}, dimensions={0} | all-to-all | bytes 196608 | tf_op jit(solution)/shard_map/all_to_all | solution.py:539
  87.6 0.7 shard_map.76
  88.3 14.8 %all_to_all.33 = f32[32,1,1280]{2,1,0:T(1,128)S(1)} all-to-all(f32[32,1,1280]{2,1,0:T(1,128)S(1)} %bitcast.6), channel_id=1, replica_groups=mesh['mem_0'=4,'mem_1'=4,'mem_2'=2,'tile'=8] {'mem_0','mem_1','mem_2'}, dimensions={0} | all-to-all | bytes 327680 | tf_op jit(solution)/shard_map/all_to_all | solution.py:539
  103.0 0.9 shard_map.77
  (1 shorter events, 0.0 us)
Async XLA Ops:
  3.4 12.5 %collective-permute-start = (f32[8,8,1024]{2,1,0:T(8,128)S(1)}, f32[8,8,1024]{2,1,0:T(8,128)S(1)}, u32[]{:S(2)}, u32[]{:S(2)}) collective-permute-start(f32[8,8,1024]{2,1,0:T(8,128)S(1)} %get-tuple-element.36), channel_id=1, source_target_pairs={{0,1},{1,2},{2,3},{3,4},{4,5},{5,6},{6,7},{7,0},{8,9},{9,10},{10,1... | collective-permute-start | bytes 786440 | tf_op jit(solution)/shard_map/ppermute | solution.py:555
  5.9 17.2 %collective-permute-start.1 = (f32[8,8,1024]{2,1,0:T(8,128)S(1)}, f32[8,8,1024]{2,1,0:T(8,128)S(1)}, u32[]{:S(2)}, u32[]{:S(2)}) collective-permute-start(f32[8,8,1024]{2,1,0:T(8,128)S(1)} %get-tuple-element.43), channel_id=1, source_target_pairs={{1,0},{2,1},{3,2},{4,3},{5,4},{6,5},{7,6},{0,7},{9,8},{10,9},{11,1... | collective-permute-start | bytes 786440 | tf_op jit(solution)/shard_map/ppermute | solution.py:555
  10.0 5.9 %copy-start.1 = (f32[256,256]{1,0:T(8,128)S(1)}, f32[256,256]{1,0:T(8,128)}, u32[]{:S(2)}) copy-start(f32[256,256]{1,0:T(8,128)} %lon_ref.1) | copy-start | bytes 786436
  10.0 5.9 %copy-start.2 = (f32[64,64]{1,0:T(8,128)S(1)}, f32[64,64]{1,0:T(8,128)}, u32[]{:S(2)}) copy-start(f32[64,64]{1,0:T(8,128)} %lat_ref.1) | copy-start | bytes 49156
  10.0 5.9 %copy-start.3 = (f32[2,4,5]{2,1,0:T(4,128)S(1)}, f32[2,4,5]{2,1,0:T(4,128)}, u32[]{:S(2)}) copy-start(f32[2,4,5]{2,1,0:T(4,128)} %param.7) | copy-start | bytes 484
  10.0 21.8 %all-to-all-start = ((f32[8,64,256]{2,1,0:T(8,128)}), f32[8,64,256]{2,1,0:T(8,128)}, u32[]{:S(2)}, u32[]{:S(2)}) async-start(f32[8,64,256]{2,1,0:T(8,128)} %get-tuple-element.39.refs_1_), calls=%async_computation | async-start | bytes 1048576 | tf_op jit(solution)/shard_map/all_to_all | solution.py:539
  18.1 9.6 %collective-permute-start.2 = (bf16[64,1024]{1,0:T(8,128)(2,1)S(1)}, bf16[64,1024]{1,0:T(8,128)(2,1)S(1)}, u32[]{:S(2)}, u32[]{:S(2)}) collective-permute-start(bf16[64,1024]{1,0:T(8,128)(2,1)S(1)} %get-tuple-element.46), channel_id=1, source_target_pairs={{0,64},{64,128},{128,192},{192,0},{1,65},{65,129},{129,193},{193,1... | collective-permute-start | bytes 393224 | tf_op jit(solution)/shard_map/ppermute | solution.py:608
  19.4 8.3 %collective-permute-start.3 = (bf16[64,1024]{1,0:T(8,128)(2,1)S(1)}, bf16[64,1024]{1,0:T(8,128)(2,1)S(1)}, u32[]{:S(2)}, u32[]{:S(2)}) collective-permute-start(bf16[64,1024]{1,0:T(8,128)(2,1)S(1)} %get-tuple-element.47), channel_id=1, source_target_pairs={{0,128},{64,192},{128,0},{192,64},{1,129},{65,193},{129,1},{193,65... | collective-permute-start | bytes 393224 | tf_op jit(solution)/shard_map/ppermute | solution.py:608
  22.1 5.7 %collective-permute-start.4 = (bf16[64,1024]{1,0:T(8,128)(2,1)S(1)}, bf16[64,1024]{1,0:T(8,128)(2,1)S(1)}, u32[]{:S(2)}, u32[]{:S(2)}) collective-permute-start(bf16[64,1024]{1,0:T(8,128)(2,1)S(1)} %get-tuple-element.48), channel_id=1, source_target_pairs={{0,192},{64,0},{128,64},{192,128},{1,193},{65,1},{129,65},{193,129... | collective-permute-start | bytes 393224 | tf_op jit(solution)/shard_map/ppermute | solution.py:608
  62.8 9.4 %copy-start.5 = (bf16[1,2,160,128]{3,2,1,0:T(8,128)(2,1)S(1)}, bf16[1,2,160,128]{3,2,1,0:T(8,128)(2,1)}, u32[]{:S(2)}) copy-start(bf16[1,2,160,128]{3,2,1,0:T(8,128)(2,1)} %get-tuple-element.62.refs_6_) | copy-start | bytes 245764
  64.0 8.2 %copy-start.4 = (bf16[2,128,192]{2,1,0:T(8,128)(2,1)S(1)}, bf16[2,128,192]{2,1,0:T(8,128)(2,1)}, u32[]{:S(2)}) copy-start(bf16[2,128,192]{2,1,0:T(8,128)(2,1)} %get-tuple-element.61.refs_5_) | copy-start | bytes 294916
  64.0 8.2 %collective-permute-start.5 = (f32[8,8,1024]{2,1,0:T(8,128)S(1)}, f32[8,8,1024]{2,1,0:T(8,128)S(1)}, u32[]{:S(2)}, u32[]{:S(2)}) collective-permute-start(f32[8,8,1024]{2,1,0:T(8,128)S(1)} %get-tuple-element.59), channel_id=1, source_target_pairs={{0,1},{1,2},{2,3},{3,4},{4,5},{5,6},{6,7},{7,0},{8,9},{9,10},{10,1... | collective-permute-start | bytes 786440 | tf_op jit(solution)/shard_map/ppermute | solution.py:555
  64.3 7.9 %collective-permute-start.6 = (f32[8,8,1024]{2,1,0:T(8,128)S(1)}, f32[8,8,1024]{2,1,0:T(8,128)S(1)}, u32[]{:S(2)}, u32[]{:S(2)}) collective-permute-start(f32[8,8,1024]{2,1,0:T(8,128)S(1)} %get-tuple-element.60), channel_id=1, source_target_pairs={{1,0},{2,1},{3,2},{4,3},{5,4},{6,5},{7,6},{0,7},{9,8},{10,9},{11,1... | collective-permute-start | bytes 786440 | tf_op jit(solution)/shard_map/ppermute | solution.py:555
  66.7 10.5 %all-to-all-start.3 = ((f32[8,8,256]{2,1,0:T(8,128)}), f32[8,8,256]{2,1,0:T(8,128)S(1)}, u32[]{:S(2)}, u32[]{:S(2)}) async-start(f32[8,8,256]{2,1,0:T(8,128)} %get-tuple-element.65), calls=%async_computation.3 | async-start | bytes 131072 | tf_op jit(solution)/shard_map/all_to_all | solution.py:539
  72.2 5.0 %copy-start = (bf16[2,64,64]{2,1,0:T(8,128)(2,1)S(1)}, bf16[2,64,64]{2,1,0:T(8,128)(2,1)}, u32[]{:S(2)}) copy-start(bf16[2,64,64]{2,1,0:T(8,128)(2,1)} %get-tuple-element.66.lats_ref) | copy-start | bytes 49156
